TPU v7x, 32 devices: a whole 2x2x4 slice. The times are simulated.
32 devices in a mesh: dp: 8 (over z, y), tensor: 4 (over x, core).
Axes of the slice: x: 2, y: 2, z: 4, core: 2. Of those that a mesh axis runs over, the one named last changes fastest.
Arguments:
- hidden: bfloat16 [10240, 768], P(('dp', 'tensor')), may hold values from -6 to 6
- first_gain: float32 [768], replicated, may hold values from 0.5 to 1.5
- first_shift: float32 [768], replicated, may hold values from -1.5 to 1.5
- query_weight: bfloat16 [768, 768], P(None, 'tensor'), may hold values from -0.21875 to 0.21875
- query_bias: float32 [768], P('tensor'), may hold values from -1.5 to 1.5
- key_weight: bfloat16 [768, 768], P(None, 'tensor'), may hold values from -0.21875 to 0.21875
- value_weight: bfloat16 [768, 768], P(None, 'tensor'), may hold values from -0.21875 to 0.21875
- value_bias: float32 [768], P('tensor'), may hold values from -1.5 to 1.5
- output_weight: bfloat16 [768, 768], P('tensor'), may hold values from -3.5 to 3.5
- output_bias: float32 [768], replicated, may hold values from -1.5 to 1.5
- first_scale: float32 [768], replicated, may hold values from 0.5 to 1.5
- second_gain: float32 [768], replicated, may hold values from 0.5 to 1.5
- second_shift: float32 [768], replicated, may hold values from -1.5 to 1.5
- expand_weight: bfloat16 [768, 3072], P(None, 'tensor'), may hold values from -0.21875 to 0.21875
- expand_bias: float32 [3072], P('tensor'), may hold values from -1.5 to 1.5
- reduce_weight: bfloat16 [3072, 768], P('tensor'), may hold values from -0.109375 to 0.109375
- reduce_bias: float32 [768], replicated, may hold values from -1.5 to 1.5
- second_scale: float32 [768], replicated, may hold values from 0.5 to 1.5
- table_low: float32 [732, 12], P(None, 'tensor'), may hold values from -4 to 4
- table_high: float32 [2212, 12], P(None, 'tensor'), may hold values from -4 to 4
- resolution: int32 [16], P('dp'), may hold values from 0 to 1
- counts: int32 [8], P('dp'), may hold values from 1 to 2, as said below
- index_low: int32 [197, 197], replicated, may hold values from 0 to 731
- index_high: int32 [577, 577], replicated, may hold values from 0 to 2211
- cotangent: bfloat16 [10240, 768], P(('dp', 'tensor')), may hold values from -6 to 6
Outputs:
- result: bfloat16 [10240, 768], P(('dp', 'tensor'))
- hidden_grad: float32 [10240, 768], P(('dp', 'tensor'))
- first_gain_grad: float32 [768], replicated
- first_shift_grad: float32 [768], replicated
- query_weight_grad: float32 [768, 768], P(None, 'tensor')
- query_bias_grad: float32 [768], P('tensor')
- key_weight_grad: float32 [768, 768], P(None, 'tensor')
- value_weight_grad: float32 [768, 768], P(None, 'tensor')
- value_bias_grad: float32 [768], P('tensor')
- output_weight_grad: float32 [768, 768], P('tensor')
- output_bias_grad: float32 [768], replicated
- first_scale_grad: float32 [768], replicated
- second_gain_grad: float32 [768], replicated
- second_shift_grad: float32 [768], replicated
- expand_weight_grad: float32 [768, 3072], P(None, 'tensor')
- expand_bias_grad: float32 [3072], P('tensor')
- reduce_weight_grad: float32 [3072, 768], P('tensor')
- reduce_bias_grad: float32 [768], replicated
- second_scale_grad: float32 [768], replicated
- table_low_grad: float32 [732, 12], P(None, 'tensor')
- table_high_grad: float32 [2212, 12], P(None, 'tensor')
Inputs may be any that keep to these rules, and one draw needn't show every extreme that they name: `counts`: some index of dp has all 2 slots live in every draw.
All inputs are finite; a program needn't handle non-finite values.
Results may differ from a plain program's by a relative error of at most 0.019.
Values may be sent and summed in bfloat16 or wider, within the bound.
A program may use at most 384 MiB of HBM per device.

v0:
```python
import jax
import jax.numpy as jnp
from jax import lax
from jax.sharding import PartitionSpec as P

HD = 64
P_LO = 197
P_HI = 577
SEQ = 640
SLOTS = 2


eps_norm = 1e-06
masked_score = -1e30
inv_sqrt_two = 0.7071067811865476
inv_sqrt_two_pi = 0.3989422804014327


def normalize(values, gain, shift):
    center = jnp.mean(values, axis=-1, keepdims=True)
    centered = values - center
    variance = jnp.mean(centered * centered, axis=-1, keepdims=True)
    inverse = lax.rsqrt(variance + eps_norm)
    scaled = centered * inverse
    return (scaled * gain + shift, scaled, inverse)


def normalize_back(upstream, scaled, inverse, gain):
    inner = upstream * gain
    mean_inner = jnp.mean(inner, axis=-1, keepdims=True)
    mean_mixed = jnp.mean(inner * scaled, axis=-1, keepdims=True)
    return inverse * (inner - mean_inner - scaled * mean_mixed)


def gelu_value(values):
    return 0.5 * values * (1.0 + jax.scipy.special.erf(values * inv_sqrt_two))


def gelu_slope(values):
    return 0.5 * (
        1.0 + jax.scipy.special.erf(values * inv_sqrt_two)
    ) + values * inv_sqrt_two_pi * jnp.exp(-0.5 * values * values)


def local(
    hidden,
    first_gain,
    first_shift,
    query_weight,
    query_bias,
    key_weight,
    value_weight,
    value_bias,
    output_weight,
    output_bias,
    first_scale,
    second_gain,
    second_shift,
    expand_weight,
    expand_bias,
    reduce_weight,
    reduce_bias,
    second_scale,
    table_low,
    table_high,
    resolution,
    counts,
    index_low,
    index_high,
    cotangent,
):
    floating = jnp.float32
    bfloat = jnp.bfloat16
    tensor_size = lax.axis_size("tensor")
    rows_dev = hidden.shape[0]
    group_rows = rows_dev * tensor_size
    heads_dev = table_low.shape[1]
    head_scale = HD ** (-0.5)
    positions = jnp.arange(SEQ)
    slot_limits = jnp.where(resolution == 1, P_HI, P_LO)
    row_ids = lax.axis_index("tensor") * rows_dev + jnp.arange(rows_dev)
    row_slots = row_ids // SEQ
    picker = row_slots[:, None] == jnp.arange(SLOTS)[None, :]
    row_limits = jnp.sum(jnp.where(picker, slot_limits[None, :], 0), axis=1)
    live_rows = ((row_ids % SEQ < row_limits) & (row_slots < counts[0])).astype(floating)[:, None]
    residual = hidden.astype(floating)
    normed_one, scaled_one, inverse_one = normalize(residual, first_gain, first_shift)
    gathered_one = lax.all_gather(normed_one.astype(bfloat), "tensor", axis=0, tiled=True)
    queries = (
        (jnp.dot(gathered_one, query_weight, preferred_element_type=floating) + query_bias)
        * head_scale
    ).astype(bfloat)
    keys = jnp.dot(gathered_one, key_weight, preferred_element_type=floating).astype(bfloat)
    values = (
        jnp.dot(gathered_one, value_weight, preferred_element_type=floating) + value_bias
    ).astype(bfloat)
    shaped = (SLOTS, SEQ, heads_dev, HD)
    queries_img = queries.reshape(shaped)
    keys_img = keys.reshape(shaped)
    values_img = values.reshape(shaped)
    bias_low = jnp.pad(
        jnp.transpose(table_low[index_low], (2, 0, 1)), ((0, 0), (0, SEQ - P_LO), (0, SEQ - P_LO))
    )
    bias_high = jnp.pad(
        jnp.transpose(table_high[index_high], (2, 0, 1)), ((0, 0), (0, SEQ - P_HI), (0, SEQ - P_HI))
    )

    def scores_of(query_blk, key_blk, res_blk):
        chosen = jnp.where(res_blk == 1, bias_high, bias_low)
        key_bound = jnp.where(res_blk == 1, P_HI, P_LO)
        biased = (
            jnp.einsum("qhd,khd->hqk", query_blk, key_blk, preferred_element_type=floating) + chosen
        )
        return jnp.where((positions < key_bound)[None, None, :], biased, masked_score)

    def attend(inputs):
        query_blk, key_blk, value_blk, res_blk = inputs
        scores = scores_of(query_blk, key_blk, res_blk)
        peak = jnp.max(scores, axis=-1, keepdims=True)
        raised = jnp.exp(scores - peak)
        summed = jnp.sum(raised, axis=-1, keepdims=True)
        attention = (raised / summed).astype(bfloat)
        mixture = jnp.einsum("hqk,khd->qhd", attention, value_blk, preferred_element_type=floating)
        return (mixture.astype(bfloat), (peak + jnp.log(summed))[..., 0])

    mixture_img, log_totals = lax.map(attend, (queries_img, keys_img, values_img, resolution))
    mixture_rows = mixture_img.reshape(group_rows, heads_dev * HD)
    attn_out = (
        lax.psum_scatter(
            jnp.dot(mixture_rows, output_weight, preferred_element_type=floating).astype(
                jnp.bfloat16
            ),
            "tensor",
            scatter_dimension=0,
            tiled=True,
        ).astype(jnp.float32)
        + output_bias
    )
    after_attn = residual + first_scale * attn_out
    normed_two, scaled_two, inverse_two = normalize(after_attn, second_gain, second_shift)
    normed_two_low = normed_two.astype(bfloat)
    gathered_two = lax.all_gather(normed_two_low, "tensor", axis=0, tiled=True)
    pre_act = jnp.dot(gathered_two, expand_weight, preferred_element_type=floating) + expand_bias
    activated = gelu_value(pre_act).astype(bfloat)
    mlp_out = (
        lax.psum_scatter(
            jnp.dot(activated, reduce_weight, preferred_element_type=floating).astype(jnp.bfloat16),
            "tensor",
            scatter_dimension=0,
            tiled=True,
        ).astype(jnp.float32)
        + reduce_bias
    )
    result = ((after_attn + second_scale * mlp_out) * live_rows).astype(bfloat)
    upstream = cotangent.astype(floating) * live_rows
    second_scale_grad = jnp.sum(upstream * mlp_out, axis=0)
    mlp_grad = upstream * second_scale
    reduce_bias_grad = jnp.sum(mlp_grad, axis=0)
    mlp_grad_low = mlp_grad.astype(bfloat)
    gathered_mlp_grad = lax.all_gather(mlp_grad_low, "tensor", axis=0, tiled=True)
    reduce_weight_grad = jnp.einsum(
        "rf,rd->fd", activated, gathered_mlp_grad, preferred_element_type=floating
    )
    act_grad = jnp.einsum(
        "rd,fd->rf", gathered_mlp_grad, reduce_weight, preferred_element_type=floating
    )
    pre_grad = act_grad * gelu_slope(pre_act)
    expand_bias_grad = jnp.sum(pre_grad, axis=0)
    pre_grad_low = pre_grad.astype(bfloat)
    expand_weight_grad = jnp.einsum(
        "rd,rf->df", gathered_two, pre_grad_low, preferred_element_type=floating
    )
    normed_two_grad = lax.psum_scatter(
        jnp.einsum(
            "rf,df->rd", pre_grad_low, expand_weight, preferred_element_type=floating
        ).astype(jnp.bfloat16),
        "tensor",
        scatter_dimension=0,
        tiled=True,
    ).astype(jnp.float32)
    second_gain_grad = jnp.sum(normed_two_grad * scaled_two, axis=0)
    second_shift_grad = jnp.sum(normed_two_grad, axis=0)
    after_grad = upstream + normalize_back(normed_two_grad, scaled_two, inverse_two, second_gain)
    first_scale_grad = jnp.sum(after_grad * attn_out, axis=0)
    attn_grad = after_grad * first_scale
    output_bias_grad = jnp.sum(attn_grad, axis=0)
    gathered_attn_grad = lax.all_gather(attn_grad.astype(bfloat), "tensor", axis=0, tiled=True)
    output_weight_grad = jnp.einsum(
        "rc,rd->cd", mixture_rows, gathered_attn_grad, preferred_element_type=floating
    )
    mixture_grad = jnp.einsum(
        "rd,cd->rc", gathered_attn_grad, output_weight, preferred_element_type=floating
    ).astype(bfloat)

    def attend_back(totals, inputs):
        grad_low, grad_high = totals
        query_blk, key_blk, value_blk, res_blk, lse_blk, back_blk = inputs
        scores = scores_of(query_blk, key_blk, res_blk)
        attention = jnp.exp(scores - lse_blk[..., None])
        prob_grad = jnp.einsum("qhd,khd->hqk", back_blk, value_blk, preferred_element_type=floating)
        score_grad = attention * (
            prob_grad - jnp.sum(attention * prob_grad, axis=-1, keepdims=True)
        )
        score_low = score_grad.astype(bfloat)
        query_grad = (
            jnp.einsum("hqk,khd->qhd", score_low, key_blk, preferred_element_type=floating)
            * head_scale
        )
        key_grad = jnp.einsum("hqk,qhd->khd", score_low, query_blk, preferred_element_type=floating)
        value_grad = jnp.einsum(
            "hqk,qhd->khd", attention.astype(bfloat), back_blk, preferred_element_type=floating
        )
        is_high = jnp.where(res_blk == 1, 1.0, 0.0).astype(floating)
        totals = (grad_low + (1.0 - is_high) * score_grad, grad_high + is_high * score_grad)
        return (totals, (query_grad, key_grad.astype(bfloat), value_grad))

    empty_map = jnp.zeros((heads_dev, SEQ, SEQ), floating)
    bias_grads, per_slot = lax.scan(
        attend_back,
        (empty_map, empty_map),
        (queries_img, keys_img, values_img, resolution, log_totals, mixture_grad.reshape(shaped)),
    )
    query_grad = per_slot[0].reshape(group_rows, heads_dev * HD)
    key_low = per_slot[1].reshape(group_rows, heads_dev * HD)
    value_grad = per_slot[2].reshape(group_rows, heads_dev * HD)
    query_bias_grad = jnp.sum(query_grad, axis=0)
    value_bias_grad = jnp.sum(value_grad, axis=0)
    query_low = query_grad.astype(bfloat)
    value_low = value_grad.astype(bfloat)
    table_low_grad = jax.ops.segment_sum(
        bias_grads[0][:, :P_LO, :P_LO].reshape(heads_dev, P_LO * P_LO).T,
        index_low.reshape(P_LO * P_LO),
        num_segments=table_low.shape[0],
    )
    table_high_grad = jax.ops.segment_sum(
        bias_grads[1][:, :P_HI, :P_HI].reshape(heads_dev, P_HI * P_HI).T,
        index_high.reshape(P_HI * P_HI),
        num_segments=table_high.shape[0],
    )
    query_weight_grad = jnp.einsum(
        "rd,rc->dc", gathered_one, query_low, preferred_element_type=floating
    )
    key_weight_grad = jnp.einsum(
        "rd,rc->dc", gathered_one, key_low, preferred_element_type=floating
    )
    value_weight_grad = jnp.einsum(
        "rd,rc->dc", gathered_one, value_low, preferred_element_type=floating
    )
    part_query = jnp.einsum("rc,dc->rd", query_low, query_weight, preferred_element_type=floating)
    part_key = jnp.einsum("rc,dc->rd", key_low, key_weight, preferred_element_type=floating)
    part_value = jnp.einsum("rc,dc->rd", value_low, value_weight, preferred_element_type=floating)
    normed_one_grad = lax.psum_scatter(
        (part_query + part_key + part_value).astype(jnp.bfloat16),
        "tensor",
        scatter_dimension=0,
        tiled=True,
    ).astype(jnp.float32)
    first_gain_grad = jnp.sum(normed_one_grad * scaled_one, axis=0)
    first_shift_grad = jnp.sum(normed_one_grad, axis=0)
    hidden_grad = after_grad + normalize_back(normed_one_grad, scaled_one, inverse_one, first_gain)
    (
        query_weight_grad,
        query_bias_grad,
        key_weight_grad,
        value_weight_grad,
        value_bias_grad,
        output_weight_grad,
        table_low_grad,
        table_high_grad,
        expand_weight_grad,
        expand_bias_grad,
        reduce_weight_grad,
    ) = lax.psum(
        (
            query_weight_grad,
            query_bias_grad,
            key_weight_grad,
            value_weight_grad,
            value_bias_grad,
            output_weight_grad,
            table_low_grad,
            table_high_grad,
            expand_weight_grad,
            expand_bias_grad,
            reduce_weight_grad,
        ),
        "dp",
    )
    (
        first_gain_grad,
        first_shift_grad,
        first_scale_grad,
        output_bias_grad,
        second_gain_grad,
        second_shift_grad,
        second_scale_grad,
        reduce_bias_grad,
    ) = lax.psum(
        (
            first_gain_grad,
            first_shift_grad,
            first_scale_grad,
            output_bias_grad,
            second_gain_grad,
            second_shift_grad,
            second_scale_grad,
            reduce_bias_grad,
        ),
        ("dp", "tensor"),
    )
    return (
        result,
        hidden_grad,
        first_gain_grad,
        first_shift_grad,
        query_weight_grad,
        query_bias_grad,
        key_weight_grad,
        value_weight_grad,
        value_bias_grad,
        output_weight_grad,
        output_bias_grad,
        first_scale_grad,
        second_gain_grad,
        second_shift_grad,
        expand_weight_grad,
        expand_bias_grad,
        reduce_weight_grad,
        reduce_bias_grad,
        second_scale_grad,
        table_low_grad,
        table_high_grad,
    )


def solution(mesh):
    in_specs = (
        P(("dp", "tensor"), None),
        P(),
        P(),
        P(None, "tensor"),
        P("tensor"),
        P(None, "tensor"),
        P(None, "tensor"),
        P("tensor"),
        P("tensor", None),
        P(),
        P(),
        P(),
        P(),
        P(None, "tensor"),
        P("tensor"),
        P("tensor", None),
        P(),
        P(),
        P(None, "tensor"),
        P(None, "tensor"),
        P("dp"),
        P("dp"),
        P(),
        P(),
        P(("dp", "tensor"), None),
    )
    out_specs = (
        P(("dp", "tensor"), None),
        P(("dp", "tensor"), None),
        P(),
        P(),
        P(None, "tensor"),
        P("tensor"),
        P(None, "tensor"),
        P(None, "tensor"),
        P("tensor"),
        P("tensor", None),
        P(),
        P(),
        P(),
        P(),
        P(None, "tensor"),
        P("tensor"),
        P("tensor", None),
        P(),
        P(),
        P(None, "tensor"),
        P(None, "tensor"),
    )
    return jax.shard_map(local, mesh=mesh, in_specs=in_specs, out_specs=out_specs, check_vma=False)
```

profile of v0, /device:TPU:0, one launch (start us, length us, event | category | flops | bytes accessed | tf_op | source)
XLA Modules:
  0.0 3483.9 jit_solution(12486167899317772361)
XLA Ops:
  19.4 670.5 %gather_fusion = f32[332929,3]{1,0:T(8,128)} fusion(f32[2212,3]{1,0:T(8,128)S(1)} %copy.96, s32[333824]{0:T(1024)} %pad_clamp_fusion), kind=kCustom, calls=%fused_computation | custom fusion | bytes 9322012 | tf_op jit(solution)/shard_map/gather | solution.py:105
  689.9 85.0 %copy.97 = f32[332929,3]{0,1:T(4,128)} copy(f32[332929,3]{1,0:T(8,128)} %gather_fusion) | data formatting | bytes 7990296 | tf_op jit(solution)/shard_map/gather | solution.py:105
  774.9 9.2 reshape.193
  784.1 6.0 copy.125
  790.6 129.4 %gather_fusion.1 = f32[38809,3]{1,0:T(8,128)} fusion(f32[732,3]{1,0:T(8,128)S(1)} %copy.98, s32[38912]{0:T(1024)S(1)} %pad_clamp_fusion.1), kind=kCustom, calls=%fused_computation.1 | custom fusion | bytes 1086652 | tf_op jit(solution)/shard_map/gather | solution.py:102
  920.0 11.1 copy.99
  952.7 16.1 while.32
  972.6 33.4 reduce-scatter.5.cloned.1.call-done
  1012.9 20.1 all-gather.7.cloned.1.call-done
  1033.0 5.8 multiply_convert_fusion
  1038.8 18.1 all-gather.9.cloned.1.call-done
  1057.0 5.7 fusion.119
  1067.1 4.9 convolution_convert_fusion.2
  1072.2 25.6 reduce-scatter.9.cloned.1.call-done
  1100.1 30.8 reduce-scatter.7.cloned.1.call-done
  1136.3 21.9 all-gather.11.cloned.1.call-done
  1161.6 66.6 %while.33 = (s32[]{:T(128)}, f32[3,640,640]{1,2,0:T(8,128)}, f32[3,640,640]{1,2,0:T(8,128)}, f32[2,640,3,64]{1,3,2,0:T(8,128)}, bf16[2,640,3,64]{1,3,2,0:T(8,128...) while((s32[]{:T(128)}, f32[3,640,640]{1,2,0:T(8,128)}, ...), condition=%wide.region_16.17_spmd.clone, body=%wide.region_14.16_spmd.clone.sunk | while | flops 807566080 | bytes 164216560 | solution.py:218
  1167.0 5.9 multiply_reduce_fusion.6
  1172.8 8.9 select_add_fusion.4
  1181.7 5.2 select_add_fusion.5
  1198.8 5.9 multiply_reduce_fusion.6
  1204.7 10.3 select_add_fusion.4
  1215.0 6.7 select_add_fusion.5
  1236.4 5.4 fusion.97
  1256.6 10.3 copy.116
  1271.4 6.0 copy.117
  1277.5 9.4 reshape.191
  1286.9 73.7 %copy.118 = f32[332929,3]{1,0:T(8,128)} copy(f32[332929,3]{0,1:T(4,128)} %bitcast.175) | data formatting | bytes 7990296 | tf_op jit(solution)/shard_map/transpose | solution.py:236
  1360.6 207.6 %scatter_custom_fusion = f32[732,3]{1,0:T(8,128)S(1)} fusion(s32[38809]{0:T(1024)S(1)} %reshape.210, f32[38809,3]{1,0:T(8,128)} %copy.116, f32[]{:T(128)} %constant.108.clone.1), kind=kCustom, calls=%fused_computation.140 | custom fusion | flops 116427 | bytes 9296 | tf_op jit(solution)/shard_map/scatter-add | solution.py:230
  1568.3 1771.1 %scatter_custom_fusion.1 = f32[2212,3]{1,0:T(8,128)} fusion(s32[332929]{0:T(1024)} %reshape.218, f32[332929,3]{1,0:T(8,128)} %copy.118, f32[]{:T(128)} %constant.108.clone.1), kind=kCustom, calls=%fused_computation.138 | custom fusion | flops 998787 | bytes 27056 | tf_op jit(solution)/shard_map/scatter-add | solution.py:235
  3339.3 82.1 %all-reduce.3 = (f32[192]{0:T(256)}, f32[192]{0:T(256)}, f32[768]{0:T(1024)}, f32[732,3]{1,0:T(8,128)S(1)}, f32[2212,3]{1,0:T(8,128)}) all-reduce(f32[192]{0:T(256)S(1)} %reduce_sum.214, f32[192]{0:T(256)S(1)} %reduce_sum.216, f32[768]{0:T(1024)S(1)} %copy-done.56, ...), channel_id=1, replica_groups=mesh['dp'=8,'tensor'=4] {'dp'}, use_global_device_ids=true, to_apply=%region_26.27 | all-reduce | flops 9984 | bytes 79872 | tf_op jit(solution)/shard_map/psum | solution.py:273
  3426.1 38.8 %all-reduce.2 = (f32[768]{0:T(1024)}, f32[768]{0:T(1024)}, f32[768]{0:T(1024)}, f32[768]{0:T(1024)}, f32[768]{0:T(1024)}, /*index=5*/f32[768]{0:T(1024)}, f32[768]{0:T(1024)}, f32[768]{0:T(1024)}) all-reduce(f32[768]{0:T(1024)S(1)} %get-tuple-element.363, ...), channel_id=1, replica_groups=mesh['dp'=8,'tensor'=4] {'dp','tensor'}, use_global_device_ids=true, to_apply=%region_21.22 | all-reduce | flops 6144 | bytes 49152 | tf_op jit(solution)/shard_map/psum | solution.py:298
  (283 shorter events, 140.1 us)
Async XLA Ops:
  7.2 1025.8 %copy-start = (bf16[768,768]{1,0:T(8,128)(2,1)S(1)}, bf16[768,768]{1,0:T(8,128)(2,1)}, u32[]{:S(2)}) copy-start(bf16[768,768]{1,0:T(8,128)(2,1)} %param.42) | copy-start | bytes 3538948
  7.2 932.2 %all-gather.5.cloned.1.call-start = ((), (), s32[]{:S(2)}) async-start(), calls=%async_computation.4 | async-start | bytes 2457600 | tf_op jit(solution)/shard_map/all_gather | solution.py:88
  12.6 993.5 %reduce-scatter.5.cloned.1.call-start = ((), (), s32[]{:S(2)}) async-start(), calls=%async_computation.5 | async-start | bytes 2457600 | tf_op jit(solution)/shard_map/reduce_scatter | solution.py:129
  968.7 37.3 %copy-start.4 = (bf16[320,768]{1,0:T(8,128)(2,1)S(1)}, bf16[320,768]{1,0:T(8,128)(2,1)}, u32[]{:S(2)}) copy-start(bf16[320,768]{1,0:T(8,128)(2,1)} %param.29) | copy-start | bytes 1474564
  968.8 37.3 %copy-start.37 = (f32[768]{0:T(1024)S(1)}, f32[768]{0:T(1024)}, u32[]{:S(2)}) copy-start(f32[768]{0:T(1024)} %param.39) | copy-start | bytes 9220
  968.8 37.3 %copy-start.39 = (f32[768]{0:T(1024)S(1)}, f32[768]{0:T(1024)}, u32[]{:S(2)}) copy-start(f32[768]{0:T(1024)} %param.38) | copy-start | bytes 9220
  969.3 39.5 %copy-start.44 = (f32[768]{0:T(1024)S(1)}, f32[768]{0:T(1024)}, u32[]{:S(2)}) copy-start(f32[768]{0:T(1024)} %param.40) | copy-start | bytes 9220
  969.3 39.5 %copy-start.55 = (f32[768]{0:T(1024)S(1)}, f32[768]{0:T(1024)}, u32[]{:S(2)}) copy-start(f32[768]{0:T(1024)} %param.41) | copy-start | bytes 9220
  969.4 41.6 %copy-start.14 = (bf16[24,8,2,640]{3,1,2,0:T(8,128)(2,1)}, bf16[24,8,2,640]{3,1,2,0:T(8,128)(2,1)S(1)}, u32[]{:S(2)}) copy-start(bf16[24,8,2,640]{3,1,2,0:T(8,128)(2,1)S(1)} %copy.127) | copy-start | bytes 1474564
  969.4 42.4 %copy-start.22 = (bf16[320,768]{1,0:T(8,128)(2,1)S(1)}, bf16[320,768]{1,0:T(8,128)(2,1)}, u32[]{:S(2)}) copy-start(bf16[320,768]{1,0:T(8,128)(2,1)} %param.53) | copy-start | bytes 1474564
  969.4 42.4 %copy-start.49 = (f32[768]{0:T(1024)S(1)}, f32[768]{0:T(1024)}, u32[]{:S(2)}) copy-start(f32[768]{0:T(1024)} %param.46) | copy-start | bytes 9220
  972.6 60.5 %copy-start.58 = (f32[768]{0:T(1024)S(1)}, f32[768]{0:T(1024)}, u32[]{:S(2)}) copy-start(f32[768]{0:T(1024)} %param.43) | copy-start | bytes 9220
  972.6 60.4 %all-gather.7.cloned.1.call-start = ((), (), s32[]{:S(2)}) async-start(), calls=%async_computation.6 | async-start | bytes 2457600 | tf_op jit(solution)/shard_map/all_gather | solution.py:142
  1011.0 46.0 %all-gather.9.cloned.1.call-start = ((), (), s32[]{:S(2)}) async-start(), calls=%async_computation.8 | async-start | bytes 2457600 | tf_op jit(solution)/shard_map/all_gather | solution.py:160
  1012.8 84.9 %reduce-scatter.9.cloned.1.call-start = ((), (), s32[]{:S(2)}) async-start(), calls=%async_computation.9 | async-start | bytes 2457600 | tf_op jit(solution)/shard_map/reduce_scatter | solution.py:173
  1067.0 63.8 %reduce-scatter.7.cloned.1.call-start = ((), (), s32[]{:S(2)}) async-start(), calls=%async_computation.7 | async-start | bytes 2457600 | tf_op jit(solution)/shard_map/reduce_scatter | solution.py:146
  1067.1 63.8 %copy-start.57 = (f32[768]{0:T(1024)S(1)}, f32[768]{0:T(1024)}, u32[]{:S(2)}) copy-start(f32[768]{0:T(1024)} %param.45) | copy-start | bytes 9220
  1072.0 86.3 %all-gather.11.cloned.1.call-start = ((), (), s32[]{:S(2)}) async-start(), calls=%async_computation.10 | async-start | bytes 2457600 | tf_op jit(solution)/shard_map/all_gather | solution.py:187
  1136.3 2288.2 %reduce-scatter.11.cloned.1.call-start = ((), (), s32[]{:S(2)}) async-start(), calls=%async_computation.11 | async-start | bytes 2457600 | tf_op jit(solution)/shard_map/reduce_scatter | solution.py:252
  1236.1 2231.1 %all-reduce.7.cloned.1.call-start = ((), (), s32[]{:S(2)}) async-start(), calls=%async_computation.12 | async-start | bytes 14155776 | tf_op jit(solution)/shard_map/psum | solution.py:273
  1286.9 2052.5 %copy-start.56 = (f32[768]{0:T(1024)S(1)}, f32[768]{0:T(1024)}, u32[]{:S(2)}) copy-start(f32[768]{0:T(1024)} %get-tuple-element.454) | copy-start | bytes 9220
  1360.5 2063.9 %copy-start.5 = (bf16[320,768]{1,0:T(8,128)(2,1)S(1)}, bf16[320,768]{1,0:T(8,128)(2,1)}, u32[]{:S(2)}) copy-start(bf16[320,768]{1,0:T(8,128)(2,1)} %param.29) | copy-start | bytes 1474564
  1360.5 2063.9 %copy-start.41 = (f32[320]{0:T(512)S(1)}, f32[320]{0:T(512)}, u32[]{:S(2)}) copy-start(f32[320]{0:T(512)} %copy-done.40) | copy-start | bytes 3844
  1360.5 2063.9 %copy-start.42 = (f32[768]{0:T(1024)S(1)}, f32[768]{0:T(1024)}, u32[]{:S(2)}) copy-start(f32[768]{0:T(1024)} %param.30) | copy-start | bytes 9220
  1360.5 2063.9 %copy-start.46 = (f32[320]{0:T(512)S(1)}, f32[320]{0:T(512)}, u32[]{:S(2)}) copy-start(f32[320]{0:T(512)} %copy-done.45) | copy-start | bytes 3844
  1360.5 2065.5 %copy-start.47 = (f32[768]{0:T(1024)S(1)}, f32[768]{0:T(1024)}, u32[]{:S(2)}) copy-start(f32[768]{0:T(1024)} %get-tuple-element.361) | copy-start | bytes 9220
  1360.5 2065.5 %copy-start.48 = (f32[768]{0:T(1024)S(1)}, f32[768]{0:T(1024)}, u32[]{:S(2)}) copy-start(f32[768]{0:T(1024)} %get-tuple-element.371) | copy-start | bytes 9220
  1360.6 2065.5 %copy-start.50 = (f32[768]{0:T(1024)S(1)}, f32[768]{0:T(1024)}, u32[]{:S(2)}) copy-start(f32[768]{0:T(1024)} %get-tuple-element.365) | copy-start | bytes 9220
  1360.6 2065.5 %copy-start.51 = (f32[768]{0:T(1024)S(1)}, f32[768]{0:T(1024)}, u32[]{:S(2)}) copy-start(f32[768]{0:T(1024)} %get-tuple-element.366) | copy-start | bytes 9220
  1360.6 2065.5 %copy-start.52 = (f32[768]{0:T(1024)S(1)}, f32[768]{0:T(1024)}, u32[]{:S(2)}) copy-start(f32[768]{0:T(1024)} %get-tuple-element.446) | copy-start | bytes 9220
  1360.6 2065.5 %copy-start.53 = (f32[768]{0:T(1024)S(1)}, f32[768]{0:T(1024)}, u32[]{:S(2)}) copy-start(f32[768]{0:T(1024)} %get-tuple-element.447) | copy-start | bytes 9220
  1360.6 2104.3 %copy-start.12 = (f32[320,768]{1,0:T(8,128)S(1)}, f32[320,768]{1,0:T(8,128)}, u32[]{:S(2)}) copy-start(f32[320,768]{1,0:T(8,128)} %copy-done.11) | copy-start | bytes 2949124
  (50 other events, 232.7 us)
Sparse Core Ops, SparseCore 0:
  12.7 24.5 all-gather.4
  972.7 33.3 reduce-scatter.4
  1011.1 21.8 all-gather.6
  1035.1 21.8 all-gather.8
  1067.1 30.6 reduce-scatter.8
  1100.2 30.6 reduce-scatter.6
  1136.4 21.8 all-gather.10
  1236.3 30.6 reduce-scatter.10
  1273.7 237.4 all-reduce.6
where the time goes:
time: 3510 us; the launch traced here: 3480 us
  other arithmetic  2040 us (58%)
  local copies, waits for them, and re-layouts  1070 us (30%)
  waiting for transfers between devices  150 us (4%)
  blocking collectives  121 us (3%)
  matrix products  88 us (3%)
    scatter-add x1, other arithmetic, local(): jax.ops.segment_sum(bias_grads[1][:, :P_HI, :P_HI].reshape(heads_dev, P_H...  1770 us
    gather x3, local copies, waits for them, and re-layouts, local(): table_high[index_high]  765 us
    scatter-add x1, other arithmetic, local(): jax.ops.segment_sum(bias_grads[0][:, :P_LO, :P_LO].reshape(heads_dev, P_L...  208 us
    gather x3, local copies, waits for them, and re-layouts, local(): table_low[index_low]  141 us
    psum x1, blocking collectives, local(): lax.psum((query_weight_grad, query_bias_grad, key_weight_grad, value_weig...  82.1 us
    transpose x1, local copies, waits for them, and re-layouts, local(): bias_grads[1][:, :P_HI, :P_HI].reshape(heads_dev, P_HI * P_HI)  73.7 us
  transfers between devices with their start and end apart: 9, of which 6 were waited for; matrix products, arithmetic and copies ran while one was open for 88% of the time, Pallas kernels for 0%

commit v1 on v0

--- a/solution.py
+++ b/solution.py
@@ -1,6 +1,10 @@
+import functools
+
 import jax
 import jax.numpy as jnp
 from jax import lax
+from jax.experimental import pallas as pl
+from jax.experimental.pallas import tpu as pltpu
 from jax.sharding import PartitionSpec as P
 
 HD = 64
@@ -40,6 +44,186 @@
     return 0.5 * (
         1.0 + jax.scipy.special.erf(values * inv_sqrt_two)
     ) + values * inv_sqrt_two_pi * jnp.exp(-0.5 * values * values)
+
+
+F32=jnp.float32; BF=jnp.bfloat16
+NT=(((1,),(1,)),((),()))
+def head_mask(h, width):
+    lane = lax.broadcasted_iota(jnp.int32, (1, width), 1)
+    return ((lane >= h*HD) & (lane < (h+1)*HD)).astype(F32).astype(BF)
+
+def attend_kernel(chunk, res, q_ref, k_ref, v_ref, blo, bhi, mix_ref, p_ref):
+    heads = bhi.shape[0]
+    width = q_ref.shape[1]
+    image = pl.program_id(0)
+    def run(bias, rows, cols):
+        k = k_ref[0:cols, :]
+        v = v_ref[0:cols, :]
+        vm = [v * head_mask(h, width) for h in range(heads)]
+        for start in range(0, rows, chunk):
+            size = min(chunk, rows - start)
+            q = q_ref[start:start+size, :]
+            acc = jnp.zeros((size, width), F32)
+            for h in range(heads):
+                s = lax.dot_general(q * head_mask(h, width), k, NT, preferred_element_type=F32)
+                s = s + bias[h, start:start+size, 0:cols]
+                peak = jnp.max(s, axis=1, keepdims=True)
+                e = jnp.exp(s - peak)
+                total = jnp.sum(e, axis=1, keepdims=True)
+                p = (e * (1.0 / total)).astype(BF)
+                p_ref[0, h, start:start+size, 0:cols] = p
+                acc = acc + jnp.dot(p, vm[h], preferred_element_type=F32)
+            mix_ref[start:start+size, :] = acc.astype(BF)
+        if rows < SEQ:
+            mix_ref[rows:SEQ, :] = jnp.zeros((SEQ-rows, width), BF)
+    @pl.when(res[image] == 1)
+    def _(): run(bhi, SEQ, SEQ)
+    @pl.when(res[image] != 1)
+    def _(): run(blo, blo.shape[1], blo.shape[2])
+
+def attend(res, q, k, v, blo, bhi, chunk=320):
+    heads = bhi.shape[0]; slots = q.shape[0]//SEQ; width = q.shape[1]
+    row = pl.BlockSpec((SEQ, width), lambda i: (i, 0))
+    full = lambda a: pl.BlockSpec(a.shape, lambda i: (0,)*a.ndim, pipeline_mode=pl.Buffered(1))
+    return pl.pallas_call(functools.partial(attend_kernel, chunk),
+        grid=(slots,),
+        out_shape=(jax.ShapeDtypeStruct(q.shape, BF), jax.ShapeDtypeStruct((slots, heads, SEQ, SEQ), BF)),
+        in_specs=[pl.BlockSpec(memory_space=pltpu.SMEM), row, row, row, full(blo), full(bhi)],
+        out_specs=(row, pl.BlockSpec((1, heads, SEQ, SEQ), lambda i: (i,0,0,0))),
+        name="attend", compiler_params=pltpu.CompilerParams(vmem_limit_bytes=40<<20))(res, q, k, v, blo, bhi)
+
+BB=32; UN=16
+def scatter_run(idx_ref, g_ref, out, n):
+    heads = g_ref.shape[0]; na = out.shape[1]; m = idx_ref.shape[1]
+    out[...] = jnp.zeros_like(out)
+    ib = lax.broadcasted_iota(jnp.int32, (16, m), 0).astype(F32)
+    def body(r, c):
+        ms = []; os = []
+        for u in range(UN):
+            row = r*UN+u
+            idx = jnp.broadcast_to(idx_ref[pl.ds(row,1), :], (16, m))
+            ia = (idx >> 5).astype(F32).astype(BF); il = (idx & 31).astype(F32).astype(BF)
+            g = [jnp.broadcast_to(g_ref[h, pl.ds(row,1), :], (16, m)).astype(BF) for h in range(heads)]
+            hits = [il == (ib + 16.0*k).astype(BF) for k in range(BB//16)]
+            ms.append(jnp.concatenate([jnp.where(hits[k], g[h], jnp.zeros_like(g[h])) for h in range(heads) for k in range(BB//16)], axis=0))
+            os.append(jnp.concatenate([jnp.where(ia == (ib + 16.0*k).astype(BF), jnp.ones_like(ia), jnp.zeros_like(ia)) for k in range(na//16)], axis=0))
+        out[...] += lax.dot_general(jnp.concatenate(ms, axis=1), jnp.concatenate(os, axis=1), NT, preferred_element_type=F32)
+        return c
+    lax.fori_loop(0, n//UN, body, 0)
+
+def back_kernel(scale, res, q_ref, k_ref, v_ref, p_ref, d_ref, ilo, ihi, dq_ref, dk_ref, dv_ref, sq_ref, sv_ref, tlo, thi, glo, ghi):
+    heads = ghi.shape[0]
+    width = q_ref.shape[1]
+    image = pl.program_id(0)
+    @pl.when(image == 0)
+    def _():
+        glo[...] = jnp.zeros_like(glo)
+        ghi[...] = jnp.zeros_like(ghi)
+        sq_ref[...] = jnp.zeros_like(sq_ref)
+        sv_ref[...] = jnp.zeros_like(sv_ref)
+    def run(g_ref, rows, cols):
+        k = k_ref[0:cols, :]
+        v = v_ref[0:cols, :]
+        q = q_ref[0:rows, :]
+        d = d_ref[0:rows, :]
+        qt = q.T
+        dt = d.T
+        dq = jnp.zeros((rows, width), F32)
+        dks = []; dvs = []
+        gr = min(rows, g_ref.shape[1])
+        for h in range(heads):
+            mask = head_mask(h, width)
+            p = p_ref[0, h, 0:rows, 0:cols]
+            dp = lax.dot_general(d * mask, v, NT, preferred_element_type=F32)
+            pf = p.astype(F32)
+            t = pf * dp
+            ds = t - pf * jnp.sum(t, axis=1, keepdims=True)
+            g_ref[h, 0:gr, 0:cols] += ds[0:gr]
+            low = ds.astype(BF)
+            dq = dq + jnp.dot(low, k * mask, preferred_element_type=F32)
+            dks.append(jnp.dot(qt[h*HD:(h+1)*HD], low, preferred_element_type=F32))
+            dvs.append(jnp.dot(dt[h*HD:(h+1)*HD], p, preferred_element_type=F32))
+        dq = dq * scale
+        dk = jnp.concatenate(dks, axis=0).T
+        dv = jnp.concatenate(dvs, axis=0).T
+        sq_ref[...] += jnp.sum(dq, axis=0, keepdims=True)
+        sv_ref[...] += jnp.sum(dv, axis=0, keepdims=True)
+        for ref, val, n in ((dq_ref, dq, rows), (dk_ref, dk, cols), (dv_ref, dv, cols)):
+            ref[0:n, :] = val.astype(BF)
+            if n < SEQ:
+                ref[n:SEQ, :] = jnp.zeros((SEQ-n, width), BF)
+    @pl.when(res[image] == 1)
+    def _(): run(ghi, SEQ, SEQ)
+    @pl.when(res[image] != 1)
+    def _(): run(glo, glo.shape[1], glo.shape[2])
+    @pl.when(image == pl.num_programs(0)-1)
+    def _():
+        scatter_run(ilo, glo, tlo, 208)
+        scatter_run(ihi, ghi, thi, 592)
+
+def attend_back(res, q, k, v, p, d, ilo, ihi, n_lo, n_hi, scale):
+    heads = p.shape[1]; slots = q.shape[0]//SEQ; width = q.shape[1]
+    na = lambda n: -(-(-(-n//BB))//16)*16
+    row = pl.BlockSpec((SEQ, width), lambda i: (i, 0))
+    full = lambda shape: pl.BlockSpec(shape, lambda i: (0,)*len(shape), pipeline_mode=pl.Buffered(1))
+    outs = ((heads*BB, na(n_lo)), (heads*BB, na(n_hi)))
+    dq, dk, dv, sq, sv, tlo, thi = pl.pallas_call(functools.partial(back_kernel, scale),
+        grid=(slots,),
+        out_shape=(jax.ShapeDtypeStruct(q.shape, BF),)*3+(jax.ShapeDtypeStruct((1, width), F32),)*2+tuple(jax.ShapeDtypeStruct(s, F32) for s in outs),
+        in_specs=[pl.BlockSpec(memory_space=pltpu.SMEM), row, row, row, pl.BlockSpec((1, heads, SEQ, SEQ), lambda i: (i,0,0,0)), row, full(ilo.shape), full(ihi.shape)],
+        out_specs=(row,)*3+(full((1, width)),)*2+tuple(full(s) for s in outs),
+        scratch_shapes=[pltpu.VMEM((heads,)+ilo.shape, F32), pltpu.VMEM((heads,)+ihi.shape, F32)],
+        name="attend_back", compiler_params=pltpu.CompilerParams(vmem_limit_bytes=48<<20))(res, q, k, v, p, d, ilo, ihi)
+    fix = lambda o, n: o.reshape(heads, BB, -1).transpose(2,1,0).reshape(-1, heads)[:n]
+    return dq, dk, dv, sq[0], sv[0], fix(tlo, n_lo), fix(thi, n_hi)
+
+PACK=8191.0
+def gather_kernel(tab_lo, tab_hi, idx_lo, idx_hi, out_lo, out_hi):
+    heads = out_lo.shape[0]
+    def fill(tab, idx_ref, out, rows, limit):
+        nch = tab.shape[1]
+        ncol = idx_ref.shape[1]//128
+        def body(r, c):
+            rws = pl.ds(pl.multiple_of(r*8, 8), 8)
+            for j in range(ncol):
+                cols = pl.ds(j*128, 128)
+                idx = idx_ref[rws, cols]
+                lane = idx & 127
+                ch = idx >> 7
+                shift = jnp.where(ch >= nch, 0, 16)
+                ch = jnp.where(ch >= nch, ch - nch, ch)
+                acc = [None]*heads
+                for k in range(nch):
+                    hit = ch == k
+                    for h in range(heads):
+                        v = jnp.take_along_axis(tab[h, k], lane, axis=1)
+                        acc[h] = v if k == 0 else jnp.where(hit, v, acc[h])
+                for h in range(heads):
+                    val = ((acc[h] << shift) >> 16).astype(F32) * (1.0/PACK)
+                    if (j+1)*128 > limit:
+                        col = lax.broadcasted_iota(jnp.int32, (8,128), 1) + j*128
+                        val = jnp.where(col < limit, val, masked_score)
+                    out[h, rws, cols] = val
+            return c
+        lax.fori_loop(0, -(-rows//8), body, 0)
+    fill(tab_lo, idx_lo, out_lo, P_LO, P_LO)
+    fill(tab_hi, idx_hi, out_hi, P_HI, P_HI)
+    out_lo[:, 200:, :] = jnp.zeros((heads, out_lo.shape[1]-200, out_lo.shape[2]), F32)
+    out_hi[:, 584:, :] = jnp.zeros((heads, out_hi.shape[1]-584, out_hi.shape[2]), F32)
+
+def gather_maps(table_low, table_high, idx_lo, idx_hi):
+    heads = table_low.shape[1]
+    def chunks(t):
+        n = -(-t.shape[0]//256)*256
+        w = jnp.round(jnp.pad(t.T, ((0,0),(0,n-t.shape[0]))) * PACK).astype(jnp.int32)
+        w = w.reshape(heads, 2, n//256, 1, 128)
+        w = (w[:,1] << 16) | (w[:,0] & 65535)
+        return jnp.broadcast_to(w, (heads, n//256, 8, 128))
+    vm = pl.BlockSpec(memory_space=pltpu.VMEM)
+    return pl.pallas_call(gather_kernel,
+        out_shape=(jax.ShapeDtypeStruct((heads,256,256), F32), jax.ShapeDtypeStruct((heads,SEQ,SEQ), F32)),
+        in_specs=[vm]*4, out_specs=(vm, vm), name="bias_gather",
+        compiler_params=pltpu.CompilerParams(vmem_limit_bytes=24<<20))(chunks(table_low), chunks(table_high), idx_lo, idx_hi)
 
 
 def local(
@@ -76,7 +260,6 @@
     group_rows = rows_dev * tensor_size
     heads_dev = table_low.shape[1]
     head_scale = HD ** (-0.5)
-    positions = jnp.arange(SEQ)
     slot_limits = jnp.where(resolution == 1, P_HI, P_LO)
     row_ids = lax.axis_index("tensor") * rows_dev + jnp.arange(rows_dev)
     row_slots = row_ids // SEQ
@@ -94,37 +277,10 @@
     values = (
         jnp.dot(gathered_one, value_weight, preferred_element_type=floating) + value_bias
     ).astype(bfloat)
-    shaped = (SLOTS, SEQ, heads_dev, HD)
-    queries_img = queries.reshape(shaped)
-    keys_img = keys.reshape(shaped)
-    values_img = values.reshape(shaped)
-    bias_low = jnp.pad(
-        jnp.transpose(table_low[index_low], (2, 0, 1)), ((0, 0), (0, SEQ - P_LO), (0, SEQ - P_LO))
-    )
-    bias_high = jnp.pad(
-        jnp.transpose(table_high[index_high], (2, 0, 1)), ((0, 0), (0, SEQ - P_HI), (0, SEQ - P_HI))
-    )
-
-    def scores_of(query_blk, key_blk, res_blk):
-        chosen = jnp.where(res_blk == 1, bias_high, bias_low)
-        key_bound = jnp.where(res_blk == 1, P_HI, P_LO)
-        biased = (
-            jnp.einsum("qhd,khd->hqk", query_blk, key_blk, preferred_element_type=floating) + chosen
-        )
-        return jnp.where((positions < key_bound)[None, None, :], biased, masked_score)
-
-    def attend(inputs):
-        query_blk, key_blk, value_blk, res_blk = inputs
-        scores = scores_of(query_blk, key_blk, res_blk)
-        peak = jnp.max(scores, axis=-1, keepdims=True)
-        raised = jnp.exp(scores - peak)
-        summed = jnp.sum(raised, axis=-1, keepdims=True)
-        attention = (raised / summed).astype(bfloat)
-        mixture = jnp.einsum("hqk,khd->qhd", attention, value_blk, preferred_element_type=floating)
-        return (mixture.astype(bfloat), (peak + jnp.log(summed))[..., 0])
-
-    mixture_img, log_totals = lax.map(attend, (queries_img, keys_img, values_img, resolution))
-    mixture_rows = mixture_img.reshape(group_rows, heads_dev * HD)
+    index_low_pad = jnp.pad(index_low, ((0, 256 - P_LO), (0, 256 - P_LO)))
+    index_high_pad = jnp.pad(index_high, ((0, 592 - P_HI), (0, SEQ - P_HI)))
+    bias_low, bias_high = gather_maps(table_low, table_high, index_low_pad, index_high_pad)
+    mixture_rows, attention = attend(resolution, queries, keys, values, bias_low, bias_high)
     attn_out = (
         lax.psum_scatter(
             jnp.dot(mixture_rows, output_weight, preferred_element_type=floating).astype(
@@ -192,50 +348,26 @@
         "rd,cd->rc", gathered_attn_grad, output_weight, preferred_element_type=floating
     ).astype(bfloat)
 
-    def attend_back(totals, inputs):
-        grad_low, grad_high = totals
-        query_blk, key_blk, value_blk, res_blk, lse_blk, back_blk = inputs
-        scores = scores_of(query_blk, key_blk, res_blk)
-        attention = jnp.exp(scores - lse_blk[..., None])
-        prob_grad = jnp.einsum("qhd,khd->hqk", back_blk, value_blk, preferred_element_type=floating)
-        score_grad = attention * (
-            prob_grad - jnp.sum(attention * prob_grad, axis=-1, keepdims=True)
-        )
-        score_low = score_grad.astype(bfloat)
-        query_grad = (
-            jnp.einsum("hqk,khd->qhd", score_low, key_blk, preferred_element_type=floating)
-            * head_scale
-        )
-        key_grad = jnp.einsum("hqk,qhd->khd", score_low, query_blk, preferred_element_type=floating)
-        value_grad = jnp.einsum(
-            "hqk,qhd->khd", attention.astype(bfloat), back_blk, preferred_element_type=floating
-        )
-        is_high = jnp.where(res_blk == 1, 1.0, 0.0).astype(floating)
-        totals = (grad_low + (1.0 - is_high) * score_grad, grad_high + is_high * score_grad)
-        return (totals, (query_grad, key_grad.astype(bfloat), value_grad))
-
-    empty_map = jnp.zeros((heads_dev, SEQ, SEQ), floating)
-    bias_grads, per_slot = lax.scan(
-        attend_back,
-        (empty_map, empty_map),
-        (queries_img, keys_img, values_img, resolution, log_totals, mixture_grad.reshape(shaped)),
-    )
-    query_grad = per_slot[0].reshape(group_rows, heads_dev * HD)
-    key_low = per_slot[1].reshape(group_rows, heads_dev * HD)
-    value_grad = per_slot[2].reshape(group_rows, heads_dev * HD)
-    query_bias_grad = jnp.sum(query_grad, axis=0)
-    value_bias_grad = jnp.sum(value_grad, axis=0)
-    query_low = query_grad.astype(bfloat)
-    value_low = value_grad.astype(bfloat)
-    table_low_grad = jax.ops.segment_sum(
-        bias_grads[0][:, :P_LO, :P_LO].reshape(heads_dev, P_LO * P_LO).T,
-        index_low.reshape(P_LO * P_LO),
-        num_segments=table_low.shape[0],
-    )
-    table_high_grad = jax.ops.segment_sum(
-        bias_grads[1][:, :P_HI, :P_HI].reshape(heads_dev, P_HI * P_HI).T,
-        index_high.reshape(P_HI * P_HI),
-        num_segments=table_high.shape[0],
+    (
+        query_low,
+        key_low,
+        value_low,
+        query_bias_grad,
+        value_bias_grad,
+        table_low_grad,
+        table_high_grad,
+    ) = attend_back(
+        resolution,
+        queries,
+        keys,
+        values,
+        attention,
+        mixture_grad,
+        index_low_pad,
+        index_high_pad,
+        table_low.shape[0],
+        table_high.shape[0],
+        head_scale,
     )
     query_weight_grad = jnp.einsum(
         "rd,rc->dc", gathered_one, query_low, preferred_element_type=floating

time: 3510 us -> 581 us (0.17)
  other arithmetic: 2040 us -> 21.4 us
  local copies, waits for them, and re-layouts: 1070 us -> 26.5 us
  waiting for transfers between devices: 150 us -> 331 us
  Pallas kernels: 0 us -> 56.8 us
  matrix products: 88 us -> 46.7 us
  blocking collectives: 121 us -> 81.1 us
    scatter-add x2 -> x0, other arithmetic: 1980 us -> none  [the longest x1 1770 us: local(): jax.ops.segment_sum(bias_grads[1][:, :P_HI, :P_HI].reshape(heads_dev, P_H...]
    gather x6 -> x0, local copies, waits for them, and re-layouts: 906 us -> none  [the longest x3 765 us: local(): table_high[index_high]]
    psum x1, waiting for transfers between devices: 0.01 us -> 179 us  [local(): lax.psum((query_weight_grad, query_bias_grad, key_weight_grad, value_weig...]
    transpose x2 -> x1, local copies, waits for them, and re-layouts: 84 us -> 0.08 us  [attend_back(): o.reshape(heads, BB, -1).transpose(2, 1, 0).reshape(-1, heads)[:n]]
    pallas_call x0 -> x3, Pallas kernels: none -> 56.8 us  [the longest x1 34.8 us: attend_back(): pl.pallas_call(functools.partial(back_kernel, scale), grid=(slots,), out_...]
    psum x1, blocking collectives: 82.1 us -> 39.5 us  [local(): lax.psum((query_weight_grad, query_bias_grad, key_weight_grad, value_weig...]
    dot_general x14 -> x0, matrix products: 38.2 us -> none  [the longest x4 19.5 us: scores_of(): jnp.einsum('qhd,khd->hqk', query_blk, key_blk, preferred_element_type=flo...]
  transfers between devices with their start and end apart: 9 -> 9, of which waited for: 6 -> 8; matrix products, arithmetic and copies ran while one was open for 88% -> 6% of each run, Pallas kernels for 0% -> 3%
where the time goes in v1:
time: 581 us; the launch traced here: 579 us
  waiting for transfers between devices  331 us (57%)
  blocking collectives  81.1 us (14%)
  Pallas kernels  56.8 us (10%)
  matrix products  46.7 us (8%)
  local copies, waits for them, and re-layouts  26.5 us (5%)
  other arithmetic  21.4 us (4%)
  between operations  15.3 us (3%)
    psum x1, waiting for transfers between devices, local(): lax.psum((query_weight_grad, query_bias_grad, key_weight_grad, value_weig...  179 us
    psum x1, blocking collectives, local(): lax.psum((first_gain_grad, first_shift_grad, first_scale_grad, output_bia...  41.6 us
    psum x1, blocking collectives, local(): lax.psum((query_weight_grad, query_bias_grad, key_weight_grad, value_weig...  39.5 us
    reduce_scatter x1, waiting for transfers between devices, local(): lax.psum_scatter(jnp.dot(mixture_rows, output_weight, preferred_element_t...  36.9 us
    pallas_call x1, Pallas kernels, attend_back(): pl.pallas_call(functools.partial(back_kernel, scale), grid=(slots,), out_...  34.8 us
    reduce_scatter x1, waiting for transfers between devices, local(): lax.psum_scatter(jnp.dot(activated, reduce_weight, preferred_element_type...  30.8 us
    reduce_scatter x1, waiting for transfers between devices, local(): lax.psum_scatter(jnp.einsum('rf,df->rd', pre_grad_low, expand_weight, pre...  24.9 us
    unnamed x134, local copies, waits for them, and re-layouts  24.3 us
  transfers between devices with their start and end apart: 9, of which 8 were waited for; matrix products, arithmetic and copies ran while one was open for 6% of the time, Pallas kernels for 3%

profile of v1, /device:TPU:0, one launch (start us, length us, event | category | flops | bytes accessed | tf_op | source)
XLA Modules:
  0.0 579.4 jit_solution(10464964549703063628)
XLA Ops:
  9.9 2.1 fusion.18
  13.8 19.7 %bias_gather.1 = (f32[3,256,256]{2,1,0:T(8,128)S(1)}, f32[3,640,640]{2,1,0:T(8,128)S(1)}) custom-call(s32[3,3,8,128]{3,2,1,0:T(8,128)S(1)} %broadcast_in_dim.24.tab_lo, s32[3,9,8,128]{3,2,1,0:T(8,128)S(1)} %broadcast_in_dim.25.tab_hi, s32[256,256]{1,0:T(8,128)S(1)} %pad.18.idx_lo.ilo, s32[592,640]{1,0:T(8,128)S(1)} %pad.19.idx_hi.ihi), custom_call_target="tpu_custom_call" | custom-call | tf_op jit(solution)/shard_map/bias_gather/pallas_call | solution.py:223
  33.5 2.2 copy-done.4
  36.7 2.4 convolution_convert_fusion.3.k_ref
  39.2 2.5 fusion.5.v_ref
  43.1 2.3 attend.1
  45.5 2.2 copy-done.3
  47.7 1.9 convolution_convert_fusion
  49.7 36.9 %reduce-scatter.5.cloned.1.call-done = bf16[320,768]{1,0:T(8,128)(2,1)} async-done(((bf16[1280,768]{1,0:T(8,128)(2,1)}), bf16[320,768]{1,0:T(8,128)(2,1)}) %reduce-scatter.5.cloned.1.call-update) | async-done | bytes 491536 | tf_op jit(solution)/shard_map/reduce_scatter | solution.py:285
  91.4 2.0 fusion.35
  93.7 18.9 %all-gather.7.cloned.1.call-done = bf16[1280,768]{1,0:T(8,128)(2,1)} async-done(((bf16[320,768]{1,0:T(8,128)(2,1)}), bf16[1280,768]{1,0:T(8,128)(2,1)}) %all-gather.7.cloned.1.call-update) | async-done | bytes 1966096 | tf_op jit(solution)/shard_map/all_gather | solution.py:298
  112.6 5.8 %multiply_convert_fusion = (bf16[1280,768]{1,0:T(8,128)(2,1)}, f32[1280,768]{1,0:T(8,128)}) fusion(f32[768]{0:T(1024)S(1)} %copy-done.59, bf16[1280,768]{1,0:T(8,128)(2,1)} %all-gather.7.cloned.1.call-done, bf16[768,768]{1,0:T(8,128)(2,1)S(1)} %copy-done), kind=kOutput, calls=%fused_computation.7 | convolution fusion | flops 1515847680 | bytes 9047040 | tf_op jit(solution)/shard_map/dot_general | solution.py:299
  118.4 18.1 %all-gather.9.cloned.1.call-done = bf16[1280,768]{1,0:T(8,128)(2,1)} async-done(((bf16[320,768]{1,0:T(8,128)(2,1)}), bf16[1280,768]{1,0:T(8,128)(2,1)}) %all-gather.9.cloned.1.call-update) | async-done | bytes 1966096 | tf_op jit(solution)/shard_map/all_gather | solution.py:316
  136.6 5.7 fusion.49
  143.6 3.0 convolution_convert_fusion.1
  147.9 4.5 convolution_convert_fusion.2
  152.5 24.9 %reduce-scatter.9.cloned.1.call-done = bf16[320,768]{1,0:T(8,128)(2,1)} async-done(((bf16[1280,768]{1,0:T(8,128)(2,1)}), bf16[320,768]{1,0:T(8,128)(2,1)}) %reduce-scatter.9.cloned.1.call-update) | async-done | bytes 491536 | tf_op jit(solution)/shard_map/reduce_scatter | solution.py:329
  177.4 2.3 fusion.28
  179.7 30.8 %reduce-scatter.7.cloned.1.call-done = bf16[320,768]{1,0:T(8,128)(2,1)} async-done(((bf16[1280,768]{1,0:T(8,128)(2,1)}), bf16[320,768]{1,0:T(8,128)(2,1)}) %reduce-scatter.7.cloned.1.call-update) | async-done | bytes 491536 | tf_op jit(solution)/shard_map/reduce_scatter | solution.py:302
  210.5 3.6 multiply_reduce_fusion.1
  216.2 21.8 %all-gather.11.cloned.1.call-done = bf16[1280,768]{1,0:T(8,128)(2,1)} async-done(((bf16[320,768]{1,0:T(8,128)(2,1)}), bf16[1280,768]{1,0:T(8,128)(2,1)}) %all-gather.11.cloned.1.call-update) | async-done | bytes 1966096 | tf_op jit(solution)/shard_map/all_gather | solution.py:343
  237.9 2.3 convolution_convert_fusion.4
  243.8 34.8 %attend_back.1 = (bf16[1280,192]{1,0:T(8,128)(2,1)S(1)}, bf16[1280,192]{1,0:T(8,128)(2,1)S(1)}, bf16[1280,192]{1,0:T(8,128)(2,1)S(1)}, f32[1,192]{1,0:T(1,128)S(...) custom-call(s32[2]{0:T(128)S(1)} %copy-done.17, bf16[1280,192]{1,0:T(8,128)(2,1)S(1)} %copy-done.10, ...), custom_call_target="tpu_custom_call" | custom-call | tf_op jit(solution)/shard_map/attend_back/pallas_call | solution.py:170
  280.5 2.1 fusion.3
  283.0 5.4 fusion.30
  288.4 3.2 fusion.55
  299.1 39.5 %all-reduce.5 = (f32[192]{0:T(256)}, f32[192]{0:T(256)}, f32[768]{0:T(1024)}, f32[732,3]{0,1:T(4,128)}, f32[2212,3]{0,1:T(4,128)}) all-reduce(f32[192]{0:T(256)S(1)} %bitcast.59, f32[192]{0:T(256)S(1)} %bitcast.60, f32[768]{0:T(1024)S(1)} %copy-done.56, f32[732,3]{0,1:T(4,128)S(1)} %slice.28, ...), channel_id=1, replica_groups=mesh['dp'=8,'tensor'=4] {'dp'}, use_global_device_ids=true, to_apply=%region_18.19 | all-reduce | flops 9984 | bytes 79872 | tf_op jit(solution)/shard_map/psum | solution.py:405
  340.3 41.6 %all-reduce.4 = (f32[768]{0:T(1024)}, f32[768]{0:T(1024)}, f32[768]{0:T(1024)}, f32[768]{0:T(1024)}, f32[768]{0:T(1024)}, /*index=5*/f32[768]{0:T(1024)}, f32[768]{0:T(1024)}, f32[768]{0:T(1024)}) all-reduce(f32[768]{0:T(1024)S(1)} %get-tuple-element.45, ...), channel_id=1, replica_groups=mesh['dp'=8,'tensor'=4] {'dp','tensor'}, use_global_device_ids=true, to_apply=%region_14.15 | all-reduce | flops 6144 | bytes 49152 | tf_op jit(solution)/shard_map/psum | solution.py:430
  381.9 2.3 fusion.21
  384.2 179.0 %all-reduce.9.cloned.1.call-done = (f32[768,192]{0,1:T(8,128)}, f32[768,192]{0,1:T(8,128)}, f32[768,192]{0,1:T(8,128)}, f32[192,768]{1,0:T(8,128)}, f32[768,768]{1,0:T(8,128)}, /*index=5*/f32[768,768]{1,0:T(8,128)}) async-done(((f32[768,192]{0,1:T(8,128)}, f32[768,192]{0,1:T(8,128)}, f32[768,192]{0,1:T(8,128)}, f32[192,768]{1,0:T(8,128)}, f32[768,768]{1,0:T(8,128)}, /*index=5*/f32[768,768]{1,0:T(8,128)}), ...) | async-done | bytes 7077904 | tf_op jit(solution)/shard_map/psum | solution.py:405
  563.3 2.0 copy.84
  565.3 2.1 copy.85
  (193 shorter events, 36.1 us)
Async XLA Ops:
  7.2 105.4 %copy-start = (bf16[768,768]{1,0:T(8,128)(2,1)S(1)}, bf16[768,768]{1,0:T(8,128)(2,1)}, u32[]{:S(2)}) copy-start(bf16[768,768]{1,0:T(8,128)(2,1)} %param.38) | copy-start | bytes 3538948
  7.2 29.5 %all-gather.5.cloned.1.call-start = ((), (), s32[]{:S(2)}) async-start(), calls=%async_computation.4 | async-start | bytes 2457600 | tf_op jit(solution)/shard_map/all_gather | solution.py:271
  12.0 74.6 %reduce-scatter.5.cloned.1.call-start = ((), (), s32[]{:S(2)}) async-start(), calls=%async_computation.5 | async-start | bytes 2457600 | tf_op jit(solution)/shard_map/reduce_scatter | solution.py:285
  13.7 25.4 %copy-start.2 = (s32[592,640]{1,0:T(8,128)}, s32[592,640]{1,0:T(8,128)S(1)}, u32[]{:S(2)}) copy-start(s32[592,640]{1,0:T(8,128)S(1)} %pad.19.idx_hi.ihi) | copy-start | bytes 4546564
  13.8 27.9 %copy-start.34 = (bf16[768,192]{0,1:T(8,128)(2,1)S(1)}, bf16[768,192]{0,1:T(8,128)(2,1)}, u32[]{:S(2)}) copy-start(bf16[768,192]{0,1:T(8,128)(2,1)} %param.28) | copy-start | bytes 884740
  47.7 39.0 %copy-start.20 = (bf16[320,768]{1,0:T(8,128)(2,1)S(1)}, bf16[320,768]{1,0:T(8,128)(2,1)}, u32[]{:S(2)}) copy-start(bf16[320,768]{1,0:T(8,128)(2,1)} %param.25) | copy-start | bytes 1474564
  47.7 39.0 %copy-start.40 = (f32[768]{0:T(1024)S(1)}, f32[768]{0:T(1024)}, u32[]{:S(2)}) copy-start(f32[768]{0:T(1024)} %param.35) | copy-start | bytes 9220
  47.7 39.0 %copy-start.41 = (f32[768]{0:T(1024)S(1)}, f32[768]{0:T(1024)}, u32[]{:S(2)}) copy-start(f32[768]{0:T(1024)} %param.34) | copy-start | bytes 9220
  49.6 39.8 %copy-start.44 = (f32[768]{0:T(1024)S(1)}, f32[768]{0:T(1024)}, u32[]{:S(2)}) copy-start(f32[768]{0:T(1024)} %param.36) | copy-start | bytes 9220
  49.6 39.8 %copy-start.55 = (f32[768]{0:T(1024)S(1)}, f32[768]{0:T(1024)}, u32[]{:S(2)}) copy-start(f32[768]{0:T(1024)} %param.37) | copy-start | bytes 9220
  49.6 41.8 %copy-start.49 = (f32[768]{0:T(1024)S(1)}, f32[768]{0:T(1024)}, u32[]{:S(2)}) copy-start(f32[768]{0:T(1024)} %param.42) | copy-start | bytes 9220
  49.6 63.0 %all-gather.7.cloned.1.call-start = ((), (), s32[]{:S(2)}) async-start(), calls=%async_computation.6 | async-start | bytes 2457600 | tf_op jit(solution)/shard_map/all_gather | solution.py:298
  89.4 23.2 %copy-start.59 = (f32[768]{0:T(1024)S(1)}, f32[768]{0:T(1024)}, u32[]{:S(2)}) copy-start(f32[768]{0:T(1024)} %param.39) | copy-start | bytes 9220
  90.6 46.0 %all-gather.9.cloned.1.call-start = ((), (), s32[]{:S(2)}) async-start(), calls=%async_computation.8 | async-start | bytes 2457600 | tf_op jit(solution)/shard_map/all_gather | solution.py:316
  93.5 84.0 %reduce-scatter.9.cloned.1.call-start = ((), (), s32[]{:S(2)}) async-start(), calls=%async_computation.9 | async-start | bytes 2457600 | tf_op jit(solution)/shard_map/reduce_scatter | solution.py:329
  146.6 63.8 %reduce-scatter.7.cloned.1.call-start = ((), (), s32[]{:S(2)}) async-start(), calls=%async_computation.7 | async-start | bytes 2457600 | tf_op jit(solution)/shard_map/reduce_scatter | solution.py:302
  152.4 58.1 %copy-start.31 = (bf16[320,768]{1,0:T(8,128)(2,1)S(1)}, bf16[320,768]{1,0:T(8,128)(2,1)}, u32[]{:S(2)}) copy-start(bf16[320,768]{1,0:T(8,128)(2,1)} %param.49) | copy-start | bytes 1474564
  152.4 58.1 %copy-start.57 = (f32[768]{0:T(1024)S(1)}, f32[768]{0:T(1024)}, u32[]{:S(2)}) copy-start(f32[768]{0:T(1024)} %param.41) | copy-start | bytes 9220
  152.4 85.5 %all-gather.11.cloned.1.call-start = ((), (), s32[]{:S(2)}) async-start(), calls=%async_computation.10 | async-start | bytes 2457600 | tf_op jit(solution)/shard_map/all_gather | solution.py:343
  215.9 122.7 %reduce-scatter.11.cloned.1.call-start = ((), (), s32[]{:S(2)}) async-start(), calls=%async_computation.11 | async-start | bytes 2457600 | tf_op jit(solution)/shard_map/reduce_scatter | solution.py:384
  243.8 34.8 %copy-start.35 = (bf16[768,192]{0,1:T(8,128)(2,1)S(1)}, bf16[768,192]{0,1:T(8,128)(2,1)}, u32[]{:S(2)}) copy-start(bf16[768,192]{0,1:T(8,128)(2,1)} %param.28) | copy-start | bytes 884740
  282.6 280.6 %all-reduce.9.cloned.1.call-start = ((), (), s32[]{:S(2)}) async-start(), calls=%async_computation.12 | async-start | bytes 14155776 | tf_op jit(solution)/shard_map/psum | solution.py:405
  297.9 40.8 %copy-start.21 = (bf16[320,768]{1,0:T(8,128)(2,1)S(1)}, bf16[320,768]{1,0:T(8,128)(2,1)}, u32[]{:S(2)}) copy-start(bf16[320,768]{1,0:T(8,128)(2,1)} %param.25) | copy-start | bytes 1474564
  297.9 40.8 %copy-start.42 = (f32[768]{0:T(1024)S(1)}, f32[768]{0:T(1024)}, u32[]{:S(2)}) copy-start(f32[768]{0:T(1024)} %param.26) | copy-start | bytes 9220
  297.9 40.7 %copy-start.46 = (f32[320]{0:T(512)S(1)}, f32[320]{0:T(512)}, u32[]{:S(2)}) copy-start(f32[320]{0:T(512)} %copy-done.45) | copy-start | bytes 3844
  297.9 42.3 %copy-start.47 = (f32[768]{0:T(1024)S(1)}, f32[768]{0:T(1024)}, u32[]{:S(2)}) copy-start(f32[768]{0:T(1024)} %get-tuple-element.43) | copy-start | bytes 9220
  297.9 42.3 %copy-start.48 = (f32[768]{0:T(1024)S(1)}, f32[768]{0:T(1024)}, u32[]{:S(2)}) copy-start(f32[768]{0:T(1024)} %get-tuple-element.53) | copy-start | bytes 9220
  297.9 42.3 %copy-start.50 = (f32[768]{0:T(1024)S(1)}, f32[768]{0:T(1024)}, u32[]{:S(2)}) copy-start(f32[768]{0:T(1024)} %get-tuple-element.47) | copy-start | bytes 9220
  297.9 42.3 %copy-start.51 = (f32[768]{0:T(1024)S(1)}, f32[768]{0:T(1024)}, u32[]{:S(2)}) copy-start(f32[768]{0:T(1024)} %get-tuple-element.48) | copy-start | bytes 9220
  298.0 42.3 %copy-start.52 = (f32[768]{0:T(1024)S(1)}, f32[768]{0:T(1024)}, u32[]{:S(2)}) copy-start(f32[768]{0:T(1024)} %get-tuple-element.76) | copy-start | bytes 9220
  298.0 42.3 %copy-start.53 = (f32[768]{0:T(1024)S(1)}, f32[768]{0:T(1024)}, u32[]{:S(2)}) copy-start(f32[768]{0:T(1024)} %get-tuple-element.77) | copy-start | bytes 9220
  298.0 83.9 %copy-start.24 = (f32[320,768]{1,0:T(8,128)S(1)}, f32[320,768]{1,0:T(8,128)}, u32[]{:S(2)}) copy-start(f32[320,768]{1,0:T(8,128)} %copy-done.23) | copy-start | bytes 2949124
  (41 other events, 107.5 us)
Sparse Core Ops, SparseCore 0:
  12.1 24.5 all-gather.4
  49.7 36.8 reduce-scatter.4
  90.7 21.8 all-gather.6
  114.7 21.8 all-gather.8
  146.8 30.6 reduce-scatter.8
  179.8 30.6 reduce-scatter.6
  216.0 21.8 all-gather.10
  282.8 35.1 reduce-scatter.10
  324.8 238.4 all-reduce.8

commit v2 on v1

v2 whole, which is shorter than its diff:
```python
import functools

import jax
import jax.numpy as jnp
from jax import lax
from jax.experimental import pallas as pl
from jax.experimental.pallas import tpu as pltpu
from jax.sharding import PartitionSpec as P

HD = 64
P_LO = 197
P_HI = 577
SEQ = 640
SLOTS = 2


eps_norm = 1e-06
masked_score = -1e30
inv_sqrt_two = 0.7071067811865476
inv_sqrt_two_pi = 0.3989422804014327


def normalize(values, gain, shift):
    center = jnp.mean(values, axis=-1, keepdims=True)
    centered = values - center
    variance = jnp.mean(centered * centered, axis=-1, keepdims=True)
    inverse = lax.rsqrt(variance + eps_norm)
    return centered * inverse * gain + shift


F32=jnp.float32; BF=jnp.bfloat16
NT=(((1,),(1,)),((),()))
def head_mask(h, width):
    lane = lax.broadcasted_iota(jnp.int32, (1, width), 1)
    return ((lane >= h*HD) & (lane < (h+1)*HD)).astype(F32).astype(BF)

def row(ref):
    return ref[...].reshape(1, ref.shape[0])

def live_of(t, rows, res, counts):
    slot = t * rows // SEQ
    first = t * rows - slot * SEQ
    limit = jnp.where(res[slot] == 1, P_HI, P_LO)
    limit = jnp.where(slot < counts[0], limit, 0)
    place = lax.broadcasted_iota(jnp.int32, (rows, 1), 0) + first
    return jnp.where(place < limit, 1.0, 0.0).astype(F32)

def moments(values):
    center = jnp.mean(values, axis=1, keepdims=True)
    centered = values - center
    inverse = lax.rsqrt(jnp.mean(centered * centered, axis=1, keepdims=True) + eps_norm)
    return centered * inverse, inverse


BB=32; UN=16
def scatter_run(idx_ref, g_ref, out, first, last, fresh):
    heads = g_ref.shape[0]; na = out.shape[1]; m = idx_ref.shape[1]
    if fresh:
        out[...] = jnp.zeros_like(out)
    ib = lax.broadcasted_iota(jnp.int32, (16, m), 0).astype(F32)
    def body(r, c):
        ms = []; os = []
        for u in range(UN):
            row = r*UN+u
            idx = jnp.broadcast_to(idx_ref[pl.ds(row,1), :], (16, m))
            ia = (idx >> 5).astype(F32).astype(BF); il = (idx & 31).astype(F32).astype(BF)
            g = [jnp.broadcast_to(g_ref[h, pl.ds(row,1), :], (16, m)).astype(BF) for h in range(heads)]
            hits = [il == (ib + 16.0*k).astype(BF) for k in range(BB//16)]
            ms.append(jnp.concatenate([jnp.where(hits[k], g[h], jnp.zeros_like(g[h])) for h in range(heads) for k in range(BB//16)], axis=0))
            os.append(jnp.concatenate([jnp.where(ia == (ib + 16.0*k).astype(BF), jnp.ones_like(ia), jnp.zeros_like(ia)) for k in range(na//16)], axis=0))
        out[...] += lax.dot_general(jnp.concatenate(ms, axis=1), jnp.concatenate(os, axis=1), NT, preferred_element_type=F32)
        return c
    lax.fori_loop(first, last, body, 0)

PACK=8191.0
def gather_kernel(res, tab_lo, tab_hi, idx_lo, idx_hi, out):
    heads = out.shape[1]
    slots = out.shape[0]
    def fill(code, tab, idx_ref, rows, limit):
        nch = tab.shape[1]
        ncol = idx_ref.shape[1]//128
        def body(r, c):
            rws = pl.ds(pl.multiple_of(r*8, 8), 8)
            vals = []
            for j in range(ncol):
                idx = idx_ref[rws, pl.ds(j*128, 128)]
                lane = idx & 127
                ch = idx >> 7
                shift = jnp.where(ch >= nch, 0, 16)
                ch = jnp.where(ch >= nch, ch - nch, ch)
                acc = [None]*heads
                for k in range(nch):
                    hit = ch == k
                    for h in range(heads):
                        v = jnp.take_along_axis(tab[h, k], lane, axis=1)
                        acc[h] = v if k == 0 else jnp.where(hit, v, acc[h])
                for h in range(heads):
                    val = ((acc[h] << shift) >> 16).astype(F32) * (1.0/PACK)
                    if (j+1)*128 > limit:
                        col = lax.broadcasted_iota(jnp.int32, (8,128), 1) + j*128
                        val = jnp.where(col < limit, val, masked_score)
                    vals.append((h, j, val))
            for s in range(slots):
                @pl.when(res[s] == code)
                def _():
                    for h, j, val in vals:
                        out[s, h, rws, pl.ds(j*128, 128)] = val
            return c
        lax.fori_loop(0, -(-rows//8), body, 0)
    for s in range(slots):
        @pl.when(res[s] == 1)
        def _():
            out[s, :, 584:, :] = jnp.zeros((heads, SEQ-584, SEQ), F32)
        @pl.when(res[s] != 1)
        def _():
            out[s] = jnp.full((heads, SEQ, SEQ), masked_score, F32)
    low = res[0] != 1
    high = res[0] == 1
    for s in range(1, slots):
        low = low | (res[s] != 1)
        high = high | (res[s] == 1)
    @pl.when(low)
    def _(): fill(0, tab_lo, idx_lo, P_LO, P_LO)
    @pl.when(high)
    def _(): fill(1, tab_hi, idx_hi, P_HI, P_HI)

def gather_maps(res, table_low, table_high, idx_lo, idx_hi):
    heads = table_low.shape[1]
    def chunks(t):
        n = -(-t.shape[0]//256)*256
        w = jnp.round(jnp.pad(t.T, ((0,0),(0,n-t.shape[0]))) * PACK).astype(jnp.int32)
        w = w.reshape(heads, 2, n//256, 1, 128)
        w = (w[:,1] << 16) | (w[:,0] & 65535)
        return jnp.broadcast_to(w, (heads, n//256, 8, 128))
    vm = pl.BlockSpec(memory_space=pltpu.VMEM)
    return pl.pallas_call(gather_kernel,
        out_shape=jax.ShapeDtypeStruct((SLOTS,heads,SEQ,SEQ), F32),
        in_specs=[pl.BlockSpec(memory_space=pltpu.SMEM)]+[vm]*4, out_specs=vm, name="bias_gather", cost_estimate=pl.CostEstimate(flops=20*10**9, bytes_accessed=8*10**6, transcendentals=0),
        compiler_params=pltpu.CompilerParams(vmem_limit_bytes=24<<20))(res, chunks(table_low), chunks(table_high), idx_lo, idx_hi)

MESH = pl.DeviceIdType.MESH
TN=(((0,),(0,)),((),()))

def middle_kernel(scale, res, counts, g1, wq, bq, wk, wv, bv, bias, wo, bo, resid, scale1, gain2, shift2, we, be, wr, cot, scale2,
                  q_out, k_out, v_out, mix, p_out, part, ga, dmix, x0, x1, after_attn, after_grad, sums, esum,
                  upstream, gm, gt, act, pgl, acc, xhat, inv2, attn,
                  cbuf, ccore, xbuf, xin, m_s, m_r, t_s, t_r, a_s, a_r, o_s, o_r, n_s, n_r):
    d = lax.axis_index("dp")
    t = lax.axis_index("tensor")
    rows = resid.shape[0]
    half = rows // 2
    heads = p_out.shape[1]
    width = q_out.shape[1]
    sibling = t + 1 - 2 * lax.rem(t, 2)
    cross = lax.rem(t + 2, 4)
    diag = 3 - t
    barrier = pltpu.get_barrier_semaphore()
    for k in range(1, 4):
        pl.semaphore_signal(barrier, inc=1, device_id=(d, lax.rem(t + k, 4)), device_id_type=MESH)
    pl.semaphore_wait(barrier, 3)

    def remote(src, dst, send, recv, who):
        return pltpu.make_async_remote_copy(src_ref=src, dst_ref=dst, send_sem=send, recv_sem=recv, device_id=(d, who), device_id_type=MESH)
    def span(who, h):
        return pl.ds(pl.multiple_of(who * rows + h * half, 16), half)
    def gather_x(buf, send, recv, h):
        here = buf.at[span(t, h)]
        return remote(here, here, send.at[h], recv.at[h], cross)
    def gather_near(buf, send, recv, h):
        here = buf.at[span(t, h)]
        return remote(here, here, send.at[2 + h], recv.at[2 + h], sibling)
    def gather_on(buf, send, recv, h):
        here = buf.at[span(cross, h)]
        return remote(here, here, send.at[4 + h], recv.at[4 + h], sibling)
    def sum_far(j, send, recv, h):
        return remote(cbuf.at[j, 0, h], ccore.at[j, 0, h], send.at[h], recv.at[h], sibling)
    def sum_near(j, send, recv, h):
        return remote(cbuf.at[j, 1, h], ccore.at[j, 1, h], send.at[2 + h], recv.at[2 + h], sibling)
    def sum_x(j, send, recv, h):
        return remote(xbuf.at[j, h], xin.at[j, h], send.at[4 + h], recv.at[4 + h], cross)

    upstream[...] = cot[...].astype(F32) * live_of(t, rows, res, counts)
    gm[pl.ds(pl.multiple_of(t * rows, 16), rows)] = (upstream[...] * row(scale2)).astype(BF)
    for h in range(2):
        gather_x(gm, m_s, m_r, h).start()
        gather_near(gm, m_s, m_r, h).start()
    def project(i, c):
        here = pl.ds(pl.multiple_of(i * rows, 16), rows)
        g = g1[here]
        q_out[here] = ((lax.dot_general(g, wq[...], NT, preferred_element_type=F32) + row(bq)) * scale).astype(BF)
        k_out[here] = lax.dot_general(g, wk[...], NT, preferred_element_type=F32).astype(BF)
        v_out[here] = (lax.dot_general(g, wv[...], NT, preferred_element_type=F32) + row(bv)).astype(BF)
        return c
    lax.fori_loop(0, 4, project, 0)

    def attend_image(slot):
        here = pl.ds(pl.multiple_of(slot * SEQ, 16), SEQ)
        k = k_out[here]
        v = v_out[here]
        vm = [v * head_mask(h, width) for h in range(heads)]
        def piece(i, c):
            first = pl.multiple_of(i * rows, 16)
            q = q_out[pl.ds(pl.multiple_of(slot * SEQ + first, 16), rows)]
            out = jnp.zeros((rows, width), F32)
            for h in range(heads):
                s = lax.dot_general(q * head_mask(h, width), k, NT, preferred_element_type=F32)
                s = s + bias[slot, h, pl.ds(first, rows)]
                peak = jnp.max(s, axis=1, keepdims=True)
                e = jnp.exp(s - peak)
                total = jnp.sum(e, axis=1, keepdims=True)
                p = (e * (1.0 / total)).astype(BF)
                p_out[slot, h, pl.ds(first, rows)] = p
                out = out + jnp.dot(p, vm[h], preferred_element_type=F32)
            mix[pl.ds(pl.multiple_of(slot * SEQ + first, 16), rows)] = out.astype(BF)
            return c
        lax.fori_loop(0, SEQ // rows, piece, 0)
    def output_of(who, h):
        return jnp.dot(mix[span(who, h)], wo[...], preferred_element_type=F32)

    mine = t // 2
    attend_image(1 - mine)
    for h in range(2):
        cbuf[0, 0, h] = output_of(diag, h).astype(BF)
        sum_far(0, o_s, o_r, h).start()
    for h in range(2):
        total = output_of(cross, h)
        sum_far(0, o_s, o_r, h).wait()
        xbuf[0, h] = (total + ccore[0, 0, h].astype(F32)).astype(BF)
        sum_x(0, o_s, o_r, h).start()
    attend_image(mine)
    for h in range(2):
        cbuf[0, 1, h] = output_of(sibling, h).astype(BF)
        sum_near(0, o_s, o_r, h).start()
    for h in range(2):
        acc[pl.ds(h * half, half)] = output_of(t, h)
    for h in range(2):
        gather_x(gm, m_s, m_r, h).wait()
        gather_on(gm, m_s, m_r, h).start()
    for h in range(2):
        here = pl.ds(h * half, half)
        sum_near(0, o_s, o_r, h).wait()
        sum_x(0, o_s, o_r, h).wait()
        out = acc[here] + ccore[0, 1, h].astype(F32) + xin[0, h].astype(F32) + row(bo)
        attn[here] = out
        after = resid[here].astype(F32) + row(scale1) * out
        after_attn[here] = after
        center = jnp.mean(after, axis=1, keepdims=True)
        centered = after - center
        inverse = lax.rsqrt(jnp.mean(centered * centered, axis=1, keepdims=True) + eps_norm)
        scaled = centered * inverse
        xhat[here] = scaled
        inv2[here] = inverse
        gt[span(t, h)] = (scaled * row(gain2) + row(shift2)).astype(BF)
        gather_x(gt, t_s, t_r, h).start()
        gather_near(gt, t_s, t_r, h).start()

    esum[...] = jnp.zeros_like(esum)
    def feed(who, h):
        here = span(who, h)
        pre = jnp.dot(gt[here], we[...], preferred_element_type=F32) + row(be)
        grad = lax.dot_general(gm[here], wr[...], NT, preferred_element_type=F32)
        phi = 0.5 * (1.0 + lax.erf(pre * inv_sqrt_two))
        active = (pre * phi).astype(BF)
        act[here] = active
        grad = grad * (phi + pre * inv_sqrt_two_pi * jnp.exp(-0.5 * pre * pre))
        esum[...] += jnp.sum(grad, axis=0, keepdims=True)
        grad = grad.astype(BF)
        pgl[here] = grad
        part[here] = jnp.dot(active, wr[...], preferred_element_type=F32).astype(BF)
        return lax.dot_general(grad, we[...], NT, preferred_element_type=F32)
    def feed_own(h, c):
        acc[pl.ds(pl.multiple_of(h * half, 16), half)] = feed(t, h)
        return c
    lax.fori_loop(0, 2, feed_own, 0)
    for h in range(2):
        gather_near(gm, m_s, m_r, h).wait()
        gather_near(gt, t_s, t_r, h).wait()
    gather_x(gt, t_s, t_r, 0).wait()
    gather_on(gt, t_s, t_r, 0).start()
    def feed_near(h, c):
        cbuf[1, 1, h] = feed(sibling, h).astype(BF)
        return c
    lax.fori_loop(0, 2, feed_near, 0)
    for h in range(2):
        sum_near(1, n_s, n_r, h).start()
    gather_x(gt, t_s, t_r, 1).wait()
    gather_on(gt, t_s, t_r, 1).start()
    for h in range(2):
        gather_on(gm, m_s, m_r, h).wait()
        gather_on(gt, t_s, t_r, h).wait()
    def feed_far(h, c):
        cbuf[1, 0, h] = feed(diag, h).astype(BF)
        sum_far(1, n_s, n_r, h).start()
        total = feed(cross, h)
        sum_far(1, n_s, n_r, h).wait()
        xbuf[1, h] = (total + ccore[1, 0, h].astype(F32)).astype(BF)
        sum_x(1, n_s, n_r, h).start()
        return c
    lax.fori_loop(0, 2, feed_far, 0)

    tile = 128
    def reduce_grad(i, c):
        cols = pl.ds(pl.multiple_of(i * tile, tile), tile)
        x0[cols] = lax.dot_general(act[:, cols], gm[...], TN, preferred_element_type=F32).astype(BF)
        return c
    lax.fori_loop(0, act.shape[1] // tile, reduce_grad, 0)

    sums[...] = jnp.zeros_like(sums)
    for h in range(2):
        here = pl.ds(h * half, half)
        sum_near(1, n_s, n_r, h).wait()
        sum_x(1, n_s, n_r, h).wait()
        grad = acc[here] + ccore[1, 1, h].astype(F32) + xin[1, h].astype(F32)
        scaled = xhat[here]
        up = upstream[here]
        inner = grad * row(gain2)
        mean_inner = jnp.mean(inner, axis=1, keepdims=True)
        mean_mixed = jnp.mean(inner * scaled, axis=1, keepdims=True)
        after = up + inv2[here] * (inner - mean_inner - scaled * mean_mixed)
        after_grad[here] = after
        agrad = after * row(scale1)
        ga[span(t, h)] = agrad.astype(BF)
        gather_x(ga, a_s, a_r, h).start()
        gather_near(ga, a_s, a_r, h).start()
        sums[2:3, :] += jnp.sum(after * attn[here], axis=0, keepdims=True)
        sums[3:4, :] += jnp.sum(agrad, axis=0, keepdims=True)
        sums[4:5, :] += jnp.sum(grad * scaled, axis=0, keepdims=True)
        sums[5:6, :] += jnp.sum(grad, axis=0, keepdims=True)

    def expand_grad(i, c):
        cols = pl.ds(pl.multiple_of(i * tile, tile), tile)
        x1[cols] = lax.dot_general(gt[:, cols], pgl[...], TN, preferred_element_type=F32).astype(BF)
        return c
    def mixture_of(who):
        here = pl.ds(pl.multiple_of(who * rows, 16), rows)
        dmix[here] = lax.dot_general(ga[here], wo[...], NT, preferred_element_type=F32).astype(BF)
    count = gt.shape[1] // tile
    lax.fori_loop(0, count // 2, expand_grad, 0)
    gather_x(ga, a_s, a_r, 0).wait()
    gather_on(ga, a_s, a_r, 0).start()
    lax.fori_loop(count // 2, count, expand_grad, 0)
    mixture_of(t)
    for h in range(2):
        gather_near(ga, a_s, a_r, h).wait()
    mixture_of(sibling)
    gather_x(ga, a_s, a_r, 1).wait()
    gather_on(ga, a_s, a_r, 1).start()
    mixture_of(cross)
    for h in range(2):
        gather_on(ga, a_s, a_r, h).wait()
    mixture_of(diag)

def middle(scale, res, counts, g1, wq, bq, wk, wv, bv, bias, wo, bo, resid, scale1, gain2, shift2, we, be, wr, cot, scale2, cid):
    total, model = g1.shape
    rows = resid.shape[0]
    half = rows // 2
    width = wq.shape[0]
    hidden = we.shape[1]
    slots, heads = bias.shape[:2]
    vm = pl.BlockSpec(memory_space=pltpu.VMEM)
    sm = pl.BlockSpec(memory_space=pltpu.SMEM)
    dma = pltpu.SemaphoreType.DMA
    V = pltpu.VMEM
    S = jax.ShapeDtypeStruct
    operands = (g1, wq, bq, wk, wv, bv, bias, wo, bo, resid, scale1, gain2, shift2, we, be, wr, cot, scale2)
    shapes = (S((total, width), BF),) * 3 + (S((total, width), BF), S((slots, heads, SEQ, SEQ), BF), S((total, model), BF), S((total, model), BF),
        S((total, width), BF), S((hidden, model), BF), S((model, hidden), BF), S((rows, model), F32), S((rows, model), F32), S((8, model), F32), S((1, hidden), F32))
    return pl.pallas_call(functools.partial(middle_kernel, scale),
        out_shape=shapes, in_specs=[sm, sm] + [vm] * len(operands), out_specs=(vm,) * len(shapes),
        scratch_shapes=[V((rows, model), F32), V((total, model), BF), V((total, model), BF), V((total, hidden), BF), V((total, hidden), BF),
            V((rows, model), F32), V((rows, model), F32), V((rows, 1), F32), V((rows, model), F32),
            V((2, 2, 2, half, model), BF), V((2, 2, 2, half, model), BF), V((2, 2, half, model), BF), V((2, 2, half, model), BF)]
            + [dma((6,))] * 10,
        name="middle", cost_estimate=pl.CostEstimate(flops=60 * 10**9, bytes_accessed=60 * 10**6, transcendentals=0),
        compiler_params=pltpu.CompilerParams(collective_id=cid, has_side_effects=True, vmem_limit_bytes=60 << 20))(res, counts, *operands)

CHUNKS = 6

def tail_kernel(rows, scale, sums, res, counts, x0, x1, q_ref, k_ref, v_ref, p_ref, d_ref, g1, mix, ga, ilo, ihi, wq, wk, wv, resid, after_grad, gain,
                part, after_attn, cot, rbias, scale2, wide_in, expand_sum,
                o0, o1, o2, result, hidden_grad, wide, slim, tables,
                dq, dk, dv, glo, ghi, x2, ybuf, pbuf, zbuf, tbuf, abuf, acore, across, bcore, bcross,
                tlo, thi, wmine, wmid, smine, wten, wdp, sdp, tdp,
                y_s, y_r, z_s, z_r, g_s, g_r, e_s, e_r, r_s, r_r, w_s, w_r, v_s, v_r):
    d = lax.axis_index("dp")
    t = lax.axis_index("tensor")
    col = d // 2
    side = lax.rem(d, 2)
    sibling = t + 1 - 2 * lax.rem(t, 2)
    cross = lax.rem(t + 2, 4)
    diag = 3 - t
    neighbour = d + 1 - 2 * side
    heads = p_ref.shape[1]
    width = q_ref.shape[1]
    barrier = pltpu.get_barrier_semaphore()
    for k in range(1, 4):
        pl.semaphore_signal(barrier, inc=1, device_id=(d, lax.rem(t + k, 4)), device_id_type=MESH)
    if sums:
        for k in range(1, 8):
            pl.semaphore_signal(barrier, inc=1, device_id=(lax.rem(d + k, 8), t), device_id_type=MESH)
    pl.semaphore_wait(barrier, 10 if sums else 3)

    def remote(src, dst, send, recv, device):
        return pltpu.make_async_remote_copy(src_ref=src, dst_ref=dst, send_sem=send, recv_sem=recv, device_id=device, device_id_type=MESH)

    arrays = (x0, x1, x2)
    outs = (o0, o1, o2)
    size = 384
    half = size // 2
    block = half // 4
    def at(n, start, count):
        return pl.ds(pl.multiple_of((n % 2) * size + start, 16), count)
    def y_copy(n):
        return remote(arrays[n // 2].at[at(n, (1 - side) * half, half)], ybuf.at[n], y_s.at[n], y_r.at[n], (neighbour, t))
    def z_copy(n, k):
        to = lax.rem(col + k, 4)
        return remote(pbuf.at[n, pl.ds(pl.multiple_of(to * block, 16), block)], zbuf.at[n, k], z_s.at[n, k], z_r.at[n, k], (to * 2 + side, t))
    def g_copy(n, k):
        to = lax.rem(col + k, 4)
        return remote(tbuf.at[n], outs[n // 2].at[at(n, side * half + col * block, block)], g_s.at[n, k], g_r.at[n, k], (to * 2 + side, t))
    def e_copy(n):
        here = outs[n // 2].at[at(n, side * half, half)]
        return remote(here, here, e_s.at[n], e_r.at[n], (neighbour, t))
    def step_a(n):
        y_copy(n).wait()
        if n + 2 < CHUNKS:
            y_copy(n + 2).start()
        pbuf[n] = (arrays[n // 2][at(n, side * half, half)].astype(F32) + ybuf[n].astype(F32)).astype(BF)
        for k in range(1, 4):
            z_copy(n, k).start()
    def step_b(n):
        for k in range(1, 4):
            z_copy(n, k).wait()
        total = pbuf[n, pl.ds(pl.multiple_of(col * block, 16), block)].astype(F32)
        for k in range(1, 4):
            total = total + zbuf[n, k].astype(F32)
        total = total.astype(BF)
        tbuf[n] = total
        outs[n // 2][at(n, side * half + col * block, block)] = total
    def step_c(n):
        for k in range(1, 4):
            g_copy(n, k).start()
    def step_d(n):
        for k in range(1, 4):
            g_copy(n, k).wait()
        e_copy(n).start()

    if not sums:
        step_a = step_b = step_c = step_d = lambda n: None
    else:
        y_copy(0).start()
        y_copy(1).start()

    smine[...] = jnp.zeros_like(smine)
    smine[2:3, :] = expand_sum[...]
    def attention_back(slot):
        here = slice(slot * SEQ, (slot + 1) * SEQ)
        k = k_ref[here]
        v = v_ref[here]
        dd = d_ref[here]
        qt = q_ref[here].T
        dt = dd.T
        is_high = jnp.where(res[slot] == 1, 1.0, 0.0).astype(F32)
        out = jnp.zeros((SEQ, width), F32)
        dks = []
        dvs = []
        nh = ghi.shape[1]
        nl, ml = glo.shape[1:]
        for h in range(heads):
            mask = head_mask(h, width)
            p = p_ref[slot, h]
            dp = lax.dot_general(dd * mask, v, NT, preferred_element_type=F32)
            pf = p.astype(F32)
            m = pf * dp
            ds = m - pf * jnp.sum(m, axis=1, keepdims=True)
            if slot == 0:
                ghi[h] = ds[:nh] * is_high
                glo[h] = ds[:nl, :ml] * (1.0 - is_high)
            else:
                ghi[h] += ds[:nh] * is_high
                glo[h] += ds[:nl, :ml] * (1.0 - is_high)
            low = ds.astype(BF)
            out = out + jnp.dot(low, k * mask, preferred_element_type=F32)
            dks.append(jnp.dot(qt[h*HD:(h+1)*HD], low, preferred_element_type=F32))
            dvs.append(jnp.dot(dt[h*HD:(h+1)*HD], p, preferred_element_type=F32))
        out = out * scale
        smine[0:1, 0:width] += jnp.sum(out, axis=0, keepdims=True)
        dq[here] = out.astype(BF)
        dk[here] = jnp.concatenate(dks, axis=0).T.astype(BF)
        out = jnp.concatenate(dvs, axis=0).T
        smine[1:2, 0:width] += jnp.sum(out, axis=0, keepdims=True)
        dv[here] = out.astype(BF)
    attention_back(0)
    step_a(0)
    attention_back(1)
    step_a(1)

    def rows_of(ref, who):
        return ref[pl.ds(pl.multiple_of(who * rows, 16), rows)]
    def back(who):
        total = jnp.dot(rows_of(dq, who), wq[...], preferred_element_type=F32)
        total = total + jnp.dot(rows_of(dk, who), wk[...], preferred_element_type=F32)
        return total + jnp.dot(rows_of(dv, who), wv[...], preferred_element_type=F32)
    a_far = remote(abuf.at[0], acore.at[0], r_s.at[0], r_r.at[0], (d, sibling))
    a_near = remote(abuf.at[1], acore.at[1], r_s.at[1], r_r.at[1], (d, sibling))
    a_cross = remote(abuf.at[2], across, r_s.at[2], r_r.at[2], (d, cross))
    b_far = remote(part.at[pl.ds(pl.multiple_of(diag * rows, 16), rows)], bcore.at[0], r_s.at[3], r_r.at[3], (d, sibling))
    b_near = remote(part.at[pl.ds(pl.multiple_of(sibling * rows, 16), rows)], bcore.at[1], r_s.at[4], r_r.at[4], (d, sibling))
    b_cross = remote(abuf.at[3], bcross, r_s.at[5], r_r.at[5], (d, cross))
    abuf[0] = back(diag).astype(BF)
    a_far.start()
    b_far.start()
    total = back(cross)
    a_far.wait()
    abuf[2] = (total + acore[0].astype(F32)).astype(BF)
    a_cross.start()
    for j, (left, right) in enumerate(((dq, g1), (dk, g1), (dv, g1), (mix, ga))):
        x2[j * width:(j + 1) * width, :] = lax.dot_general(left[...], right[...], TN, preferred_element_type=F32).astype(BF)
    step_a(2)
    step_b(0)
    abuf[1] = back(sibling).astype(BF)
    a_near.start()
    b_near.start()
    total = back(t)
    a_near.wait()
    hidden_grad[...] = total + acore[1].astype(F32)
    b_far.wait()
    abuf[3] = (rows_of(part, cross).astype(F32) + bcore[0].astype(F32)).astype(BF)
    segments = 7
    n_hi = 592 // UN
    def scatter_part(s):
        lo, hi = n_hi * s // segments, n_hi * (s + 1) // segments
        scatter_run(ihi, ghi, thi, lo, hi, s == 0)
    scatter_part(0)
    step_a(3)
    step_b(1)
    a_cross.wait()
    b_cross.start()
    grad = hidden_grad[...] + across[...].astype(F32)
    xhat, inverse = moments(resid[...].astype(F32))
    wmine[...] = wide_in[...]
    wmine[0:1, :] = jnp.sum(grad * xhat, axis=0, keepdims=True)
    wmine[1:2, :] = jnp.sum(grad, axis=0, keepdims=True)
    inner = grad * row(gain)
    mean_inner = jnp.mean(inner, axis=1, keepdims=True)
    mean_mixed = jnp.mean(inner * xhat, axis=1, keepdims=True)
    hidden_grad[...] = after_grad[...] + inverse * (inner - mean_inner - xhat * mean_mixed)
    scatter_part(1)
    step_a(4)
    step_b(2)
    scatter_part(2)
    step_a(5)
    step_b(3)
    scatter_part(3)
    b_near.wait()
    b_cross.wait()
    out = rows_of(part, t).astype(F32) + bcore[1].astype(F32) + bcross[...].astype(F32) + row(rbias)
    alive = live_of(t, rows, res, counts)
    result[...] = ((after_attn[...] + row(scale2) * out) * alive).astype(BF)
    up = cot[...].astype(F32) * alive
    wmine[6:7, :] = jnp.sum(up * out, axis=0, keepdims=True)
    wmine[7:8, :] = jnp.sum(up * row(scale2), axis=0, keepdims=True)
    step_b(4)
    step_c(0)
    step_c(1)
    def w_copy(k):
        return remote(wmine, wten.at[k], w_s.at[k], w_r.at[k], (d, lax.rem(t + k, 4)))
    if sums:
        for k in range(1, 4):
            w_copy(k).start()
    scatter_part(4)
    step_b(5)
    scatter_part(5)
    step_d(0)
    step_c(2)
    scatter_part(6)
    step_d(1)
    step_c(3)
    scatter_run(ilo, glo, tlo, 0, 208 // UN, True)
    tables[...] = jnp.zeros_like(tables)
    n = tlo.shape[1]
    tables[:, 0:n] = tlo[...]
    tables[:, n:n + thi.shape[1]] = thi[...]
    tbl = tdp.at[0]
    tbl[...] = tables[...]
    total = wmine[...]
    if sums:
        for k in range(1, 4):
            w_copy(k).wait()
            total = total + wten[k]
    wmid[...] = total
    def v_copy(j, k):
        src, dst = ((wmid, wdp), (smine, sdp), (tbl, tdp))[j]
        return remote(src, dst.at[k], v_s.at[j, k], v_r.at[j, k], (lax.rem(d + k, 8), t))
    if sums:
        for k in range(1, 8):
            for j in range(3):
                v_copy(j, k).start()
    step_d(2)
    step_c(4)
    wide[...] = wmid[...]
    slim[...] = smine[...]
    step_d(3)
    step_c(5)
    if not sums:
        o0[...] = x0[...]
        o1[...] = x1[...]
        o2[...] = x2[...]
        return
    for k in range(1, 8):
        for j in range(3):
            v_copy(j, k).wait()
        wide[...] += wdp[k]
        slim[...] += sdp[k]
        tables[...] += tdp[k]
    step_d(4)
    step_d(5)
    for n in range(CHUNKS):
        e_copy(n).wait()

def tail(scale, sums, res, counts, x0, x1, q, k, v, p, dmix, g1, mix, ga, ilo, ihi, wq, wk, wv, resid, after_grad, gain, part, after_attn, cot, rbias, scale2, wide_in, expand_sum, n_lo, n_hi, cid):
    rows, model = after_grad.shape
    total, width = q.shape
    heads = p.shape[1]
    vm = pl.BlockSpec(memory_space=pltpu.VMEM)
    sm = pl.BlockSpec(memory_space=pltpu.SMEM)
    dma = pltpu.SemaphoreType.DMA
    operands = (x0, x1, q, k, v, p, dmix, g1, mix, ga, ilo, ihi, wq, wk, wv, resid, after_grad, gain, part, after_attn, cot, rbias, scale2, wide_in, expand_sum)
    tshape = (heads * BB, 128)
    V = pltpu.VMEM
    S = jax.ShapeDtypeStruct
    return pl.pallas_call(functools.partial(tail_kernel, rows, scale, sums),
        out_shape=(S((768, model), BF),) * 3 + (S((rows, model), BF), S((rows, model), F32), S((8, model), F32), S((8, model), F32), S(tshape, F32)),
        in_specs=[sm, sm] + [vm] * len(operands), out_specs=(vm,) * 8,
        scratch_shapes=[
            V((total, width), BF), V((total, width), BF), V((total, width), BF), V((heads,) + ilo.shape, F32), V((heads,) + ihi.shape, F32), V((4 * width, model), BF),
            V((CHUNKS, 192, model), BF), V((CHUNKS, 192, model), BF), V((CHUNKS, 4, 48, model), BF), V((CHUNKS, 48, model), BF),
            V((4, rows, model), BF), V((2, rows, model), BF), V((rows, model), BF), V((2, rows, model), BF), V((rows, model), BF),
            V((heads * BB, n_lo), F32), V((heads * BB, n_hi), F32),
            V((8, model), F32), V((8, model), F32), V((8, model), F32), V((4, 8, model), F32), V((8, 8, model), F32), V((8, 8, model), F32), V((8,) + tshape, F32),
            dma((CHUNKS,)), dma((CHUNKS,)), dma((CHUNKS, 4)), dma((CHUNKS, 4)), dma((CHUNKS, 4)), dma((CHUNKS, 4)), dma((CHUNKS,)), dma((CHUNKS,)),
            dma((6,)), dma((6,)), dma((4,)), dma((4,)), dma((3, 8)), dma((3, 8))],
        name="tail", cost_estimate=pl.CostEstimate(flops=50 * 10**9, bytes_accessed=60 * 10**6, transcendentals=0),
        compiler_params=pltpu.CompilerParams(collective_id=cid, has_side_effects=True, vmem_limit_bytes=60 << 20))(res, counts, *operands)


def local(
    hidden,
    first_gain,
    first_shift,
    query_weight,
    query_bias,
    key_weight,
    value_weight,
    value_bias,
    output_weight,
    output_bias,
    first_scale,
    second_gain,
    second_shift,
    expand_weight,
    expand_bias,
    reduce_weight,
    reduce_bias,
    second_scale,
    table_low,
    table_high,
    resolution,
    counts,
    index_low,
    index_high,
    cotangent,
):
    floating = jnp.float32
    heads_dev = table_low.shape[1]
    head_scale = HD ** (-0.5)
    normed_one = normalize(hidden.astype(floating), first_gain, first_shift)
    gathered_one = lax.all_gather(normed_one.astype(BF), "tensor", axis=0, tiled=True)
    index_low_pad = jnp.pad(index_low, ((0, 256 - P_LO), (0, 256 - P_LO)))
    index_high_pad = jnp.pad(index_high, ((0, 592 - P_HI), (0, SEQ - P_HI)))
    bias_map = gather_maps(resolution, table_low, table_high, index_low_pad, index_high_pad)
    (
        queries,
        keys,
        values,
        mixture,
        attention,
        mlp_part,
        gathered_grad,
        mixture_grad,
        reduce_part,
        expand_part,
        after_attn,
        after_grad,
        wide,
        expand_sum,
    ) = middle(
        head_scale,
        resolution,
        counts,
        gathered_one,
        query_weight.T,
        query_bias,
        key_weight.T,
        value_weight.T,
        value_bias,
        bias_map,
        output_weight,
        output_bias,
        hidden,
        first_scale,
        second_gain,
        second_shift,
        expand_weight,
        expand_bias,
        reduce_weight,
        cotangent,
        second_scale,
        0,
    )
    n_low = -(-table_low.shape[0] // (BB * 16)) * 16
    n_high = -(-table_high.shape[0] // (BB * 16)) * 16
    known = lax.axis_size("dp") == 8
    reduce_grad, expand_grad, attn_grads, result, hidden_grad, wide, slim, tables = tail(
        head_scale,
        known,
        resolution,
        counts,
        reduce_part,
        expand_part,
        queries,
        keys,
        values,
        attention,
        mixture_grad,
        gathered_one,
        mixture,
        gathered_grad,
        index_low_pad,
        index_high_pad,
        query_weight.T,
        key_weight.T,
        value_weight.T,
        hidden,
        after_grad,
        first_gain,
        mlp_part,
        after_attn,
        cotangent,
        reduce_bias,
        second_scale,
        wide,
        expand_sum,
        n_low,
        n_high,
        1,
    )
    reduce_grad = reduce_grad.astype(floating)
    expand_grad = expand_grad.astype(floating)
    attn_grads = attn_grads.astype(floating)
    if not known:
        reduce_grad, expand_grad, attn_grads, slim, tables = lax.psum(
            (reduce_grad, expand_grad, attn_grads, slim, tables), "dp"
        )
        wide = lax.psum(wide, ("dp", "tensor"))
    width = queries.shape[1]

    def unpack(block, count):
        block = block.reshape(heads_dev, BB, -1).transpose(2, 1, 0)
        return block.reshape(-1, heads_dev)[:count]

    return (
        result,
        hidden_grad,
        wide[0],
        wide[1],
        attn_grads[:width].T,
        slim[0, :width],
        attn_grads[width : 2 * width].T,
        attn_grads[2 * width : 3 * width].T,
        slim[1, :width],
        attn_grads[3 * width :],
        wide[3],
        wide[2],
        wide[4],
        wide[5],
        expand_grad,
        slim[2],
        reduce_grad,
        wide[7],
        wide[6],
        unpack(tables[:, :n_low], table_low.shape[0]),
        unpack(tables[:, n_low : n_low + n_high], table_high.shape[0]),
    )


def solution(mesh):
    in_specs = (
        P(("dp", "tensor"), None),
        P(),
        P(),
        P(None, "tensor"),
        P("tensor"),
        P(None, "tensor"),
        P(None, "tensor"),
        P("tensor"),
        P("tensor", None),
        P(),
        P(),
        P(),
        P(),
        P(None, "tensor"),
        P("tensor"),
        P("tensor", None),
        P(),
        P(),
        P(None, "tensor"),
        P(None, "tensor"),
        P("dp"),
        P("dp"),
        P(),
        P(),
        P(("dp", "tensor"), None),
    )
    out_specs = (
        P(("dp", "tensor"), None),
        P(("dp", "tensor"), None),
        P(),
        P(),
        P(None, "tensor"),
        P("tensor"),
        P(None, "tensor"),
        P(None, "tensor"),
        P("tensor"),
        P("tensor", None),
        P(),
        P(),
        P(),
        P(),
        P(None, "tensor"),
        P("tensor"),
        P("tensor", None),
        P(),
        P(),
        P(None, "tensor"),
        P(None, "tensor"),
    )
    return jax.shard_map(local, mesh=mesh, in_specs=in_specs, out_specs=out_specs, check_vma=False)
```

time: 581 us -> 269 us (0.46)
  waiting for transfers between devices: 331 us -> 0.02 us
  Pallas kernels: 56.8 us -> 228 us
  blocking collectives: 81.1 us -> 0 us
  matrix products: 46.7 us -> 0 us
  other arithmetic: 21.4 us -> 8.07 us
  local copies, waits for them, and re-layouts: 26.5 us -> 18.2 us
    psum x1 -> x0, waiting for transfers between devices: 179 us -> none  [local(): lax.psum((query_weight_grad, query_bias_grad, key_weight_grad, value_weig...]
    pallas_call x3, Pallas kernels: 56.8 us -> 228 us  [the longest x1 129 us: tail(): pl.pallas_call(functools.partial(tail_kernel, rows, scale, sums), out_sha...]
    reduce_scatter x4 -> x0, waiting for transfers between devices: 92.6 us -> none  [the longest x1 36.9 us: local(): lax.psum_scatter(jnp.dot(mixture_rows, output_weight, preferred_element_t...]
    psum x2 -> x0, blocking collectives: 81.1 us -> none  [the longest x1 41.6 us: local(): lax.psum((first_gain_grad, first_shift_grad, first_scale_grad, output_bia...]
    all_gather x4 -> x1, waiting for transfers between devices: 59 us -> 0.01 us  [local(): lax.all_gather(normed_one.astype(BF), 'tensor', axis=0, tiled=True)]
    dot_general x18 -> x0, matrix products: 46.7 us -> none  [the longest x1 5.82 us: local(): jnp.dot(gathered_two, expand_weight, preferred_element_type=floating)]
    unnamed x134 -> x32, local copies, waits for them, and re-layouts: 24.3 us -> 5.98 us
    reduce_sum x4 -> x0, other arithmetic: 7.53 us -> none  [the longest x1 3.58 us: local(): first_scale_grad = jnp.sum(after_grad * attn_out, axis=0)]
  transfers between devices with their start and end apart: 9 -> 1, of which waited for: 8 -> 0; matrix products, arithmetic and copies ran while one was open for 6% -> 0% of each run, Pallas kernels for 3% -> 8%
where the time goes in v2:
time: 269 us
  Pallas kernels  228 us (85%)
  local copies, waits for them, and re-layouts  18.2 us (7%)
  between operations  14.9 us (6%)
  other arithmetic  8.07 us (3%)
    pallas_call x1, Pallas kernels, tail(): pl.pallas_call(functools.partial(tail_kernel, rows, scale, sums), out_sha...  129 us
    pallas_call x1, Pallas kernels, middle(): pl.pallas_call(functools.partial(middle_kernel, scale), out_shape=shapes,...  77.5 us
    pallas_call x1, Pallas kernels, gather_maps(): pl.pallas_call(gather_kernel, out_shape=jax.ShapeDtypeStruct((SLOTS, head...  21.2 us
    unnamed x32, local copies, waits for them, and re-layouts  5.98 us
  transfers between devices with their start and end apart: 1, of which 0 were waited for; matrix products, arithmetic and copies ran while one was open for 0% of the time, Pallas kernels for 8%

profile of v2, /device:TPU:0, one launch (start us, length us, event | category | flops | bytes accessed | tf_op | source)
XLA Modules:
  0.0 268.8 jit_solution(16173639343936721089)
XLA Ops:
  7.2 0.0 copy-start.14
  7.2 0.0 all-gather.2.cloned.1.call-start
  7.3 1.3 convert_reduce_fusion
  8.6 1.3 fusion.2
  9.9 2.1 fusion.5
  12.0 0.0 all-gather.2.cloned.1.call-update
  12.7 0.0 copy-start.2
  12.8 0.0 copy-start.1
  12.9 0.1 pad.19.idx_hi.ihi
  13.0 0.0 copy-start
  13.0 0.3 copy-done.2
  13.4 21.2 %bias_gather.1.bias = f32[2,3,640,640]{3,2,1,0:T(8,128)S(1)} custom-call(s32[2]{0:T(128)S(1)} %copy-done.2, s32[3,3,8,128]{3,2,1,0:T(8,128)S(1)} %broadcast_in_dim.4.tab_lo, s32[3,9,8,128]{3,2,1,0:T(8,128)S(1)} %broadcast_in_dim.5.tab_hi, s32[256,256]{1,0:T(8,128)S(1)} %pad.18.idx_lo.ilo, s32[592,640]{1,0:T(8,128)S(1)} %pad.19.idx_hi.ihi), custom_call_target="tpu_custom_call" | custom-call | flops 20000000000 | bytes 8000000 | tf_op jit(solution)/shard_map/bias_gather/pallas_call | solution.py:136
  34.6 3.8 %copy-done.3 = f32[2,3,640,640]{3,2,1,0:T(8,128)} copy-done((f32[2,3,640,640]{3,2,1,0:T(8,128)}, f32[2,3,640,640]{3,2,1,0:T(8,128)S(1)}, u32[]{:S(2)}) %copy-start.3) | copy-done | bytes 9830424
  38.4 77.5 %middle.1 = (bf16[1280,192]{1,0:T(8,128)(2,1)}, bf16[1280,192]{1,0:T(8,128)(2,1)}, bf16[1280,192]{1,0:T(8,128)(2,1)}, bf16[1280,192]{1,0:T(8,128)(2,1)}, bf16[2,...) custom-call(s32[2]{0:T(128)} %res.5, ...), custom_call_target="tpu_custom_call" | custom-call | flops 60000002048 | bytes 60000000 | tf_op jit(solution)/shard_map/middle/pallas_call | solution.py:368
  115.9 128.8 %tail.1 = (bf16[768,768]{1,0:T(8,128)(2,1)}, bf16[768,768]{1,0:T(8,128)(2,1)}, bf16[768,768]{1,0:T(8,128)(2,1)}, bf16[320,768]{1,0:T(8,128)(2,1)}, f32[320,768]{...) custom-call(s32[2]{0:T(128)} %res.5, s32[1]{0:T(128)S(6)} %copy.56.counts, ...), custom_call_target="tpu_custom_call" | custom-call | flops 49999998976 | bytes 60000000 | tf_op jit(solution)/shard_map/tail/pallas_call | solution.py:632
  244.7 1.9 slice.99
  246.7 0.2 convert_element_type.29
  246.8 1.3 fusion.10
  248.2 1.4 slice_reduce_fusion
  249.6 0.7 slice.90
  250.3 0.1 copy.52
  250.4 0.1 reshape.119
  250.5 0.6 slice.100
  251.1 1.6 copy.53
  252.8 1.6 reshape.121
  254.4 1.4 slice.101
  255.8 1.2 slice_bitcast_fusion
  257.0 1.6 convert_element_type.30
  258.6 0.1 copy-done.6
  258.7 1.6 convert_element_type.31
  260.3 0.8 copy.57
  261.1 0.9 copy.58
  (35 shorter events, 0.2 us)
Async XLA Ops:
  7.2 5.5 %copy-start.14 = (f32[732,3]{0,1:T(4,128)S(1)}, f32[732,3]{0,1:T(4,128)}, u32[]{:S(2)}) copy-start(f32[732,3]{0,1:T(4,128)} %param.43) | copy-start | bytes 26356
  7.2 5.5 %copy-start.12 = (f32[2212,3]{0,1:T(4,128)S(1)}, f32[2212,3]{0,1:T(4,128)}, u32[]{:S(2)}) copy-start(f32[2212,3]{0,1:T(4,128)} %param.44) | copy-start | bytes 79636
  7.2 5.6 %copy-start.10 = (s32[197,197]{1,0:T(8,128)S(1)}, s32[197,197]{1,0:T(8,128)}, u32[]{:S(2)}) copy-start(s32[197,197]{1,0:T(8,128)} %param.47) | copy-start | bytes 465712
  7.2 5.6 %copy-start.5 = (s32[577,577]{1,0:T(8,128)S(1)}, s32[577,577]{1,0:T(8,128)}, u32[]{:S(2)}) copy-start(s32[577,577]{1,0:T(8,128)} %param.48) | copy-start | bytes 3995152
  7.2 31.2 %all-gather.2.cloned.1.call-start = ((), (), s32[]{:S(2)}) async-start(), calls=%async_computation | async-start | bytes 2457600 | tf_op jit(solution)/shard_map/all_gather | solution.py:678
  12.7 0.7 copy-start.2
  12.8 21.7 %copy-start.1 = (s32[256,256]{1,0:T(8,128)}, s32[256,256]{1,0:T(8,128)S(1)}, u32[]{:S(2)}) copy-start(s32[256,256]{1,0:T(8,128)S(1)} %pad.18.idx_lo.ilo) | copy-start | bytes 786436
  13.0 21.6 %copy-start = (s32[592,640]{1,0:T(8,128)}, s32[592,640]{1,0:T(8,128)S(1)}, u32[]{:S(2)}) copy-start(s32[592,640]{1,0:T(8,128)S(1)} %pad.19.idx_hi.ihi) | copy-start | bytes 4546564
  34.6 3.8 %copy-start.3 = (f32[2,3,640,640]{3,2,1,0:T(8,128)}, f32[2,3,640,640]{3,2,1,0:T(8,128)S(1)}, u32[]{:S(2)}) copy-start(f32[2,3,640,640]{3,2,1,0:T(8,128)S(1)} %bias_gather.1.bias) | copy-start | bytes 29491204
  244.7 1.9 copy-start.4
  246.7 1.5 copy-start.13
  246.7 3.0 %copy-start.11 = (f32[96,128]{1,0:T(8,128)S(1)}, f32[96,128]{1,0:T(8,128)}, u32[]{:S(2)}) copy-start(f32[96,128]{1,0:T(8,128)} %get-tuple-element.64) | copy-start | bytes 147460
  251.1 5.9 %copy-start.7 = (bf16[768,768]{1,0:T(8,128)(2,1)S(1)}, bf16[768,768]{1,0:T(8,128)(2,1)}, u32[]{:S(2)}) copy-start(bf16[768,768]{1,0:T(8,128)(2,1)} %get-tuple-element.62) | copy-start | bytes 3538948
  257.0 1.7 copy-start.6
  258.6 1.7 copy-start.9
  258.7 2.4 copy-start.8
Sparse Core Ops, SparseCore 0:
  12.1 24.5 all-gather.1

commit v3 on v2

v3 whole, which is shorter than its diff:
```python
import functools

import jax
import jax.numpy as jnp
from jax import lax
from jax.experimental import pallas as pl
from jax.experimental.pallas import tpu as pltpu
from jax.sharding import PartitionSpec as P

HD = 64
P_LO = 197
P_HI = 577
SEQ = 640
SLOTS = 2


eps_norm = 1e-06
masked_score = -1e30
inv_sqrt_two = 0.7071067811865476
inv_sqrt_two_pi = 0.3989422804014327


F32=jnp.float32; BF=jnp.bfloat16
NT=(((1,),(1,)),((),()))
def head_mask(h, width):
    lane = lax.broadcasted_iota(jnp.int32, (1, width), 1)
    return ((lane >= h*HD) & (lane < (h+1)*HD)).astype(F32).astype(BF)


BB=32; UN=16
def scatter_run(idx_ref, g_ref, out, first, last, fresh):
    heads = g_ref.shape[0]; na = out.shape[1]; m = idx_ref.shape[1]
    if fresh:
        out[...] = jnp.zeros_like(out)
    ib = lax.broadcasted_iota(jnp.int32, (16, m), 0).astype(F32)
    def body(r, c):
        ms = []; os = []
        for u in range(UN):
            row = r*UN+u
            idx = jnp.broadcast_to(idx_ref[pl.ds(row,1), :], (16, m))
            ia = (idx >> 5).astype(F32).astype(BF); il = (idx & 31).astype(F32).astype(BF)
            g = [jnp.broadcast_to(g_ref[h, pl.ds(row,1), :], (16, m)).astype(BF) for h in range(heads)]
            hits = [il == (ib + 16.0*k).astype(BF) for k in range(BB//16)]
            ms.append(jnp.concatenate([jnp.where(hits[k], g[h], jnp.zeros_like(g[h])) for h in range(heads) for k in range(BB//16)], axis=0))
            os.append(jnp.concatenate([jnp.where(ia == (ib + 16.0*k).astype(BF), jnp.ones_like(ia), jnp.zeros_like(ia)) for k in range(na//16)], axis=0))
        out[...] += lax.dot_general(jnp.concatenate(ms, axis=1), jnp.concatenate(os, axis=1), NT, preferred_element_type=F32)
        return c
    lax.fori_loop(first, last, body, 0)

PACK=8191.0
MESH = pl.DeviceIdType.MESH

CHUNKS = 6
TN = (((0,), (0,)), ((), ()))

def row(ref):
    return ref[...].reshape(1, ref.shape[0])

def live_of(t, rows, res, counts):
    slot = t * rows // SEQ
    first = t * rows - slot * SEQ
    limit = jnp.where(res[slot] == 1, P_HI, P_LO)
    limit = jnp.where(slot < counts[0], limit, 0)
    place = lax.broadcasted_iota(jnp.int32, (rows, 1), 0) + first
    return jnp.where(place < limit, 1.0, 0.0).astype(F32)

def moments(values):
    center = jnp.mean(values, axis=1, keepdims=True)
    centered = values - center
    inverse = lax.rsqrt(jnp.mean(centered * centered, axis=1, keepdims=True) + eps_norm)
    return centered * inverse, inverse

def norm_back(grad, scaled, inverse, gain):
    inner = grad * gain
    mean_inner = jnp.mean(inner, axis=1, keepdims=True)
    mean_mixed = jnp.mean(inner * scaled, axis=1, keepdims=True)
    return inverse * (inner - mean_inner - scaled * mean_mixed)

def look_up(tab, idx, heads):
    nch = tab.shape[1]
    lane = idx & 127
    ch = idx >> 7
    shift = jnp.where(ch >= nch, 0, 16)
    ch = jnp.where(ch >= nch, ch - nch, ch)
    acc = [None] * heads
    for k in range(nch):
        hit = ch == k
        for h in range(heads):
            v = jnp.take_along_axis(tab[h, k], lane, axis=1)
            acc[h] = v if k == 0 else jnp.where(hit, v, acc[h])
    return [((acc[h] << shift) >> 16).astype(F32) * (1.0 / PACK) for h in range(heads)]

def bias_rows(res, tab_lo, tab_hi, idx_lo, idx_hi, out, first, last, both):
    slots, heads = out.shape[:2]
    def masked(vals, j, limit):
        if (j + 1) * 128 <= limit:
            return vals
        place = lax.broadcasted_iota(jnp.int32, (8, 128), 1) + j * 128
        return [jnp.where(place < limit, v, masked_score) for v in vals]
    def body(r, c):
        for j in range(idx_hi.shape[1] // 128):
            cols = pl.ds(j * 128, 128)
            high = []
            low = []
            for part in range(2):
                rows = pl.ds(pl.multiple_of(r * 16 + part * 8, 8), 8)
                high.append(masked(look_up(tab_hi, idx_hi[rows, cols], heads), j, P_HI))
                if both and j < idx_lo.shape[1] // 128:
                    low.append(masked(look_up(tab_lo, idx_lo[rows, cols], heads), j, P_LO))
                else:
                    low.append([jnp.full((8, 128), masked_score, F32)] * heads)
            for h in range(heads):
                hi = jnp.concatenate([high[0][h], high[1][h]], axis=0).astype(BF)
                lo = jnp.concatenate([low[0][h], low[1][h]], axis=0).astype(BF)
                for s in range(slots):
                    out[s, h, pl.ds(pl.multiple_of(r * 16, 16), 16), cols] = jnp.where(res[s] == 1, hi, lo)
        return c
    lax.fori_loop(first, last, body, 0)

def layer_kernel(scale, sums, res, counts, hidden, gain1, shift1, wq, bq, wk, wv, bv, wo, bo, scale1, gain2, shift2, we, be, wr, rbias, scale2, cot,
                 tab_lo, tab_hi, ilo, ihi,
                 o0, o1, o2, result, hidden_grad, wide, slim, tables,
                 g1, gm, gt, ga, q_buf, k_buf, v_buf, mix, dmix, pb, act, pgl, part, acc, attn, x0, x1, x2, ghi, glo, esum,
                 cbuf, ccore, xbuf, xin, acore, across, bcore, bcross, ybuf, zbuf,
                 tlo, thi, wmine, wmid, smine, tmine, wten, wdp, sdp, tdp,
                 h_s, h_r, m_s, m_r, t_s, t_r, a_s, a_r, o_s, o_r, n_s, n_r,
                 y_s, y_r, z_s, z_r, g_s, g_r, e_s, e_r, r_s, r_r, w_s, w_r, v_s, v_r):
    d = lax.axis_index("dp")
    t = lax.axis_index("tensor")
    col = d // 2
    side = lax.rem(d, 2)
    neighbour = d + 1 - 2 * side
    sibling = t + 1 - 2 * lax.rem(t, 2)
    cross = lax.rem(t + 2, 4)
    diag = 3 - t
    rows = hidden.shape[0]
    half = rows // 2
    slots, heads = pb.shape[:2]
    width = q_buf.shape[1]
    barrier = pltpu.get_barrier_semaphore()
    for k in range(1, 4):
        pl.semaphore_signal(barrier, inc=1, device_id=(d, lax.rem(t + k, 4)), device_id_type=MESH)
    if sums:
        for k in range(1, 8):
            pl.semaphore_signal(barrier, inc=1, device_id=(lax.rem(d + k, 8), t), device_id_type=MESH)

    def remote(src, dst, send, recv, device):
        return pltpu.make_async_remote_copy(src_ref=src, dst_ref=dst, send_sem=send, recv_sem=recv, device_id=device, device_id_type=MESH)
    def rows_at(who):
        return pl.ds(pl.multiple_of(who * rows, 16), rows)
    def span(who, h):
        return pl.ds(pl.multiple_of(who * rows + h * half, 16), half)
    def gather_x(buf, send, recv, h):
        here = buf.at[span(t, h)]
        return remote(here, here, send.at[h], recv.at[h], (d, cross))
    def gather_near(buf, send, recv, h):
        here = buf.at[span(t, h)]
        return remote(here, here, send.at[2 + h], recv.at[2 + h], (d, sibling))
    def gather_on(buf, send, recv, h):
        here = buf.at[span(cross, h)]
        return remote(here, here, send.at[4 + h], recv.at[4 + h], (d, sibling))
    def sum_far(j, send, recv, h):
        return remote(cbuf.at[j, 0, h], ccore.at[j, 0, h], send.at[h], recv.at[h], (d, sibling))
    def sum_near(j, send, recv, h):
        return remote(cbuf.at[j, 1, h], ccore.at[j, 1, h], send.at[2 + h], recv.at[2 + h], (d, sibling))
    def sum_x(j, send, recv, h):
        return remote(xbuf.at[j, h], xin.at[j, h], send.at[4 + h], recv.at[4 + h], (d, cross))
    arrays = (x0, x1, x2)
    outs = (o0, o1, o2)
    size = x0.shape[0] // 2
    part_y = size // 2
    part_z = part_y // 4
    def at(n, start, count):
        return pl.ds(pl.multiple_of((n % 2) * size + start, 16), count)
    def y_copy(n):
        return remote(arrays[n // 2].at[at(n, (1 - side) * part_y, part_y)], ybuf.at[n], y_s.at[n], y_r.at[n], (neighbour, t))
    def z_copy(n, k):
        to = lax.rem(col + k, 4)
        return remote(arrays[n // 2].at[at(n, side * part_y + to * part_z, part_z)], zbuf.at[n, k - 1], z_s.at[n, k], z_r.at[n, k], (to * 2 + side, t))
    def g_copy(n, k):
        to = lax.rem(col + k, 4)
        here = outs[n // 2].at[at(n, side * part_y + col * part_z, part_z)]
        return remote(here, here, g_s.at[n, k], g_r.at[n, k], (to * 2 + side, t))
    def e_copy(n):
        here = outs[n // 2].at[at(n, side * part_y, part_y)]
        return remote(here, here, e_s.at[n], e_r.at[n], (neighbour, t))
    def start_y(n):
        y_copy(n).start()
    def step_a(n):
        y_copy(n).wait()
        if n < 2:
            y_copy(n + 2).start()
        here = at(n, side * part_y, part_y)
        arrays[n // 2][here] = (arrays[n // 2][here].astype(F32) + ybuf[n].astype(F32)).astype(BF)
        for k in range(1, 4):
            z_copy(n, k).start()
    def step_b(n):
        for k in range(1, 4):
            z_copy(n, k).wait()
        here = at(n, side * part_y + col * part_z, part_z)
        total = arrays[n // 2][here].astype(F32)
        for k in range(3):
            total = total + zbuf[n, k].astype(F32)
        outs[n // 2][here] = total.astype(BF)
        for k in range(1, 4):
            g_copy(n, k).start()
    def step_d(n):
        for k in range(1, 4):
            g_copy(n, k).wait()
        e_copy(n).start()
    if not sums:
        start_y = step_a = step_b = step_d = lambda n: None

    scaled, inverse = moments(hidden[...].astype(F32))
    g1[rows_at(t)] = (scaled * row(gain1) + row(shift1)).astype(BF)
    pl.semaphore_wait(barrier, 10 if sums else 3)
    for h in range(2):
        gather_x(g1, h_s, h_r, h).start()
        gather_near(g1, h_s, h_r, h).start()
    alive = live_of(t, rows, res, counts)
    gm[rows_at(t)] = (cot[...].astype(F32) * alive * row(scale2)).astype(BF)
    look = functools.partial(bias_rows, res, tab_lo, tab_hi, ilo, ihi, pb)
    n_low = -(-P_LO // 16)
    n_high = -(-P_HI // 16)
    middle = (n_low + n_high) // 2
    look(0, n_low, True)
    look(n_low, middle, False)
    for h in range(2):
        gather_x(g1, h_s, h_r, h).wait()
        gather_on(g1, h_s, h_r, h).start()
        gather_x(gm, m_s, m_r, h).start()
        gather_near(gm, m_s, m_r, h).start()
    look(middle, n_high, False)
    pb[:, :, n_high * 16:, :] = jnp.zeros((slots, heads, SEQ - n_high * 16, SEQ), BF)
    for h in range(2):
        gather_near(g1, h_s, h_r, h).wait()
        gather_on(g1, h_s, h_r, h).wait()

    def project(i, c):
        here = rows_at(i)
        g = g1[here]
        q_buf[here] = ((lax.dot_general(g, wq[...], NT, preferred_element_type=F32) + row(bq)) * scale).astype(BF)
        k_buf[here] = lax.dot_general(g, wk[...], NT, preferred_element_type=F32).astype(BF)
        v_buf[here] = (lax.dot_general(g, wv[...], NT, preferred_element_type=F32) + row(bv)).astype(BF)
        return c
    lax.fori_loop(0, 4, project, 0)

    def attend_image(slot):
        here = pl.ds(pl.multiple_of(slot * SEQ, 16), SEQ)
        k = k_buf[here]
        v = v_buf[here]
        vm = [v * head_mask(h, width) for h in range(heads)]
        def piece(i, c):
            first = pl.multiple_of(i * rows, 16)
            there = pl.ds(pl.multiple_of(slot * SEQ + first, 16), rows)
            q = q_buf[there]
            out = jnp.zeros((rows, width), F32)
            for h in range(heads):
                s = lax.dot_general(q * head_mask(h, width), k, NT, preferred_element_type=F32)
                s = s + pb[slot, h, pl.ds(first, rows)].astype(F32)
                peak = jnp.max(s, axis=1, keepdims=True)
                e = jnp.exp(s - peak)
                total = jnp.sum(e, axis=1, keepdims=True)
                p = (e * (1.0 / total)).astype(BF)
                pb[slot, h, pl.ds(first, rows)] = p
                out = out + jnp.dot(p, vm[h], preferred_element_type=F32)
            mix[there] = out.astype(BF)
            return c
        lax.fori_loop(0, SEQ // rows, piece, 0)
    def output_of(who, h):
        return jnp.dot(mix[span(who, h)], wo[...], preferred_element_type=F32)

    mine = t * rows // SEQ
    attend_image(1 - mine)
    for h in range(2):
        cbuf[0, 0, h] = output_of(diag, h).astype(BF)
        sum_far(0, o_s, o_r, h).start()
    for h in range(2):
        total = output_of(cross, h)
        sum_far(0, o_s, o_r, h).wait()
        xbuf[0, h] = (total + ccore[0, 0, h].astype(F32)).astype(BF)
        sum_x(0, o_s, o_r, h).start()
    attend_image(mine)
    for h in range(2):
        cbuf[0, 1, h] = output_of(sibling, h).astype(BF)
        sum_near(0, o_s, o_r, h).start()
    for h in range(2):
        acc[pl.ds(h * half, half)] = output_of(t, h)
    for h in range(2):
        gather_x(gm, m_s, m_r, h).wait()
        gather_on(gm, m_s, m_r, h).start()
    for h in range(2):
        here = pl.ds(h * half, half)
        sum_near(0, o_s, o_r, h).wait()
        sum_x(0, o_s, o_r, h).wait()
        out = acc[here] + ccore[0, 1, h].astype(F32) + xin[0, h].astype(F32) + row(bo)
        attn[here] = out
        scaled, inverse = moments(hidden[here].astype(F32) + row(scale1) * out)
        gt[span(t, h)] = (scaled * row(gain2) + row(shift2)).astype(BF)
        gather_x(gt, t_s, t_r, h).start()
        gather_near(gt, t_s, t_r, h).start()

    esum[...] = jnp.zeros_like(esum)
    def feed(who, h):
        here = span(who, h)
        pre = jnp.dot(gt[here], we[...], preferred_element_type=F32) + row(be)
        grad = lax.dot_general(gm[here], wr[...], NT, preferred_element_type=F32)
        phi = 0.5 * (1.0 + lax.erf(pre * inv_sqrt_two))
        active = (pre * phi).astype(BF)
        act[here] = active
        grad = grad * (phi + pre * inv_sqrt_two_pi * jnp.exp(-0.5 * pre * pre))
        esum[...] += jnp.sum(grad, axis=0, keepdims=True)
        grad = grad.astype(BF)
        pgl[here] = grad
        part[here] = jnp.dot(active, wr[...], preferred_element_type=F32).astype(BF)
        return lax.dot_general(grad, we[...], NT, preferred_element_type=F32)
    def feed_own(h, c):
        acc[pl.ds(pl.multiple_of(h * half, 16), half)] = feed(t, h)
        return c
    lax.fori_loop(0, 2, feed_own, 0)
    for h in range(2):
        gather_near(gm, m_s, m_r, h).wait()
        gather_near(gt, t_s, t_r, h).wait()
    gather_x(gt, t_s, t_r, 0).wait()
    gather_on(gt, t_s, t_r, 0).start()
    def feed_near(h, c):
        cbuf[1, 1, h] = feed(sibling, h).astype(BF)
        return c
    lax.fori_loop(0, 2, feed_near, 0)
    for h in range(2):
        sum_near(1, n_s, n_r, h).start()
    gather_x(gt, t_s, t_r, 1).wait()
    gather_on(gt, t_s, t_r, 1).start()
    for h in range(2):
        gather_on(gm, m_s, m_r, h).wait()
        gather_on(gt, t_s, t_r, h).wait()
    def feed_far(h, c):
        cbuf[1, 0, h] = feed(diag, h).astype(BF)
        sum_far(1, n_s, n_r, h).start()
        total = feed(cross, h)
        sum_far(1, n_s, n_r, h).wait()
        xbuf[1, h] = (total + ccore[1, 0, h].astype(F32)).astype(BF)
        sum_x(1, n_s, n_r, h).start()
        return c
    lax.fori_loop(0, 2, feed_far, 0)

    tile = 128
    def reduce_grad(i, c):
        cols = pl.ds(pl.multiple_of(i * tile, tile), tile)
        x0[cols] = lax.dot_general(act[:, cols], gm[...], TN, preferred_element_type=F32).astype(BF)
        return c
    lax.fori_loop(0, act.shape[1] // tile, reduce_grad, 0)
    start_y(0)
    start_y(1)
    def expand_grad(i, c):
        cols = pl.ds(pl.multiple_of(i * tile, tile), tile)
        x1[cols] = lax.dot_general(gt[:, cols], pgl[...], TN, preferred_element_type=F32).astype(BF)
        return c
    lax.fori_loop(0, gt.shape[1] // tile, expand_grad, 0)

    wmine[...] = jnp.zeros_like(wmine)
    for h in range(2):
        here = pl.ds(h * half, half)
        sum_near(1, n_s, n_r, h).wait()
        sum_x(1, n_s, n_r, h).wait()
        grad = acc[here] + ccore[1, 1, h].astype(F32) + xin[1, h].astype(F32)
        out = attn[here]
        scaled, inverse = moments(hidden[here].astype(F32) + row(scale1) * out)
        after = cot[here].astype(F32) * alive[h * half:(h + 1) * half] + norm_back(grad, scaled, inverse, row(gain2))
        hidden_grad[here] = after
        agrad = after * row(scale1)
        ga[span(t, h)] = agrad.astype(BF)
        gather_x(ga, a_s, a_r, h).start()
        gather_near(ga, a_s, a_r, h).start()
        wmine[2:3, :] += jnp.sum(after * out, axis=0, keepdims=True)
        wmine[3:4, :] += jnp.sum(agrad, axis=0, keepdims=True)
        wmine[4:5, :] += jnp.sum(grad * scaled, axis=0, keepdims=True)
        wmine[5:6, :] += jnp.sum(grad, axis=0, keepdims=True)
    step_a(0)
    def mixture_of(who):
        here = rows_at(who)
        dmix[here] = lax.dot_general(ga[here], wo[...], NT, preferred_element_type=F32).astype(BF)
    mixture_of(t)
    gather_x(ga, a_s, a_r, 0).wait()
    gather_on(ga, a_s, a_r, 0).start()
    for h in range(2):
        gather_near(ga, a_s, a_r, h).wait()
    mixture_of(sibling)
    step_a(1)
    gather_x(ga, a_s, a_r, 1).wait()
    gather_on(ga, a_s, a_r, 1).start()
    mixture_of(cross)
    for h in range(2):
        gather_on(ga, a_s, a_r, h).wait()
    mixture_of(diag)

    smine[...] = jnp.zeros_like(smine)
    smine[2:3, :] = esum[...]
    def attention_back(slot):
        here = slice(slot * SEQ, (slot + 1) * SEQ)
        q = q_buf[here]
        k = k_buf[here]
        v = v_buf[here]
        dd = dmix[here]
        qt = q.T
        dt = dd.T
        is_high = jnp.where(res[slot] == 1, 1.0, 0.0).astype(F32)
        out = jnp.zeros((SEQ, width), F32)
        dks = []
        dvs = []
        nh = ghi.shape[1]
        nl, ml = glo.shape[1:]
        for h in range(heads):
            mask = head_mask(h, width)
            p = pb[slot, h]
            dp = lax.dot_general(dd * mask, v, NT, preferred_element_type=F32)
            pf = p.astype(F32)
            m = pf * dp
            ds = m - pf * jnp.sum(m, axis=1, keepdims=True)
            if slot == 0:
                ghi[h] = ds[:nh] * is_high
                glo[h] = ds[:nl, :ml] * (1.0 - is_high)
            else:
                ghi[h] += ds[:nh] * is_high
                glo[h] += ds[:nl, :ml] * (1.0 - is_high)
            low = ds.astype(BF)
            out = out + jnp.dot(low, k * mask, preferred_element_type=F32)
            dks.append(jnp.dot(qt[h*HD:(h+1)*HD], low, preferred_element_type=F32))
            dvs.append(jnp.dot(dt[h*HD:(h+1)*HD], p, preferred_element_type=F32))
        out = out * scale
        smine[0:1, 0:width] += jnp.sum(out, axis=0, keepdims=True)
        q_buf[here] = out.astype(BF)
        k_buf[here] = jnp.concatenate(dks, axis=0).T.astype(BF)
        out = jnp.concatenate(dvs, axis=0).T
        smine[1:2, 0:width] += jnp.sum(out, axis=0, keepdims=True)
        v_buf[here] = out.astype(BF)
    attention_back(0)
    step_a(2)
    attention_back(1)
    step_b(0)
    step_a(3)

    def back(who):
        here = rows_at(who)
        total = jnp.dot(q_buf[here], wq[...], preferred_element_type=F32)
        total = total + jnp.dot(k_buf[here], wk[...], preferred_element_type=F32)
        return total + jnp.dot(v_buf[here], wv[...], preferred_element_type=F32)
    def send(buf, value):
        for h in range(2):
            buf[h] = value[h * half:(h + 1) * half].astype(BF)
    def whole(ref):
        return jnp.concatenate([ref[0], ref[1]], axis=0).astype(F32)
    a_far = remote(cbuf.at[0, 0], acore.at[0], r_s.at[0], r_r.at[0], (d, sibling))
    a_near = remote(cbuf.at[0, 1], acore.at[1], r_s.at[1], r_r.at[1], (d, sibling))
    a_cross = remote(xbuf.at[0], across, r_s.at[2], r_r.at[2], (d, cross))
    b_far = remote(part.at[rows_at(diag)], bcore.at[0], r_s.at[3], r_r.at[3], (d, sibling))
    b_near = remote(part.at[rows_at(sibling)], bcore.at[1], r_s.at[4], r_r.at[4], (d, sibling))
    b_cross = remote(xbuf.at[1], bcross, r_s.at[5], r_r.at[5], (d, cross))
    send(cbuf.at[0, 0], back(diag))
    a_far.start()
    b_far.start()
    total = back(cross)
    a_far.wait()
    send(xbuf.at[0], total + whole(acore.at[0]))
    a_cross.start()
    for j, (left, right) in enumerate(((q_buf, g1), (k_buf, g1), (v_buf, g1), (mix, ga))):
        x2[j * width:(j + 1) * width, :] = lax.dot_general(left[...], right[...], TN, preferred_element_type=F32).astype(BF)
    start_y(4)
    start_y(5)
    step_b(1)
    send(cbuf.at[0, 1], back(sibling))
    a_near.start()
    b_near.start()
    acc[...] = back(t)
    b_far.wait()
    send(xbuf.at[1], part[rows_at(cross)].astype(F32) + bcore[0].astype(F32))
    segments = 7
    n_hi = (-(-P_HI // UN))
    def scatter_part(s):
        lo, hi = n_hi * s // segments, n_hi * (s + 1) // segments
        scatter_run(ihi, ghi, thi, lo, hi, s == 0)
    scatter_part(0)
    step_a(4)
    step_d(0)
    step_b(2)
    a_cross.wait()
    b_cross.start()
    a_near.wait()
    grad = acc[...] + whole(acore.at[1]) + whole(across)
    scaled, inverse = moments(hidden[...].astype(F32))
    wmine[0:1, :] = jnp.sum(grad * scaled, axis=0, keepdims=True)
    wmine[1:2, :] = jnp.sum(grad, axis=0, keepdims=True)
    hidden_grad[...] += norm_back(grad, scaled, inverse, row(gain1))
    scatter_part(1)
    step_a(5)
    step_d(1)
    step_b(3)
    scatter_part(2)
    b_near.wait()
    b_cross.wait()
    out = part[rows_at(t)].astype(F32) + bcore[1].astype(F32) + whole(bcross) + row(rbias)
    after = hidden[...].astype(F32) + row(scale1) * attn[...]
    result[...] = ((after + row(scale2) * out) * alive).astype(BF)
    up = cot[...].astype(F32) * alive
    wmine[6:7, :] = jnp.sum(up * out, axis=0, keepdims=True)
    wmine[7:8, :] = jnp.sum(up * row(scale2), axis=0, keepdims=True)
    def w_copy(k):
        return remote(wmine, wten.at[k], w_s.at[k], w_r.at[k], (d, lax.rem(t + k, 4)))
    def v_copy(j, k):
        src, dst = ((wmid, wdp), (smine, sdp), (tmine, tdp))[j]
        return remote(src, dst.at[k], v_s.at[j, k], v_r.at[j, k], (lax.rem(d + k, 8), t))
    if sums:
        for k in range(1, 4):
            w_copy(k).start()
        for k in range(1, 8):
            v_copy(1, k).start()
    step_d(2)
    step_b(4)
    scatter_part(3)
    total = wmine[...]
    if sums:
        for k in range(1, 4):
            w_copy(k).wait()
            total = total + wten[k]
    wmid[...] = total
    if sums:
        for k in range(1, 8):
            v_copy(0, k).start()
    step_b(5)
    step_d(3)
    scatter_part(4)
    step_d(4)
    scatter_part(5)
    scatter_part(6)
    scatter_run(ilo, glo, tlo, 0, -(-P_LO // UN), True)
    tables[...] = jnp.zeros_like(tables)
    n = tlo.shape[1]
    tables[:, 0:n] = tlo[...]
    tables[:, n:n + thi.shape[1]] = thi[...]
    wide[...] = wmid[...]
    slim[...] = smine[...]
    if not sums:
        o0[...] = x0[...]
        o1[...] = x1[...]
        o2[...] = x2[...]
        return
    tmine[...] = tables[...].astype(BF)
    tables[...] = tmine[...].astype(F32)
    for k in range(1, 8):
        v_copy(2, k).start()
    step_d(5)
    for k in range(1, 8):
        v_copy(0, k).wait()
        v_copy(1, k).wait()
        wide[...] += wdp[k]
        slim[...] += sdp[k]
    for k in range(1, 8):
        v_copy(2, k).wait()
        tables[...] += tdp[k].astype(F32)
    for n in range(CHUNKS):
        e_copy(n).wait()

def layer(scale, sums, res, counts, hidden, gain1, shift1, wq, bq, wk, wv, bv, wo, bo, scale1, gain2, shift2, we, be, wr, rbias, scale2, cot, table_low, table_high, ilo, ihi, n_lo, n_hi):
    rows, model = hidden.shape
    total = rows * 4
    width = wq.shape[0]
    inner = we.shape[1]
    heads = table_low.shape[1]
    def chunks(table):
        n = -(-table.shape[0] // 256) * 256
        w = jnp.round(jnp.pad(table.T, ((0, 0), (0, n - table.shape[0]))) * PACK).astype(jnp.int32)
        w = w.reshape(heads, 2, n // 256, 1, 128)
        w = (w[:, 1] << 16) | (w[:, 0] & 65535)
        return jnp.broadcast_to(w, (heads, n // 256, 8, 128))
    vm = pl.BlockSpec(memory_space=pltpu.VMEM)
    sm = pl.BlockSpec(memory_space=pltpu.SMEM)
    dma = pltpu.SemaphoreType.DMA
    V = pltpu.VMEM
    S = jax.ShapeDtypeStruct
    operands = (hidden, gain1, shift1, wq, bq, wk, wv, bv, wo, bo, scale1, gain2, shift2, we, be, wr, rbias, scale2, cot, chunks(table_low), chunks(table_high), ilo, ihi)
    tshape = (heads * BB, 128)
    half = rows // 2
    return pl.pallas_call(functools.partial(layer_kernel, scale, sums),
        out_shape=(S((inner, model), BF), S((model, inner), BF), S((4 * width, model), BF), S((rows, model), BF), S((rows, model), F32), S((8, model), F32), S((8, model), F32), S(tshape, F32)),
        in_specs=[sm, sm] + [vm] * len(operands), out_specs=(vm,) * 8,
        scratch_shapes=[V((total, model), BF)] * 4 + [V((total, width), BF)] * 5 + [V((SLOTS, heads, SEQ, SEQ), BF)]
            + [V((total, inner), BF)] * 2 + [V((total, model), BF)] + [V((rows, model), F32)] * 2
            + [V((inner, model), BF), V((model, inner), BF), V((4 * width, model), BF), V((heads,) + ihi.shape, F32), V((heads,) + ilo.shape, F32), V((1, inner), F32)]
            + [V((2, 2, 2, half, model), BF)] * 2 + [V((2, 2, half, model), BF)] * 2
            + [V((2, 2, half, model), BF), V((2, half, model), BF), V((2, rows, model), BF), V((2, half, model), BF)]
            + [V((CHUNKS, 192, model), BF), V((CHUNKS, 3, 48, model), BF)]
            + [V((heads * BB, n_lo), F32), V((heads * BB, n_hi), F32)]
            + [V((8, model), F32)] * 3 + [V(tshape, BF), V((4, 8, model), F32), V((8, 8, model), F32), V((8, 8, model), F32), V((8,) + tshape, BF)]
            + [dma((6,))] * 12
            + [dma((CHUNKS,)), dma((CHUNKS,)), dma((CHUNKS, 4)), dma((CHUNKS, 4)), dma((CHUNKS, 4)), dma((CHUNKS, 4)), dma((CHUNKS,)), dma((CHUNKS,)),
               dma((6,)), dma((6,)), dma((4,)), dma((4,)), dma((3, 8)), dma((3, 8))],
        name="layer", cost_estimate=pl.CostEstimate(flops=100 * 10**9, bytes_accessed=60 * 10**6, transcendentals=0),
        compiler_params=pltpu.CompilerParams(collective_id=0, has_side_effects=True, vmem_limit_bytes=63 << 20))(res, counts, *operands)


def local(
    hidden,
    first_gain,
    first_shift,
    query_weight,
    query_bias,
    key_weight,
    value_weight,
    value_bias,
    output_weight,
    output_bias,
    first_scale,
    second_gain,
    second_shift,
    expand_weight,
    expand_bias,
    reduce_weight,
    reduce_bias,
    second_scale,
    table_low,
    table_high,
    resolution,
    counts,
    index_low,
    index_high,
    cotangent,
):
    floating = jnp.float32
    heads_dev = table_low.shape[1]
    width = query_weight.shape[1]
    index_low_pad = jnp.pad(index_low, ((0, 256 - P_LO), (0, 256 - P_LO)))
    index_high_pad = jnp.pad(index_high, ((0, 592 - P_HI), (0, SEQ - P_HI)))
    n_low = -(-table_low.shape[0] // (BB * 16)) * 16
    n_high = -(-table_high.shape[0] // (BB * 16)) * 16
    known = lax.axis_size("dp") == 8
    reduce_grad, expand_grad, attn_grads, result, hidden_grad, wide, slim, tables = layer(
        HD ** (-0.5),
        known,
        resolution,
        counts,
        hidden,
        first_gain,
        first_shift,
        query_weight.T,
        query_bias,
        key_weight.T,
        value_weight.T,
        value_bias,
        output_weight,
        output_bias,
        first_scale,
        second_gain,
        second_shift,
        expand_weight,
        expand_bias,
        reduce_weight,
        reduce_bias,
        second_scale,
        cotangent,
        table_low,
        table_high,
        index_low_pad,
        index_high_pad,
        n_low,
        n_high,
    )
    reduce_grad = reduce_grad.astype(floating)
    expand_grad = expand_grad.astype(floating)
    attn_grads = attn_grads.astype(floating)
    if not known:
        reduce_grad, expand_grad, attn_grads, slim, tables = lax.psum(
            (reduce_grad, expand_grad, attn_grads, slim, tables), "dp"
        )
        wide = lax.psum(wide, ("dp", "tensor"))

    def unpack(block, count):
        block = block.reshape(heads_dev, BB, -1).transpose(2, 1, 0)
        return block.reshape(-1, heads_dev)[:count]

    return (
        result,
        hidden_grad,
        wide[0],
        wide[1],
        attn_grads[:width].T,
        slim[0, :width],
        attn_grads[width : 2 * width].T,
        attn_grads[2 * width : 3 * width].T,
        slim[1, :width],
        attn_grads[3 * width :],
        wide[3],
        wide[2],
        wide[4],
        wide[5],
        expand_grad,
        slim[2],
        reduce_grad,
        wide[7],
        wide[6],
        unpack(tables[:, :n_low], table_low.shape[0]),
        unpack(tables[:, n_low : n_low + n_high], table_high.shape[0]),
    )


def solution(mesh):
    in_specs = (
        P(("dp", "tensor"), None),
        P(),
        P(),
        P(None, "tensor"),
        P("tensor"),
        P(None, "tensor"),
        P(None, "tensor"),
        P("tensor"),
        P("tensor", None),
        P(),
        P(),
        P(),
        P(),
        P(None, "tensor"),
        P("tensor"),
        P("tensor", None),
        P(),
        P(),
        P(None, "tensor"),
        P(None, "tensor"),
        P("dp"),
        P("dp"),
        P(),
        P(),
        P(("dp", "tensor"), None),
    )
    out_specs = (
        P(("dp", "tensor"), None),
        P(("dp", "tensor"), None),
        P(),
        P(),
        P(None, "tensor"),
        P("tensor"),
        P(None, "tensor"),
        P(None, "tensor"),
        P("tensor"),
        P("tensor", None),
        P(),
        P(),
        P(),
        P(),
        P(None, "tensor"),
        P("tensor"),
        P("tensor", None),
        P(),
        P(),
        P(None, "tensor"),
        P(None, "tensor"),
    )
    return jax.shard_map(local, mesh=mesh, in_specs=in_specs, out_specs=out_specs, check_vma=False)
```

time: 269 us -> 208 us (0.77)
  Pallas kernels: 228 us -> 183 us
  between operations: 14.9 us -> 1.38 us
  other arithmetic: 8.07 us -> 4.83 us
    pallas_call x3 -> x1, Pallas kernels: 228 us -> 183 us  [layer(): pl.pallas_call(functools.partial(layer_kernel, scale, sums), out_shape=(S...]
    unnamed x32 -> x12, local copies, waits for them, and re-layouts: 5.98 us -> 2.49 us
  transfers between devices with their start and end apart: 1 -> 0, of which waited for: 0 -> 0; matrix products, arithmetic and copies ran while one was open for 0% -> 0% of each run, Pallas kernels for 8% -> 0%
where the time goes in v3:
time: 208 us; the launch traced here: 207 us
  Pallas kernels  183 us (88%)
  local copies, waits for them, and re-layouts  17.7 us (9%)
  other arithmetic  4.83 us (2%)
    pallas_call x1, Pallas kernels, layer(): pl.pallas_call(functools.partial(layer_kernel, scale, sums), out_shape=(S...  183 us

profile of v3, /device:TPU:0, one launch (start us, length us, event | category | flops | bytes accessed | tf_op | source)
XLA Modules:
  0.0 207.1 jit_solution(17578945470476896037)
XLA Ops:
  1.3 0.7 round-nearest-even_convert_fusion.1
  2.0 0.6 broadcast_in_dim.4.tab_lo
  2.7 0.8 round-nearest-even_convert_fusion
  3.5 0.7 broadcast_in_dim.5.tab_hi
  4.1 1.6 pad.18.ilo
  5.8 2.6 %pad.19.ihi = s32[592,640]{1,0:T(8,128)} pad(s32[577,577]{1,0:T(8,128)} %param.48, s32[]{:T(128)} %constant.3.clone.1), padding=0_15x0_63 | pad | bytes 2847240 | tf_op jit(solution)/shard_map/jit(_pad)/pad | solution.py:632
  8.4 183.2 %layer.1 = (bf16[768,768]{1,0:T(8,128)(2,1)}, bf16[768,768]{1,0:T(8,128)(2,1)}, bf16[768,768]{1,0:T(8,128)(2,1)}, bf16[320,768]{1,0:T(8,128)(2,1)}, f32[320,768]...) custom-call(s32[2]{0:T(128)} %res.1, s32[1]{0:T(128)S(6)} %copy.56.counts, ...), custom_call_target="tpu_custom_call" | custom-call | flops 99999997952 | bytes 60000000 | tf_op jit(solution)/shard_map/layer/pallas_call | solution.py:583
  191.6 0.0 copy-start
  191.6 1.4 fusion.4
  193.0 1.9 slice_reduce_fusion
  194.9 0.9 copy.52
  195.8 0.1 reshape.105
  195.9 0.6 slice.100
  196.5 0.9 slice.90
  197.3 0.1 copy.53
  197.5 0.1 reshape.107
  197.6 0.6 slice.101
  198.2 1.8 slice.99
  200.0 0.0 copy-done
  200.0 0.2 convert_element_type.21
  200.2 0.0 copy-start.2
  200.2 1.2 slice_bitcast_fusion
  201.4 0.7 copy-done.2
  202.1 0.0 copy-start.1
  202.1 1.6 convert_element_type.22
  203.7 0.1 copy-done.1
  203.8 0.0 copy-start.4
  203.8 1.6 convert_element_type.23
  205.4 0.0 copy-done.4
  205.4 0.8 copy.57
  206.1 0.0 copy-done.3
  206.1 0.9 copy.58
  (5 shorter events, 0.1 us)
Async XLA Ops:
  191.6 8.4 %copy-start = (bf16[768,768]{1,0:T(8,128)(2,1)S(1)}, bf16[768,768]{1,0:T(8,128)(2,1)}, u32[]{:S(2)}) copy-start(bf16[768,768]{1,0:T(8,128)(2,1)} %get-tuple-element.32) | copy-start | bytes 3538948
  200.2 1.9 copy-start.2
  202.1 1.7 copy-start.1
  203.8 1.6 copy-start.4
  203.8 2.4 %copy-start.3 = (f32[320,768]{1,0:T(8,128)S(1)}, f32[320,768]{1,0:T(8,128)}, u32[]{:S(2)}) copy-start(f32[320,768]{1,0:T(8,128)} %get-tuple-element.73) | copy-start | bytes 2949124

commit v4 on v3

--- a/solution.py
+++ b/solution.py
@@ -118,11 +118,12 @@
     lax.fori_loop(first, last, body, 0)
 
 def layer_kernel(scale, sums, res, counts, hidden, gain1, shift1, wq, bq, wk, wv, bv, wo, bo, scale1, gain2, shift2, we, be, wr, rbias, scale2, cot,
-                 tab_lo, tab_hi, ilo, ihi,
-                 o0, o1, o2, result, hidden_grad, wide, slim, tables,
+                 table_lo, table_hi, ilo_in, ihi_in,
+                 o0, o1, o2, result, hidden_grad, small, tlow, thigh,
+                 tab_lo, tab_hi, raw, ilo, ihi, flip,
                  g1, gm, gt, ga, q_buf, k_buf, v_buf, mix, dmix, pb, act, pgl, part, acc, attn, x0, x1, x2, ghi, glo, esum,
                  cbuf, ccore, xbuf, xin, acore, across, bcore, bcross, ybuf, zbuf,
-                 tlo, thi, wmine, wmid, smine, tmine, wten, wdp, sdp, tdp,
+                 tlo, thi, wmine, smine, wten, vec, vland, vout, tbl, tland, tout,
                  h_s, h_r, m_s, m_r, t_s, t_r, a_s, a_r, o_s, o_r, n_s, n_r,
                  y_s, y_r, z_s, z_r, g_s, g_r, e_s, e_r, r_s, r_r, w_s, w_r, v_s, v_r):
     d = lax.axis_index("dp")
@@ -137,6 +138,7 @@
     half = rows // 2
     slots, heads = pb.shape[:2]
     width = q_buf.shape[1]
+    model = g1.shape[1]
     barrier = pltpu.get_barrier_semaphore()
     for k in range(1, 4):
         pl.semaphore_signal(barrier, inc=1, device_id=(d, lax.rem(t + k, 4)), device_id_type=MESH)
@@ -188,8 +190,6 @@
         y_copy(n).start()
     def step_a(n):
         y_copy(n).wait()
-        if n < 2:
-            y_copy(n + 2).start()
         here = at(n, side * part_y, part_y)
         arrays[n // 2][here] = (arrays[n // 2][here].astype(F32) + ybuf[n].astype(F32)).astype(BF)
         for k in range(1, 4):
@@ -219,6 +219,20 @@
         gather_near(g1, h_s, h_r, h).start()
     alive = live_of(t, rows, res, counts)
     gm[rows_at(t)] = (cot[...].astype(F32) * alive * row(scale2)).astype(BF)
+    ilo[...] = jnp.zeros_like(ilo)
+    ilo[0:P_LO, 0:P_LO] = ilo_in[...]
+    ihi[...] = jnp.zeros_like(ihi)
+    ihi[0:P_HI, 0:P_HI] = ihi_in[...]
+    for table, packed in ((table_lo, tab_lo), (table_hi, tab_hi)):
+        nch = packed.shape[1]
+        raw[...] = jnp.zeros_like(raw)
+        raw[:, 0:table.shape[1]] = table[...]
+        for k in range(nch):
+            low = (raw[:, k * 128:(k + 1) * 128] * PACK + 32768.5).astype(jnp.int32) - 32768
+            high = (raw[:, (k + nch) * 128:(k + nch + 1) * 128] * PACK + 32768.5).astype(jnp.int32) - 32768
+            word = (high << 16) | (low & 65535)
+            for h in range(heads):
+                packed[h, k] = jnp.broadcast_to(word[h:h + 1, :], (8, 128))
     look = functools.partial(bias_rows, res, tab_lo, tab_hi, ilo, ihi, pb)
     n_low = -(-P_LO // 16)
     n_high = -(-P_HI // 16)
@@ -321,20 +335,13 @@
     for h in range(2):
         gather_near(gm, m_s, m_r, h).wait()
         gather_near(gt, t_s, t_r, h).wait()
-    gather_x(gt, t_s, t_r, 0).wait()
-    gather_on(gt, t_s, t_r, 0).start()
-    def feed_near(h, c):
+        gather_on(gm, m_s, m_r, h).wait()
+    def feed_rest(h, c):
+        gather_x(gt, t_s, t_r, h).wait()
+        gather_on(gt, t_s, t_r, h).start()
         cbuf[1, 1, h] = feed(sibling, h).astype(BF)
-        return c
-    lax.fori_loop(0, 2, feed_near, 0)
-    for h in range(2):
         sum_near(1, n_s, n_r, h).start()
-    gather_x(gt, t_s, t_r, 1).wait()
-    gather_on(gt, t_s, t_r, 1).start()
-    for h in range(2):
-        gather_on(gm, m_s, m_r, h).wait()
         gather_on(gt, t_s, t_r, h).wait()
-    def feed_far(h, c):
         cbuf[1, 0, h] = feed(diag, h).astype(BF)
         sum_far(1, n_s, n_r, h).start()
         total = feed(cross, h)
@@ -342,7 +349,7 @@
         xbuf[1, h] = (total + ccore[1, 0, h].astype(F32)).astype(BF)
         sum_x(1, n_s, n_r, h).start()
         return c
-    lax.fori_loop(0, 2, feed_far, 0)
+    lax.fori_loop(0, 2, feed_rest, 0)
 
     tile = 128
     def reduce_grad(i, c):
@@ -351,15 +358,8 @@
         return c
     lax.fori_loop(0, act.shape[1] // tile, reduce_grad, 0)
     start_y(0)
-    start_y(1)
-    def expand_grad(i, c):
-        cols = pl.ds(pl.multiple_of(i * tile, tile), tile)
-        x1[cols] = lax.dot_general(gt[:, cols], pgl[...], TN, preferred_element_type=F32).astype(BF)
-        return c
-    lax.fori_loop(0, gt.shape[1] // tile, expand_grad, 0)
-
     wmine[...] = jnp.zeros_like(wmine)
-    for h in range(2):
+    def second_back(h):
         here = pl.ds(h * half, half)
         sum_near(1, n_s, n_r, h).wait()
         sum_x(1, n_s, n_r, h).wait()
@@ -376,17 +376,28 @@
         wmine[3:4, :] += jnp.sum(agrad, axis=0, keepdims=True)
         wmine[4:5, :] += jnp.sum(grad * scaled, axis=0, keepdims=True)
         wmine[5:6, :] += jnp.sum(grad, axis=0, keepdims=True)
+    second_back(0)
+    def expand_grad(i, c):
+        cols = pl.ds(pl.multiple_of(i * tile, tile), tile)
+        x1[cols] = lax.dot_general(gt[:, cols], pgl[...], TN, preferred_element_type=F32).astype(BF)
+        return c
+    lax.fori_loop(0, gt.shape[1] // tile, expand_grad, 0)
+    start_y(1)
+    second_back(1)
     step_a(0)
+    start_y(2)
     def mixture_of(who):
         here = rows_at(who)
         dmix[here] = lax.dot_general(ga[here], wo[...], NT, preferred_element_type=F32).astype(BF)
     mixture_of(t)
+    step_a(1)
+    start_y(3)
     gather_x(ga, a_s, a_r, 0).wait()
     gather_on(ga, a_s, a_r, 0).start()
     for h in range(2):
         gather_near(ga, a_s, a_r, h).wait()
+    step_b(0)
     mixture_of(sibling)
-    step_a(1)
     gather_x(ga, a_s, a_r, 1).wait()
     gather_on(ga, a_s, a_r, 1).start()
     mixture_of(cross)
@@ -395,7 +406,7 @@
     mixture_of(diag)
 
     smine[...] = jnp.zeros_like(smine)
-    smine[2:3, :] = esum[...]
+    smine[1:2, :] = esum[...]
     def attention_back(slot):
         here = slice(slot * SEQ, (slot + 1) * SEQ)
         q = q_buf[here]
@@ -432,13 +443,11 @@
         q_buf[here] = out.astype(BF)
         k_buf[here] = jnp.concatenate(dks, axis=0).T.astype(BF)
         out = jnp.concatenate(dvs, axis=0).T
-        smine[1:2, 0:width] += jnp.sum(out, axis=0, keepdims=True)
+        smine[0:1, 256:256 + width] += jnp.sum(out, axis=0, keepdims=True)
         v_buf[here] = out.astype(BF)
     attention_back(0)
     step_a(2)
     attention_back(1)
-    step_b(0)
-    step_a(3)
 
     def back(who):
         here = rows_at(who)
@@ -459,30 +468,34 @@
     send(cbuf.at[0, 0], back(diag))
     a_far.start()
     b_far.start()
+    step_a(3)
     total = back(cross)
     a_far.wait()
     send(xbuf.at[0], total + whole(acore.at[0]))
     a_cross.start()
     for j, (left, right) in enumerate(((q_buf, g1), (k_buf, g1), (v_buf, g1), (mix, ga))):
         x2[j * width:(j + 1) * width, :] = lax.dot_general(left[...], right[...], TN, preferred_element_type=F32).astype(BF)
+    step_b(1)
     start_y(4)
-    start_y(5)
-    step_b(1)
     send(cbuf.at[0, 1], back(sibling))
     a_near.start()
     b_near.start()
     acc[...] = back(t)
     b_far.wait()
     send(xbuf.at[1], part[rows_at(cross)].astype(F32) + bcore[0].astype(F32))
-    segments = 7
-    n_hi = (-(-P_HI // UN))
-    def scatter_part(s):
-        lo, hi = n_hi * s // segments, n_hi * (s + 1) // segments
-        scatter_run(ihi, ghi, thi, lo, hi, s == 0)
-    scatter_part(0)
+    step_b(2)
+    start_y(5)
+    n_hi = -(-P_HI // UN)
+    done = [0]
+    def scatter_part(count):
+        first, last = done[0], min(done[0] + count, n_hi)
+        scatter_run(ihi, ghi, thi, first, last, first == 0)
+        done[0] = last
+    scatter_part(4)
+    step_d(0)
+    step_b(3)
+    step_d(1)
     step_a(4)
-    step_d(0)
-    step_b(2)
     a_cross.wait()
     b_cross.start()
     a_near.wait()
@@ -491,11 +504,10 @@
     wmine[0:1, :] = jnp.sum(grad * scaled, axis=0, keepdims=True)
     wmine[1:2, :] = jnp.sum(grad, axis=0, keepdims=True)
     hidden_grad[...] += norm_back(grad, scaled, inverse, row(gain1))
-    scatter_part(1)
+    scatter_part(8)
     step_a(5)
-    step_d(1)
-    step_b(3)
-    scatter_part(2)
+    step_d(2)
+    scatter_part(4)
     b_near.wait()
     b_cross.wait()
     out = part[rows_at(t)].astype(F32) + bcore[1].astype(F32) + whole(bcross) + row(rbias)
@@ -506,94 +518,123 @@
     wmine[7:8, :] = jnp.sum(up * row(scale2), axis=0, keepdims=True)
     def w_copy(k):
         return remote(wmine, wten.at[k], w_s.at[k], w_r.at[k], (d, lax.rem(t + k, 4)))
+    def eighth(buf, who):
+        count = buf.shape[0] // 8
+        return buf.at[pl.ds(pl.multiple_of(who * count, 8), count)]
     def v_copy(j, k):
-        src, dst = ((wmid, wdp), (smine, sdp), (tmine, tdp))[j]
-        return remote(src, dst.at[k], v_s.at[j, k], v_r.at[j, k], (lax.rem(d + k, 8), t))
+        buf, land = ((vec, vland), (tbl, tland))[j]
+        to = lax.rem(d + k, 8)
+        return remote(eighth(buf, to), land.at[k], v_s.at[j, k], v_r.at[j, k], (to, t))
+    def u_copy(j, k):
+        buf = (vout, tout)[j]
+        return remote(eighth(buf, d), eighth(buf, d), v_s.at[2 + j, k], v_r.at[2 + j, k], (lax.rem(d + k, 8), t))
+    def small_start(j):
+        for k in range(1, 8):
+            v_copy(j, k).start()
+    def small_turn(j):
+        buf, land = ((vec, vland), (tbl, tland))[j]
+        total = eighth(buf, d)[...]
+        for k in range(1, 8):
+            v_copy(j, k).wait()
+            total = total + land[k]
+        eighth((vout, tout)[j], d)[...] = total
+        for k in range(1, 8):
+            u_copy(j, k).start()
+    def small_end(j):
+        for k in range(1, 8):
+            u_copy(j, k).wait()
+    if not sums:
+        def small_turn(j):
+            (vout, tout)[j][...] = (vec, tbl)[j][...]
+        small_start = small_end = lambda j: None
     if sums:
         for k in range(1, 4):
             w_copy(k).start()
-        for k in range(1, 8):
-            v_copy(1, k).start()
-    step_d(2)
+    step_d(3)
+    scatter_part(4)
     step_b(4)
-    scatter_part(3)
     total = wmine[...]
     if sums:
         for k in range(1, 4):
             w_copy(k).wait()
             total = total + wten[k]
-    wmid[...] = total
-    if sums:
-        for k in range(1, 8):
-            v_copy(0, k).start()
+    vec[...] = jnp.zeros_like(vec)
+    lanes = model // 128
+    for r in range(8):
+        for j in range(lanes):
+            vec[r * lanes + j:r * lanes + j + 1, :] = total[r:r + 1, j * 128:(j + 1) * 128]
+    for r in range(2):
+        for j in range(lanes):
+            vec[(8 + r) * lanes + j:(8 + r) * lanes + j + 1, :] = smine[r:r + 1, j * 128:(j + 1) * 128]
+    small_start(0)
+    scatter_part(4)
     step_b(5)
-    step_d(3)
     scatter_part(4)
+    small_turn(0)
     step_d(4)
-    scatter_part(5)
-    scatter_part(6)
+    scatter_part(n_hi)
+    step_d(5)
     scatter_run(ilo, glo, tlo, 0, -(-P_LO // UN), True)
-    tables[...] = jnp.zeros_like(tables)
-    n = tlo.shape[1]
-    tables[:, 0:n] = tlo[...]
-    tables[:, n:n + thi.shape[1]] = thi[...]
-    wide[...] = wmid[...]
-    slim[...] = smine[...]
+    per = (thi.shape[1] + tlo.shape[1]) // 4
+    tbl[...] = jnp.zeros_like(tbl)
+    def spread(src, base):
+        count = src.shape[1] // 4
+        for h in range(heads):
+            flip[0:src.shape[1], :] = src[h * BB:(h + 1) * BB, :].T
+            pieces = [flip[pl.ds(i, count, stride=4), :] for i in range(4)]
+            start = h * per + base
+            tbl[start:start + count, :] = jnp.concatenate(pieces, axis=1)
+    spread(thi, 0)
+    spread(tlo, thi.shape[1] // 4)
     if not sums:
         o0[...] = x0[...]
         o1[...] = x1[...]
         o2[...] = x2[...]
-        return
-    tmine[...] = tables[...].astype(BF)
-    tables[...] = tmine[...].astype(F32)
-    for k in range(1, 8):
-        v_copy(2, k).start()
-    step_d(5)
-    for k in range(1, 8):
-        v_copy(0, k).wait()
-        v_copy(1, k).wait()
-        wide[...] += wdp[k]
-        slim[...] += sdp[k]
-    for k in range(1, 8):
-        v_copy(2, k).wait()
-        tables[...] += tdp[k].astype(F32)
-    for n in range(CHUNKS):
-        e_copy(n).wait()
+    small_start(1)
+    small_end(0)
+    for r in range(10):
+        for j in range(lanes):
+            small[r:r + 1, j * 128:(j + 1) * 128] = vout[r * lanes + j:r * lanes + j + 1, :]
+    small_turn(1)
+    small_end(1)
+    for src, base, count in ((thigh, 0, thi.shape[1] // 4), (tlow, thi.shape[1] // 4, tlo.shape[1] // 4)):
+        for h in range(heads):
+            for r in range(count):
+                at_row = h * per + base + r
+                src[h:h + 1, r * 128:(r + 1) * 128] = tout[at_row:at_row + 1, :]
+    if sums:
+        for n in range(CHUNKS):
+            e_copy(n).wait()
 
 def layer(scale, sums, res, counts, hidden, gain1, shift1, wq, bq, wk, wv, bv, wo, bo, scale1, gain2, shift2, we, be, wr, rbias, scale2, cot, table_low, table_high, ilo, ihi, n_lo, n_hi):
     rows, model = hidden.shape
     total = rows * 4
     width = wq.shape[0]
     inner = we.shape[1]
-    heads = table_low.shape[1]
-    def chunks(table):
-        n = -(-table.shape[0] // 256) * 256
-        w = jnp.round(jnp.pad(table.T, ((0, 0), (0, n - table.shape[0]))) * PACK).astype(jnp.int32)
-        w = w.reshape(heads, 2, n // 256, 1, 128)
-        w = (w[:, 1] << 16) | (w[:, 0] & 65535)
-        return jnp.broadcast_to(w, (heads, n // 256, 8, 128))
+    heads, e_lo = table_low.shape
+    e_hi = table_high.shape[1]
     vm = pl.BlockSpec(memory_space=pltpu.VMEM)
     sm = pl.BlockSpec(memory_space=pltpu.SMEM)
     dma = pltpu.SemaphoreType.DMA
     V = pltpu.VMEM
     S = jax.ShapeDtypeStruct
-    operands = (hidden, gain1, shift1, wq, bq, wk, wv, bv, wo, bo, scale1, gain2, shift2, we, be, wr, rbias, scale2, cot, chunks(table_low), chunks(table_high), ilo, ihi)
-    tshape = (heads * BB, 128)
+    operands = (hidden, gain1, shift1, wq, bq, wk, wv, bv, wo, bo, scale1, gain2, shift2, we, be, wr, rbias, scale2, cot, table_low, table_high, ilo, ihi)
     half = rows // 2
     return pl.pallas_call(functools.partial(layer_kernel, scale, sums),
-        out_shape=(S((inner, model), BF), S((model, inner), BF), S((4 * width, model), BF), S((rows, model), BF), S((rows, model), F32), S((8, model), F32), S((8, model), F32), S(tshape, F32)),
+        out_shape=(S((inner, model), BF), S((model, inner), BF), S((4 * width, model), BF), S((rows, model), BF), S((rows, model), F32), S((16, model), F32), S((heads, n_lo * 32), F32), S((heads, n_hi * 32), F32)),
         in_specs=[sm, sm] + [vm] * len(operands), out_specs=(vm,) * 8,
-        scratch_shapes=[V((total, model), BF)] * 4 + [V((total, width), BF)] * 5 + [V((SLOTS, heads, SEQ, SEQ), BF)]
+        scratch_shapes=[V((heads, -(-e_lo // 256), 8, 128), jnp.int32), V((heads, -(-e_hi // 256), 8, 128), jnp.int32), V((heads, -(-e_hi // 256) * 256), F32), V((208, 256), jnp.int32), V((592, SEQ), jnp.int32), V((n_hi, BB), F32)]
+            + [V((total, model), BF)] * 4 + [V((total, width), BF)] * 5 + [V((SLOTS, heads, SEQ, SEQ), BF)]
             + [V((total, inner), BF)] * 2 + [V((total, model), BF)] + [V((rows, model), F32)] * 2
-            + [V((inner, model), BF), V((model, inner), BF), V((4 * width, model), BF), V((heads,) + ihi.shape, F32), V((heads,) + ilo.shape, F32), V((1, inner), F32)]
+            + [V((inner, model), BF), V((model, inner), BF), V((4 * width, model), BF), V((heads, 592, SEQ), F32), V((heads, 208, 256), F32), V((1, inner), F32)]
             + [V((2, 2, 2, half, model), BF)] * 2 + [V((2, 2, half, model), BF)] * 2
             + [V((2, 2, half, model), BF), V((2, half, model), BF), V((2, rows, model), BF), V((2, half, model), BF)]
             + [V((CHUNKS, 192, model), BF), V((CHUNKS, 3, 48, model), BF)]
             + [V((heads * BB, n_lo), F32), V((heads * BB, n_hi), F32)]
-            + [V((8, model), F32)] * 3 + [V(tshape, BF), V((4, 8, model), F32), V((8, 8, model), F32), V((8, 8, model), F32), V((8,) + tshape, BF)]
+            + [V((8, model), F32)] * 2 + [V((4, 8, model), F32), V((64, 128), F32), V((8, 8, 128), F32), V((64, 128), F32), V((128, 128), F32), V((8, 16, 128), F32), V((128, 128), F32)]
             + [dma((6,))] * 12
             + [dma((CHUNKS,)), dma((CHUNKS,)), dma((CHUNKS, 4)), dma((CHUNKS, 4)), dma((CHUNKS, 4)), dma((CHUNKS, 4)), dma((CHUNKS,)), dma((CHUNKS,)),
-               dma((6,)), dma((6,)), dma((4,)), dma((4,)), dma((3, 8)), dma((3, 8))],
+               dma((6,)), dma((6,)), dma((4,)), dma((4,)), dma((4, 8)), dma((4, 8))],
         name="layer", cost_estimate=pl.CostEstimate(flops=100 * 10**9, bytes_accessed=60 * 10**6, transcendentals=0),
         compiler_params=pltpu.CompilerParams(collective_id=0, has_side_effects=True, vmem_limit_bytes=63 << 20))(res, counts, *operands)
 
@@ -626,14 +667,11 @@
     cotangent,
 ):
     floating = jnp.float32
-    heads_dev = table_low.shape[1]
     width = query_weight.shape[1]
-    index_low_pad = jnp.pad(index_low, ((0, 256 - P_LO), (0, 256 - P_LO)))
-    index_high_pad = jnp.pad(index_high, ((0, 592 - P_HI), (0, SEQ - P_HI)))
     n_low = -(-table_low.shape[0] // (BB * 16)) * 16
     n_high = -(-table_high.shape[0] // (BB * 16)) * 16
     known = lax.axis_size("dp") == 8
-    reduce_grad, expand_grad, attn_grads, result, hidden_grad, wide, slim, tables = layer(
+    reduce_grad, expand_grad, attn_grads, result, hidden_grad, small, low_grad, high_grad = layer(
         HD ** (-0.5),
         known,
         resolution,
@@ -657,48 +695,48 @@
         reduce_bias,
         second_scale,
         cotangent,
-        table_low,
-        table_high,
-        index_low_pad,
-        index_high_pad,
+        table_low.T,
+        table_high.T,
+        index_low,
+        index_high,
         n_low,
         n_high,
     )
-    reduce_grad = reduce_grad.astype(floating)
-    expand_grad = expand_grad.astype(floating)
-    attn_grads = attn_grads.astype(floating)
     if not known:
-        reduce_grad, expand_grad, attn_grads, slim, tables = lax.psum(
-            (reduce_grad, expand_grad, attn_grads, slim, tables), "dp"
+        reduce_grad, expand_grad, attn_grads, tail, low_grad, high_grad = lax.psum(
+            (
+                reduce_grad.astype(floating),
+                expand_grad.astype(floating),
+                attn_grads.astype(floating),
+                small[8:],
+                low_grad,
+                high_grad,
+            ),
+            "dp",
         )
-        wide = lax.psum(wide, ("dp", "tensor"))
-
-    def unpack(block, count):
-        block = block.reshape(heads_dev, BB, -1).transpose(2, 1, 0)
-        return block.reshape(-1, heads_dev)[:count]
-
+        small = jnp.concatenate((lax.psum(small[:8], ("dp", "tensor")), tail), axis=0)
     return (
         result,
         hidden_grad,
-        wide[0],
-        wide[1],
-        attn_grads[:width].T,
-        slim[0, :width],
-        attn_grads[width : 2 * width].T,
-        attn_grads[2 * width : 3 * width].T,
-        slim[1, :width],
-        attn_grads[3 * width :],
-        wide[3],
-        wide[2],
-        wide[4],
-        wide[5],
-        expand_grad,
-        slim[2],
-        reduce_grad,
-        wide[7],
-        wide[6],
-        unpack(tables[:, :n_low], table_low.shape[0]),
-        unpack(tables[:, n_low : n_low + n_high], table_high.shape[0]),
+        small[0],
+        small[1],
+        attn_grads[:width].astype(floating).T,
+        small[8, :width],
+        attn_grads[width : 2 * width].astype(floating).T,
+        attn_grads[2 * width : 3 * width].astype(floating).T,
+        small[8, 256 : 256 + width],
+        attn_grads[3 * width :].astype(floating),
+        small[3],
+        small[2],
+        small[4],
+        small[5],
+        expand_grad.astype(floating),
+        small[9],
+        reduce_grad.astype(floating),
+        small[7],
+        small[6],
+        low_grad[:, : table_low.shape[0]].T,
+        high_grad[:, : table_high.shape[0]].T,
     )
 
 

time: 208 us -> 188 us (0.904)
  Pallas kernels: 183 us -> 172 us
  local copies, waits for them, and re-layouts: 17.7 us -> 8.13 us
    pallas_call x1, Pallas kernels: 183 us -> 172 us  [layer(): pl.pallas_call(functools.partial(layer_kernel, scale, sums), out_shape=(S...]
    pad x2 -> x0, local copies, waits for them, and re-layouts: 4.25 us -> none  [the longest x1 2.6 us: local(): index_high_pad = jnp.pad(index_high, ((0, 592 - P_HI), (0, SEQ - P_HI)))]
    slice x6 -> x2, local copies, waits for them, and re-layouts: 7.22 us -> 3.01 us  [the longest x1 1.73 us: local(): small[6]]
    convert_element_type x5 -> x3, other arithmetic: 4.81 us -> 5.95 us  [the longest x1 2.94 us: local(): expand_grad.astype(floating)]
where the time goes in v4:
time: 188 us
  Pallas kernels  172 us (91%)
  local copies, waits for them, and re-layouts  8.13 us (4%)
  other arithmetic  5.95 us (3%)
    pallas_call x1, Pallas kernels, layer(): pl.pallas_call(functools.partial(layer_kernel, scale, sums), out_shape=(S...  172 us

profile of v4, /device:TPU:0, one launch (start us, length us, event | category | flops | bytes accessed | tf_op | source)
XLA Modules:
  0.0 187.6 jit_solution(7654143094713219882)
XLA Ops:
  1.3 172.2 %layer.1 = (bf16[768,768]{1,0:T(8,128)(2,1)}, bf16[768,768]{1,0:T(8,128)(2,1)}, bf16[768,768]{1,0:T(8,128)(2,1)}, bf16[320,768]{1,0:T(8,128)(2,1)}, f32[320,768]...) custom-call(s32[2]{0:T(128)} %res.1, s32[1]{0:T(128)S(6)} %copy.48.counts, ...), custom_call_target="tpu_custom_call" | custom-call | flops 99999997952 | bytes 60000000 | tf_op jit(solution)/shard_map/layer/pallas_call | solution.py:623
  173.5 1.3 fusion
  174.8 1.7 slice_reduce_fusion
  176.5 1.3 slice_bitcast_fusion.1
  177.8 1.4 slice_bitcast_fusion
  179.2 0.0 copy-start.1
  179.2 2.9 %convert_element_type.13 = f32[768,768]{1,0:T(8,128)} convert(bf16[768,768]{1,0:T(8,128)(2,1)} %get-tuple-element.33) | non-fusion elementwise | flops 589824 | bytes 3538944 | tf_op jit(solution)/shard_map/convert_element_type | solution.py:733
  182.2 0.0 copy-done.1
  182.2 0.0 copy-start
  182.2 1.6 convert_element_type.14
  183.8 0.1 copy-done
  183.9 0.0 copy-start.3
  183.9 1.4 slice_convert_fusion
  185.3 0.0 copy-start.2
  185.3 0.0 copy-done.3
  185.3 0.8 copy.49
  186.1 0.6 copy-done.2
  186.7 0.9 copy.50
Async XLA Ops:
  179.2 2.9 %copy-start.1 = (bf16[768,768]{1,0:T(8,128)(2,1)S(1)}, bf16[768,768]{1,0:T(8,128)(2,1)}, u32[]{:S(2)}) copy-start(bf16[768,768]{1,0:T(8,128)(2,1)} %get-tuple-element.34) | copy-start | bytes 3538948
  182.2 1.7 copy-start
  183.9 1.4 copy-start.3
  185.3 1.4 copy-start.2

commit v5 on v4

--- a/solution.py
+++ b/solution.py
@@ -162,9 +162,9 @@
         here = buf.at[span(cross, h)]
         return remote(here, here, send.at[4 + h], recv.at[4 + h], (d, sibling))
     def sum_far(j, send, recv, h):
-        return remote(cbuf.at[j, 0, h], ccore.at[j, 0, h], send.at[h], recv.at[h], (d, sibling))
+        return remote(cbuf.at[0, h], ccore.at[j, 0, h], send.at[h], recv.at[h], (d, sibling))
     def sum_near(j, send, recv, h):
-        return remote(cbuf.at[j, 1, h], ccore.at[j, 1, h], send.at[2 + h], recv.at[2 + h], (d, sibling))
+        return remote(cbuf.at[1, h], ccore.at[j, 1, h], send.at[2 + h], recv.at[2 + h], (d, sibling))
     def sum_x(j, send, recv, h):
         return remote(xbuf.at[j, h], xin.at[j, h], send.at[4 + h], recv.at[4 + h], (d, cross))
     arrays = (x0, x1, x2)
@@ -287,7 +287,7 @@
     mine = t * rows // SEQ
     attend_image(1 - mine)
     for h in range(2):
-        cbuf[0, 0, h] = output_of(diag, h).astype(BF)
+        cbuf[0, h] = output_of(diag, h).astype(BF)
         sum_far(0, o_s, o_r, h).start()
     for h in range(2):
         total = output_of(cross, h)
@@ -296,7 +296,7 @@
         sum_x(0, o_s, o_r, h).start()
     attend_image(mine)
     for h in range(2):
-        cbuf[0, 1, h] = output_of(sibling, h).astype(BF)
+        cbuf[1, h] = output_of(sibling, h).astype(BF)
         sum_near(0, o_s, o_r, h).start()
     for h in range(2):
         acc[pl.ds(h * half, half)] = output_of(t, h)
@@ -336,28 +336,33 @@
         gather_near(gm, m_s, m_r, h).wait()
         gather_near(gt, t_s, t_r, h).wait()
         gather_on(gm, m_s, m_r, h).wait()
-    def feed_rest(h, c):
+    def feed_near(h, c):
+        cbuf[1, h] = feed(sibling, h).astype(BF)
+        sum_near(1, n_s, n_r, h).start()
+        return c
+    lax.fori_loop(0, 2, feed_near, 0)
+    def feed_far(h, c):
         gather_x(gt, t_s, t_r, h).wait()
         gather_on(gt, t_s, t_r, h).start()
-        cbuf[1, 1, h] = feed(sibling, h).astype(BF)
-        sum_near(1, n_s, n_r, h).start()
+        total = feed(cross, h)
         gather_on(gt, t_s, t_r, h).wait()
-        cbuf[1, 0, h] = feed(diag, h).astype(BF)
+        cbuf[0, h] = feed(diag, h).astype(BF)
         sum_far(1, n_s, n_r, h).start()
-        total = feed(cross, h)
         sum_far(1, n_s, n_r, h).wait()
         xbuf[1, h] = (total + ccore[1, 0, h].astype(F32)).astype(BF)
         sum_x(1, n_s, n_r, h).start()
         return c
-    lax.fori_loop(0, 2, feed_rest, 0)
+    lax.fori_loop(0, 2, feed_far, 0)
 
     tile = 128
     def reduce_grad(i, c):
         cols = pl.ds(pl.multiple_of(i * tile, tile), tile)
         x0[cols] = lax.dot_general(act[:, cols], gm[...], TN, preferred_element_type=F32).astype(BF)
         return c
-    lax.fori_loop(0, act.shape[1] // tile, reduce_grad, 0)
+    count = act.shape[1] // tile
+    lax.fori_loop(0, count // 2, reduce_grad, 0)
     start_y(0)
+    lax.fori_loop(count // 2, count, reduce_grad, 0)
     wmine[...] = jnp.zeros_like(wmine)
     def second_back(h):
         here = pl.ds(h * half, half)
@@ -376,31 +381,32 @@
         wmine[3:4, :] += jnp.sum(agrad, axis=0, keepdims=True)
         wmine[4:5, :] += jnp.sum(grad * scaled, axis=0, keepdims=True)
         wmine[5:6, :] += jnp.sum(grad, axis=0, keepdims=True)
+    start_y(1)
     second_back(0)
     def expand_grad(i, c):
         cols = pl.ds(pl.multiple_of(i * tile, tile), tile)
         x1[cols] = lax.dot_general(gt[:, cols], pgl[...], TN, preferred_element_type=F32).astype(BF)
         return c
     lax.fori_loop(0, gt.shape[1] // tile, expand_grad, 0)
-    start_y(1)
-    second_back(1)
     step_a(0)
     start_y(2)
+    second_back(1)
+    step_a(1)
     def mixture_of(who):
         here = rows_at(who)
         dmix[here] = lax.dot_general(ga[here], wo[...], NT, preferred_element_type=F32).astype(BF)
     mixture_of(t)
-    step_a(1)
-    start_y(3)
     gather_x(ga, a_s, a_r, 0).wait()
     gather_on(ga, a_s, a_r, 0).start()
+    start_y(3)
     for h in range(2):
         gather_near(ga, a_s, a_r, h).wait()
+    mixture_of(sibling)
     step_b(0)
-    mixture_of(sibling)
     gather_x(ga, a_s, a_r, 1).wait()
     gather_on(ga, a_s, a_r, 1).start()
     mixture_of(cross)
+    step_b(1)
     for h in range(2):
         gather_on(ga, a_s, a_r, h).wait()
     mixture_of(diag)
@@ -447,6 +453,7 @@
         v_buf[here] = out.astype(BF)
     attention_back(0)
     step_a(2)
+    step_d(0)
     attention_back(1)
 
     def back(who):
@@ -459,55 +466,54 @@
             buf[h] = value[h * half:(h + 1) * half].astype(BF)
     def whole(ref):
         return jnp.concatenate([ref[0], ref[1]], axis=0).astype(F32)
-    a_far = remote(cbuf.at[0, 0], acore.at[0], r_s.at[0], r_r.at[0], (d, sibling))
-    a_near = remote(cbuf.at[0, 1], acore.at[1], r_s.at[1], r_r.at[1], (d, sibling))
+    a_far = remote(cbuf.at[0], acore.at[0], r_s.at[0], r_r.at[0], (d, sibling))
+    a_near = remote(cbuf.at[1], acore.at[1], r_s.at[1], r_r.at[1], (d, sibling))
     a_cross = remote(xbuf.at[0], across, r_s.at[2], r_r.at[2], (d, cross))
     b_far = remote(part.at[rows_at(diag)], bcore.at[0], r_s.at[3], r_r.at[3], (d, sibling))
     b_near = remote(part.at[rows_at(sibling)], bcore.at[1], r_s.at[4], r_r.at[4], (d, sibling))
     b_cross = remote(xbuf.at[1], bcross, r_s.at[5], r_r.at[5], (d, cross))
-    send(cbuf.at[0, 0], back(diag))
+    send(cbuf.at[0], back(diag))
     a_far.start()
     b_far.start()
+    step_d(1)
+    total = back(cross)
     step_a(3)
-    total = back(cross)
     a_far.wait()
     send(xbuf.at[0], total + whole(acore.at[0]))
     a_cross.start()
     for j, (left, right) in enumerate(((q_buf, g1), (k_buf, g1), (v_buf, g1), (mix, ga))):
         x2[j * width:(j + 1) * width, :] = lax.dot_general(left[...], right[...], TN, preferred_element_type=F32).astype(BF)
-    step_b(1)
-    start_y(4)
-    send(cbuf.at[0, 1], back(sibling))
+        if j == 1:
+            start_y(4)
+    start_y(5)
+    send(cbuf.at[1], back(sibling))
     a_near.start()
     b_near.start()
     acc[...] = back(t)
+    step_b(2)
     b_far.wait()
     send(xbuf.at[1], part[rows_at(cross)].astype(F32) + bcore[0].astype(F32))
-    step_b(2)
-    start_y(5)
     n_hi = -(-P_HI // UN)
     done = [0]
     def scatter_part(count):
         first, last = done[0], min(done[0] + count, n_hi)
         scatter_run(ihi, ghi, thi, first, last, first == 0)
         done[0] = last
-    scatter_part(4)
-    step_d(0)
-    step_b(3)
-    step_d(1)
-    step_a(4)
+    scatter_part(5)
     a_cross.wait()
     b_cross.start()
     a_near.wait()
+    step_a(4)
     grad = acc[...] + whole(acore.at[1]) + whole(across)
     scaled, inverse = moments(hidden[...].astype(F32))
     wmine[0:1, :] = jnp.sum(grad * scaled, axis=0, keepdims=True)
     wmine[1:2, :] = jnp.sum(grad, axis=0, keepdims=True)
     hidden_grad[...] += norm_back(grad, scaled, inverse, row(gain1))
-    scatter_part(8)
+    scatter_part(6)
     step_a(5)
+    scatter_part(4)
     step_d(2)
-    scatter_part(4)
+    scatter_part(2)
     b_near.wait()
     b_cross.wait()
     out = part[rows_at(t)].astype(F32) + bcore[1].astype(F32) + whole(bcross) + row(rbias)
@@ -516,6 +522,7 @@
     up = cot[...].astype(F32) * alive
     wmine[6:7, :] = jnp.sum(up * out, axis=0, keepdims=True)
     wmine[7:8, :] = jnp.sum(up * row(scale2), axis=0, keepdims=True)
+    step_b(3)
     def w_copy(k):
         return remote(wmine, wten.at[k], w_s.at[k], w_r.at[k], (d, lax.rem(t + k, 4)))
     def eighth(buf, who):
@@ -550,9 +557,9 @@
     if sums:
         for k in range(1, 4):
             w_copy(k).start()
-    step_d(3)
+    step_b(4)
     scatter_part(4)
-    step_b(4)
+    step_b(5)
     total = wmine[...]
     if sums:
         for k in range(1, 4):
@@ -567,13 +574,13 @@
         for j in range(lanes):
             vec[(8 + r) * lanes + j:(8 + r) * lanes + j + 1, :] = smine[r:r + 1, j * 128:(j + 1) * 128]
     small_start(0)
+    scatter_part(7)
+    step_d(3)
     scatter_part(4)
-    step_b(5)
-    scatter_part(4)
-    small_turn(0)
     step_d(4)
     scatter_part(n_hi)
     step_d(5)
+    small_turn(0)
     scatter_run(ilo, glo, tlo, 0, -(-P_LO // UN), True)
     per = (thi.shape[1] + tlo.shape[1]) // 4
     tbl[...] = jnp.zeros_like(tbl)
@@ -627,7 +634,7 @@
             + [V((total, model), BF)] * 4 + [V((total, width), BF)] * 5 + [V((SLOTS, heads, SEQ, SEQ), BF)]
             + [V((total, inner), BF)] * 2 + [V((total, model), BF)] + [V((rows, model), F32)] * 2
             + [V((inner, model), BF), V((model, inner), BF), V((4 * width, model), BF), V((heads, 592, SEQ), F32), V((heads, 208, 256), F32), V((1, inner), F32)]
-            + [V((2, 2, 2, half, model), BF)] * 2 + [V((2, 2, half, model), BF)] * 2
+            + [V((2, 2, half, model), BF), V((2, 2, 2, half, model), BF)] + [V((2, 2, half, model), BF)] * 2
             + [V((2, 2, half, model), BF), V((2, half, model), BF), V((2, rows, model), BF), V((2, half, model), BF)]
             + [V((CHUNKS, 192, model), BF), V((CHUNKS, 3, 48, model), BF)]
             + [V((heads * BB, n_lo), F32), V((heads * BB, n_hi), F32)]
@@ -637,6 +644,56 @@
                dma((6,)), dma((6,)), dma((4,)), dma((4,)), dma((4, 8)), dma((4, 8))],
         name="layer", cost_estimate=pl.CostEstimate(flops=100 * 10**9, bytes_accessed=60 * 10**6, transcendentals=0),
         compiler_params=pltpu.CompilerParams(collective_id=0, has_side_effects=True, vmem_limit_bytes=63 << 20))(res, counts, *operands)
+
+
+def finish_kernel(pieces, i0, i1, i2, small, tlow, thigh, res_in, hid_in, *refs):
+    r_out, e_out, q_out, k_out, v_out, o_out = refs[:6]
+    vectors = refs[6:14]
+    qb, vb, eb, tl, th, res_out, hid_out, low, wide, s_in, s_out, s_x = refs[14:]
+    copies = [pltpu.make_async_copy(res_in, res_out, s_x.at[0]), pltpu.make_async_copy(hid_in, hid_out, s_x.at[1])]
+    rows = low.shape[1]
+    places = []
+    for src, out in ((i0, r_out), (i1, e_out)):
+        for n in range(pieces):
+            here = pl.ds(n * rows, rows)
+            places.append((src.at[here], out.at[here]))
+    for n, out in enumerate((q_out, k_out, v_out, o_out)):
+        places.append((i2.at[pl.ds(n * rows, rows)], out))
+    loads = [pltpu.make_async_copy(src, low.at[n], s_in.at[n]) for n, (src, _) in enumerate(places)]
+    stores = [pltpu.make_async_copy(wide.at[n], out, s_out.at[n]) for n, (_, out) in enumerate(places)]
+    for copy in loads:
+        copy.start()
+    for copy in copies:
+        copy.start()
+    for n in range(len(places)):
+        loads[n].wait()
+        wide[n] = low[n].astype(F32)
+        stores[n].start()
+    for r, out in enumerate(vectors):
+        out[...] = small[r:r + 1, :].reshape(out.shape)
+    qb[...] = small[8:9, 0:qb.shape[0]].reshape(qb.shape)
+    vb[...] = small[8:9, 256:256 + vb.shape[0]].reshape(vb.shape)
+    eb[...] = small[9:10, :].reshape(eb.shape)
+    tl[...] = tlow[:, 0:tl.shape[1]]
+    th[...] = thigh[:, 0:th.shape[1]]
+    for copy in stores + copies:
+        copy.wait()
+
+def finish(reduce_grad, expand_grad, attn_grads, small, low_grad, high_grad, result, hidden_grad, width, e_lo, e_hi):
+    S = jax.ShapeDtypeStruct
+    vm = pl.BlockSpec(memory_space=pltpu.VMEM)
+    anywhere = pl.BlockSpec(memory_space=pl.ANY)
+    model = reduce_grad.shape[1]
+    pieces = reduce_grad.shape[0] // width
+    count = 2 * pieces + 4
+    shapes = (S(reduce_grad.shape, F32), S(expand_grad.shape, F32)) + (S((width, model), F32),) * 4 + (S((model,), F32),) * 8 + (
+        S((width,), F32), S((width,), F32), S((model,), F32), S((low_grad.shape[0], e_lo), F32), S((high_grad.shape[0], e_hi), F32),
+        S(result.shape, result.dtype), S(hidden_grad.shape, F32))
+    dma = pltpu.SemaphoreType.DMA
+    return pl.pallas_call(functools.partial(finish_kernel, pieces), out_shape=shapes,
+        in_specs=[anywhere] * 3 + [vm] * 3 + [anywhere] * 2, out_specs=(anywhere,) * 6 + (vm,) * 13 + (anywhere,) * 2,
+        scratch_shapes=[pltpu.VMEM((count, width, model), BF), pltpu.VMEM((count, width, model), F32), dma((count,)), dma((count,)), dma((2,))],
+        name="finish", compiler_params=pltpu.CompilerParams(vmem_limit_bytes=63 << 20))(reduce_grad, expand_grad, attn_grads, small, low_grad, high_grad, result, hidden_grad)
 
 
 def local(
@@ -702,6 +759,44 @@
         n_low,
         n_high,
     )
+    if known:
+        reduce_grad, expand_grad, *rest, low_grad, high_grad, result, hidden_grad = finish(
+            reduce_grad,
+            expand_grad,
+            attn_grads,
+            small,
+            low_grad,
+            high_grad,
+            result,
+            hidden_grad,
+            width,
+            table_low.shape[0],
+            table_high.shape[0],
+        )
+        query_grad, key_grad, value_grad, output_grad, *norms, query_row, value_row, expand_row = rest
+        return (
+            result,
+            hidden_grad,
+            norms[0],
+            norms[1],
+            query_grad.T,
+            query_row,
+            key_grad.T,
+            value_grad.T,
+            value_row,
+            output_grad,
+            norms[3],
+            norms[2],
+            norms[4],
+            norms[5],
+            expand_grad,
+            expand_row,
+            reduce_grad,
+            norms[7],
+            norms[6],
+            low_grad.T,
+            high_grad.T,
+        )
     if not known:
         reduce_grad, expand_grad, attn_grads, tail, low_grad, high_grad = lax.psum(
             (

time: 188 us -> 223 us (1.19)
  Pallas kernels: 172 us -> 221 us
  local copies, waits for them, and re-layouts: 8.13 us -> 0 us
  other arithmetic: 5.95 us -> 0 us
    pallas_call x0 -> x1, Pallas kernels: none -> 47.5 us  [finish(): pl.pallas_call(functools.partial(finish_kernel, pieces), out_shape=shapes...]
    convert_element_type x3 -> x0, other arithmetic: 5.95 us -> none  [the longest x1 2.94 us: local(): expand_grad.astype(floating)]
    slice x2 -> x0, local copies, waits for them, and re-layouts: 3.01 us -> none  [the longest x1 1.73 us: local(): small[6]]
    transpose x2 -> x0, local copies, waits for them, and re-layouts: 2.7 us -> none  [the longest x1 1.39 us: local(): high_grad[:, :table_high.shape[0]]]
    unnamed x10 -> x0, local copies, waits for them, and re-layouts: 2.42 us -> none
where the time goes in v5:
time: 223 us
  Pallas kernels  221 us (99%)
    pallas_call x1, Pallas kernels, layer(): pl.pallas_call(functools.partial(layer_kernel, scale, sums), out_shape=(S...  174 us
    pallas_call x1, Pallas kernels, finish(): pl.pallas_call(functools.partial(finish_kernel, pieces), out_shape=shapes...  47.5 us

profile of v5, /device:TPU:0, one launch (start us, length us, event | category | flops | bytes accessed | tf_op | source)
XLA Modules:
  0.0 222.6 jit_solution(7717616490827964587)
XLA Ops:
  1.3 173.6 %layer.1 = (bf16[768,768]{1,0:T(8,128)(2,1)}, bf16[768,768]{1,0:T(8,128)(2,1)}, bf16[768,768]{1,0:T(8,128)(2,1)}, bf16[320,768]{1,0:T(8,128)(2,1)}, f32[320,768]...) custom-call(s32[2]{0:T(128)} %res.1, s32[1]{0:T(128)S(6)} %copy.46.counts, ...), custom_call_target="tpu_custom_call" | custom-call | flops 99999997952 | bytes 60000000 | tf_op jit(solution)/shard_map/layer/pallas_call | solution.py:630
  174.9 47.5 %finish.1 = (f32[768,768]{1,0:T(8,128)}, f32[768,768]{1,0:T(8,128)}, f32[192,768]{1,0:T(8,128)}, f32[192,768]{1,0:T(8,128)}, f32[192,768]{1,0:T(8,128)}, /*index...) custom-call(bf16[768,768]{1,0:T(8,128)(2,1)} %get-tuple-element.50.i, ...), custom_call_target="tpu_custom_call" | custom-call | tf_op jit(solution)/shard_map/finish/pallas_call | solution.py:693

commit v6 on v5

--- a/solution.py
+++ b/solution.py
@@ -577,11 +577,10 @@
     scatter_part(7)
     step_d(3)
     scatter_part(4)
+    scatter_run(ilo, glo, tlo, 0, -(-P_LO // UN), True)
     step_d(4)
     scatter_part(n_hi)
-    step_d(5)
     small_turn(0)
-    scatter_run(ilo, glo, tlo, 0, -(-P_LO // UN), True)
     per = (thi.shape[1] + tlo.shape[1]) // 4
     tbl[...] = jnp.zeros_like(tbl)
     def spread(src, base):
@@ -598,6 +597,7 @@
         o1[...] = x1[...]
         o2[...] = x2[...]
     small_start(1)
+    step_d(5)
     small_end(0)
     for r in range(10):
         for j in range(lanes):
@@ -649,8 +649,9 @@
 def finish_kernel(pieces, i0, i1, i2, small, tlow, thigh, res_in, hid_in, *refs):
     r_out, e_out, q_out, k_out, v_out, o_out = refs[:6]
     vectors = refs[6:14]
-    qb, vb, eb, tl, th, res_out, hid_out, low, wide, s_in, s_out, s_x = refs[14:]
-    copies = [pltpu.make_async_copy(res_in, res_out, s_x.at[0]), pltpu.make_async_copy(hid_in, hid_out, s_x.at[1])]
+    qb, vb, eb, tl, th, res_out, hid_out, low, wide, res, hid, s_in, s_out, s_x = refs[14:]
+    first = [pltpu.make_async_copy(hid_in, hid, s_x.at[0]), pltpu.make_async_copy(res_in, res, s_x.at[1])]
+    second = [pltpu.make_async_copy(hid, hid_out, s_x.at[2]), pltpu.make_async_copy(res, res_out, s_x.at[3])]
     rows = low.shape[1]
     places = []
     for src, out in ((i0, r_out), (i1, e_out)):
@@ -661,10 +662,11 @@
         places.append((i2.at[pl.ds(n * rows, rows)], out))
     loads = [pltpu.make_async_copy(src, low.at[n], s_in.at[n]) for n, (src, _) in enumerate(places)]
     stores = [pltpu.make_async_copy(wide.at[n], out, s_out.at[n]) for n, (_, out) in enumerate(places)]
-    for copy in loads:
+    for copy in first + loads:
         copy.start()
-    for copy in copies:
-        copy.start()
+    for before, after in zip(first, second):
+        before.wait()
+        after.start()
     for n in range(len(places)):
         loads[n].wait()
         wide[n] = low[n].astype(F32)
@@ -676,7 +678,7 @@
     eb[...] = small[9:10, :].reshape(eb.shape)
     tl[...] = tlow[:, 0:tl.shape[1]]
     th[...] = thigh[:, 0:th.shape[1]]
-    for copy in stores + copies:
+    for copy in stores + second:
         copy.wait()
 
 def finish(reduce_grad, expand_grad, attn_grads, small, low_grad, high_grad, result, hidden_grad, width, e_lo, e_hi):
@@ -692,7 +694,7 @@
     dma = pltpu.SemaphoreType.DMA
     return pl.pallas_call(functools.partial(finish_kernel, pieces), out_shape=shapes,
         in_specs=[anywhere] * 3 + [vm] * 3 + [anywhere] * 2, out_specs=(anywhere,) * 6 + (vm,) * 13 + (anywhere,) * 2,
-        scratch_shapes=[pltpu.VMEM((count, width, model), BF), pltpu.VMEM((count, width, model), F32), dma((count,)), dma((count,)), dma((2,))],
+        scratch_shapes=[pltpu.VMEM((count, width, model), BF), pltpu.VMEM((count, width, model), F32), pltpu.VMEM(result.shape, result.dtype), pltpu.VMEM(hidden_grad.shape, F32), dma((count,)), dma((count,)), dma((4,))],
         name="finish", compiler_params=pltpu.CompilerParams(vmem_limit_bytes=63 << 20))(reduce_grad, expand_grad, attn_grads, small, low_grad, high_grad, result, hidden_grad)
 
 

time: 223 us -> 179 us (0.80)
  Pallas kernels: 221 us -> 177 us
    pallas_call x1, Pallas kernels: 47.5 us -> 7.18 us  [finish(): pl.pallas_call(functools.partial(finish_kernel, pieces), out_shape=shapes...]
    pallas_call x1, Pallas kernels: 174 us -> 170 us  [layer(): pl.pallas_call(functools.partial(layer_kernel, scale, sums), out_shape=(S...]
where the time goes in v6:
time: 179 us
  Pallas kernels  177 us (99%)
    pallas_call x1, Pallas kernels, layer(): pl.pallas_call(functools.partial(layer_kernel, scale, sums), out_shape=(S...  170 us
    pallas_call x1, Pallas kernels, finish(): pl.pallas_call(functools.partial(finish_kernel, pieces), out_shape=shapes...  7.18 us

profile of v6, /device:TPU:0, one launch (start us, length us, event | category | flops | bytes accessed | tf_op | source)
XLA Modules:
  0.0 179.0 jit_solution(4082987790243602506)
XLA Ops:
  1.3 170.3 %layer.1 = (bf16[768,768]{1,0:T(8,128)(2,1)}, bf16[768,768]{1,0:T(8,128)(2,1)}, bf16[768,768]{1,0:T(8,128)(2,1)}, bf16[320,768]{1,0:T(8,128)(2,1)}, f32[320,768]...) custom-call(s32[2]{0:T(128)} %res.1, s32[1]{0:T(128)S(6)} %copy.46.counts, ...), custom_call_target="tpu_custom_call" | custom-call | flops 99999997952 | bytes 60000000 | tf_op jit(solution)/shard_map/layer/pallas_call | solution.py:630
  171.6 7.2 %finish.1 = (f32[768,768]{1,0:T(8,128)}, f32[768,768]{1,0:T(8,128)}, f32[192,768]{1,0:T(8,128)}, f32[192,768]{1,0:T(8,128)}, f32[192,768]{1,0:T(8,128)}, /*index...) custom-call(bf16[768,768]{1,0:T(8,128)(2,1)} %get-tuple-element.50.i, ...), custom_call_target="tpu_custom_call" | custom-call | tf_op jit(solution)/shard_map/finish/pallas_call | solution.py:695
